TPU v7x, 512 devices: a whole 4x8x8 slice. The times are simulated.
512 devices in a mesh: seq: 64 (over x, z, core), dp: 8 (over y).
Axes of the slice: x: 4, y: 8, z: 8, core: 2. Of those that a mesh axis runs over, the one named last changes fastest.
Arguments:
- inputs: bfloat16 [8, 8192, 768], P('dp', 'seq'), may hold values from -150 to 150
- cotangent: bfloat16 [8, 8192, 768], P('dp', 'seq'), may hold values from -16 to 16
- conv_weight: bfloat16 [768, 768], replicated, may hold values from -0.125 to 0.125
- proj_weight: bfloat16 [256, 768], replicated, may hold values from -0.375 to 0.375
- gain_in: float32 [768], replicated, may hold values from 0.5 to 1.5
- bias_in: float32 [768], replicated, may hold values from -0.5 to 0.5
- gain_mid: float32 [256], replicated, may hold values from 0.5 to 1.5
- bias_mid: float32 [256], replicated, may hold values from -0.5 to 0.5
Outputs:
- block_out: bfloat16 [8, 8192, 768], P('dp', 'seq')
- input_grad: bfloat16 [8, 8192, 768], P('dp', 'seq')
- conv_grad: float32 [768, 768], P('seq')
- proj_grad: float32 [768, 256], P('seq')
All inputs are finite; a program needn't handle non-finite values.
Results may differ from a plain program's by a relative error of at most 0.015.
Values may be sent and summed in bfloat16 or wider, within the bound.
No kernel may reach another device: no remote copies, remote signals or barrier semaphores. Data moves between devices by JAX's collectives and lax.ppermute only.
A program may use at most 64 MiB of HBM per device.

v0:
```python
import math

import jax
import jax.numpy as jnp
from jax import lax
from jax.sharding import Mesh
from jax.sharding import PartitionSpec as P

SEQ = ("seq_0", "seq_1", "seq_2")


def copy_for_each(x, axis):
    copies = jnp.broadcast_to(x, (lax.axis_size(axis), *x.shape))
    return lax.all_to_all(copies, axis, split_axis=0, concat_axis=0, tiled=True)


def over_copies(x, axis):
    return copy_for_each(x, axis).sum(axis=0)


def by_axis(x, axes):
    far, near = axes
    return over_copies(over_copies(x, near), far)


def in_one(arrays, axis):
    ends = [0]
    for a in arrays:
        ends.append(ends[-1] + a.size)
    total = by_axis(jnp.concatenate([a.ravel() for a in arrays]), axis)
    return tuple((total[b:e].reshape(a.shape) for a, b, e in zip(arrays, ends, ends[1:])))


def passed_along(value, axis, steps):
    count = lax.axis_size(axis)
    first, last = (max(0, -steps), min(count, count - steps))
    return lax.ppermute(value, axis, [(source, source + steps) for source in range(first, last)])


def in_blocks(x, dim, devices):
    before, after = (x.shape[:dim], x.shape[dim + 1 :])
    return jnp.moveaxis(x.reshape(*before, devices, -1, *after), dim, 0)


def sum_at_owner(x, axis, dim):
    devices = lax.axis_size(axis)
    pieces = lax.all_to_all(in_blocks(x, dim, devices), axis, 0, 0, tiled=True)
    return jnp.sum(pieces, axis=0)


def sum_by_axis(x, axes, dim):
    far, near = axes
    pieces = in_blocks(x, dim, lax.axis_size(far))
    nearer = sum_at_owner(pieces, near, dim + 1)
    arrived = lax.all_to_all(nearer, far, split_axis=0, concat_axis=0, tiled=True)
    return arrived.sum(axis=0)


def side_by_side(arrays, axis, dim, along):
    widths = [a.shape[along] for a in arrays]
    both = jnp.concatenate(arrays, axis=along)
    filled = sum_by_axis(both, axis, dim)
    return tuple(jnp.split(filled, [sum(widths[:k]) for k in range(1, len(widths))], axis=along))


def over_copies_2(x, axis):
    everything = copy_for_each(x, axis)
    return jnp.sum(everything.astype(jnp.float32), axis=0)


def gelu_tanh(value):
    coeff = math.sqrt(2.0 / math.pi)
    return 0.5 * value * (1.0 + jnp.tanh(coeff * (value + 0.044715 * value * value * value)))


def gelu_slope(value):
    coeff = math.sqrt(2.0 / math.pi)
    inner = jnp.tanh(coeff * (value + 0.044715 * value * value * value))
    return 0.5 * (1.0 + inner) + 0.5 * value * (1.0 - inner * inner) * coeff * (
        1.0 + 3.0 * 0.044715 * value * value
    )


def normalize(value, counted):
    totals, second = in_one(
        (jnp.sum(value, axis=0), jnp.sum(value * value, axis=0)),
        (("seq_0", "seq_1"), ("seq_2", "dp")),
    )
    center = totals / counted
    squares = second / counted - center * center
    spread = jnp.sqrt(squares + 1e-05)
    return ((value - center) / spread, spread)


def back_norm(dpre, normed, gain, spread, counted):
    first, second = in_one(
        (jnp.sum(dpre, axis=0), jnp.sum(dpre * normed, axis=0)),
        (("seq_0", "seq_1"), ("seq_2", "dp")),
    )
    return gain * (dpre - first / counted - normed * (second / counted)) / spread


def per_device(inputs, cotangent, conv_weight, proj_weight, gain_in, bias_in, gain_mid, bias_mid):
    samples, places, width = inputs.shape
    central_window = proj_weight.shape[0]
    counted = samples * places * lax.axis_size(SEQ) * lax.axis_size("dp")
    stream = inputs.reshape(samples * places, width).astype(jnp.float32)
    normed_in, spread_in = normalize(stream, counted)
    pre_in = gain_in * normed_in + bias_in
    act_in = gelu_tanh(pre_in).astype(jnp.bfloat16)
    shaped = act_in.reshape(samples, places, width)
    before = passed_along(shaped, SEQ, 8).reshape(samples * places, width)
    after = passed_along(shaped, SEQ, -8).reshape(samples * places, width)
    dilated_filter_output = jnp.dot(
        act_in,
        conv_weight[:, central_window : 2 * central_window],
        preferred_element_type=jnp.float32,
    )
    dilated_filter_output = dilated_filter_output + jnp.dot(
        before, conv_weight[:, :central_window], preferred_element_type=jnp.float32
    )
    dilated_filter_output = dilated_filter_output + jnp.dot(
        after, conv_weight[:, 2 * central_window :], preferred_element_type=jnp.float32
    )
    normed_mid, spread_mid = normalize(dilated_filter_output, counted)
    pre_mid = gain_mid * normed_mid + bias_mid
    act_mid = gelu_tanh(pre_mid).astype(jnp.bfloat16)
    update = jnp.dot(act_mid, proj_weight, preferred_element_type=jnp.float32)
    block_out = (stream + update).astype(jnp.bfloat16).reshape(samples, places, width)
    flat_cot = cotangent.reshape(samples * places, width)
    dact_mid = lax.dot_general(
        flat_cot, proj_weight, (((1,), (1,)), ((), ())), preferred_element_type=jnp.float32
    )
    dpre_mid = dact_mid * gelu_slope(pre_mid)
    filter_output_gradient = back_norm(dpre_mid, normed_mid, gain_mid, spread_mid, counted).astype(
        jnp.bfloat16
    )
    dconv_shaped = filter_output_gradient.reshape(samples, places, central_window)
    grad_before = passed_along(dconv_shaped, SEQ, 8)
    grad_after = passed_along(dconv_shaped, SEQ, -8)
    stacked_windows = jnp.concatenate([grad_after, dconv_shaped, grad_before], axis=2).reshape(
        samples * places, 3 * central_window
    )
    part_conv = lax.dot_general(
        act_in, stacked_windows, (((0,), (0,)), ((), ())), preferred_element_type=jnp.float32
    )
    part_proj = lax.dot_general(
        flat_cot, act_mid, (((0,), (0,)), ((), ())), preferred_element_type=jnp.float32
    )
    shares = side_by_side((part_conv, part_proj), (("seq_0", "seq_1"), "seq_2"), 0, 1)
    conv_grad, proj_grad = (
        over_copies_2(shares[0].astype(jnp.bfloat16), "dp").astype(jnp.float32),
        over_copies_2(shares[1].astype(jnp.bfloat16), "dp").astype(jnp.float32),
    )
    dact_in = lax.dot_general(
        stacked_windows, conv_weight, (((1,), (1,)), ((), ())), preferred_element_type=jnp.float32
    )
    dpre_in = dact_in * gelu_slope(pre_in)
    input_grad = (
        flat_cot.astype(jnp.float32) + back_norm(dpre_in, normed_in, gain_in, spread_in, counted)
    ).astype(jnp.bfloat16)
    return (block_out, input_grad.reshape(samples, places, width), conv_grad, proj_grad)


def solution(mesh):
    split = Mesh(mesh.devices.reshape(4, 8, 2, mesh.shape["dp"]), ("seq_0", "seq_1", "seq_2", "dp"))
    placed = (P("dp", SEQ, None), P("dp", SEQ, None), P(), P(), P(), P(), P(), P())
    return jax.shard_map(
        per_device,
        mesh=split,
        in_specs=placed,
        out_specs=(P("dp", SEQ, None), P("dp", SEQ, None), P(SEQ, None), P(SEQ, None)),
        check_vma=False,
    )
```

profile of v0, /device:TPU:8, one launch (start us, length us, event | category | flops | bytes accessed | tf_op | source)
XLA Modules:
  0.0 260.3 jit_solution(3247535770120525244)
XLA Ops:
  0.6 1.0 convert_reduce_fusion
  1.7 1.0 fusion.4
  2.7 15.8 %all_to_all.68 = f32[16,1,1536]{2,1,0:T(1,128)S(1)} all-to-all(f32[16,1,1536]{2,1,0:T(1,128)S(1)} %broadcast_in_dim.20), channel_id=1, replica_groups=mesh['seq_0'=4,'seq_1'=8,'seq_2'=2,'dp'=8] {'seq_2','dp'}, dimensions={0} | all-to-all | bytes 196608 | tf_op jit(solution)/shard_map/all_to_all | solution.py:14
  18.7 23.3 %all_to_all.69 = f32[32,1,1536]{2,1,0:T(1,128)S(1)} all-to-all(f32[32,1,1536]{2,1,0:T(1,128)S(1)} %broadcast_in_dim.21), channel_id=1, replica_groups=mesh['seq_0'=4,'seq_1'=8,'seq_2'=2,'dp'=8] {'seq_0','seq_1'}, dimensions={0} | all-to-all | bytes 393216 | tf_op jit(solution)/shard_map/all_to_all | solution.py:14
  42.2 1.1 fusion.15
  43.3 3.7 %collective-permute-start = (bf16[1,128,768]{2,1,0:T(8,128)(2,1)S(1)}, bf16[1,128,768]{2,1,0:T(8,128)(2,1)S(1)}, u32[]{:S(2)}, u32[]{:S(2)}) collective-permute-start(bf16[1,128,768]{2,1,0:T(8,128)(2,1)S(1)} %fusion.15), channel_id=1, source_target_pairs={{0,64},{8,72},{16,80},{24,88},{32,96},{40,104},{48,112},{56,120},{... | collective-permute-start | bytes 589832 | tf_op jit(solution)/shard_map/ppermute | solution.py:37
  47.1 1.3 collective-permute-start.1
  48.4 1.5 fusion.21
  49.9 2.3 collective-permute-done
  52.4 10.3 %collective-permute-done.1 = bf16[1,128,768]{2,1,0:T(8,128)(2,1)S(1)} collective-permute-done((bf16[1,128,768]{2,1,0:T(8,128)(2,1)S(1)}, bf16[1,128,768]{2,1,0:T(8,128)(2,1)S(1)}, u32[]{:S(2)}, u32[]{:S(2)}) %collective-permute-start.1) | collective-permute-done | bytes 196640 | tf_op jit(solution)/shard_map/ppermute | solution.py:37
  63.0 10.3 %all_to_all.70 = f32[16,1,512]{2,1,0:T(1,128)S(1)} all-to-all(f32[16,1,512]{2,1,0:T(1,128)S(1)} %broadcast_in_dim.22), channel_id=1, replica_groups=mesh['seq_0'=4,'seq_1'=8,'seq_2'=2,'dp'=8] {'seq_2','dp'}, dimensions={0} | all-to-all | bytes 65536 | tf_op jit(solution)/shard_map/all_to_all | solution.py:14
  73.4 19.6 %all_to_all.71 = f32[32,1,512]{2,1,0:T(1,128)S(1)} all-to-all(f32[32,1,512]{2,1,0:T(1,128)S(1)} %broadcast_in_dim.23), channel_id=1, replica_groups=mesh['seq_0'=4,'seq_1'=8,'seq_2'=2,'dp'=8] {'seq_0','seq_1'}, dimensions={0} | all-to-all | bytes 131072 | tf_op jit(solution)/shard_map/all_to_all | solution.py:14
  93.1 0.3 fusion.53
  93.5 10.2 %all_to_all.72 = f32[16,1,512]{2,1,0:T(1,128)S(1)} all-to-all(f32[16,1,512]{2,1,0:T(1,128)S(1)} %broadcast_in_dim.24), channel_id=1, replica_groups=mesh['seq_0'=4,'seq_1'=8,'seq_2'=2,'dp'=8] {'seq_2','dp'}, dimensions={0} | all-to-all | bytes 65536 | tf_op jit(solution)/shard_map/all_to_all | solution.py:14
  103.8 13.2 %all_to_all.73 = f32[32,1,512]{2,1,0:T(1,128)S(1)} all-to-all(f32[32,1,512]{2,1,0:T(1,128)S(1)} %broadcast_in_dim.25), channel_id=1, replica_groups=mesh['seq_0'=4,'seq_1'=8,'seq_2'=2,'dp'=8] {'seq_0','seq_1'}, dimensions={0} | all-to-all | bytes 131072 | tf_op jit(solution)/shard_map/all_to_all | solution.py:14
  117.0 1.3 collective-permute-start.2
  118.3 8.5 %collective-permute-start.3 = (bf16[1,128,256]{2,1,0:T(8,128)(2,1)S(1)}, bf16[1,128,256]{2,1,0:T(8,128)(2,1)S(1)}, u32[]{:S(2)}, u32[]{:S(2)}) collective-permute-start(bf16[1,128,256]{2,1,0:T(8,128)(2,1)S(1)} %fusion.41), channel_id=1, source_target_pairs={{0,64},{8,72},{16,80},{24,88},{32,96},{40,104},{48,112},{56,120},{... | collective-permute-start | bytes 196616 | tf_op jit(solution)/shard_map/ppermute | solution.py:37
  126.8 0.3 convolution_bitcast_fusion
  127.2 1.8 collective-permute-done.3
  128.9 1.4 fusion.52
  130.3 0.7 broadcast_in_dim.52
  131.0 4.9 %all-to-all-start.6 = ((f32[16,1,1536]{2,1,0:T(1,128)}), f32[16,1,1536]{2,1,0:T(1,128)}, u32[]{:S(2)}, u32[]{:S(2)}) async-start(f32[16,1,1536]{2,1,0:T(1,128)} %broadcast_in_dim.52), calls=%async_computation.6 | async-start | bytes 196608 | tf_op jit(solution)/shard_map/all_to_all | solution.py:14
  135.9 0.5 fusion.23
  136.4 1.9 pad_maximum_fusion
  138.3 2.4 copy.44
  140.7 2.1 reshape_reshape.3
  142.8 5.7 %copy.45 = f32[2,32,12,1024]{3,1,2,0:T(8,128)} copy(f32[2,32,12,1024]{3,2,0,1:T(8,128)} %bitcast.60) | data formatting | bytes 6291456 | tf_op jit(solution)/shard_map/transpose | solution.py:42
  148.5 3.9 %all-to-all-start.8 = ((f32[2,32,12,1024]{3,1,2,0:T(8,128)}), f32[2,32,12,1024]{3,1,2,0:T(8,128)S(1)}, u32[]{:S(2)}, u32[]{:S(2)}) async-start(f32[2,32,12,1024]{3,1,2,0:T(8,128)} %copy.45), calls=%async_computation.8 | async-start | bytes 6291456 | tf_op jit(solution)/shard_map/all_to_all | solution.py:47
  152.5 1.0 reduce_sum.194
  153.4 2.6 %all-to-all-done.8 = f32[2,32,12,1024]{3,1,2,0:T(8,128)S(1)} async-done(((f32[2,32,12,1024]{3,1,2,0:T(8,128)}), f32[2,32,12,1024]{3,1,2,0:T(8,128)S(1)}, u32[]{:S(2)}, u32[]{:S(2)}) %all-to-all-start.8) | async-done | bytes 3145760 | tf_op jit(solution)/shard_map/all_to_all | solution.py:47
  156.1 0.8 broadcast_in_dim.53
  156.8 8.9 %all-to-all-start.7 = ((f32[32,1,1536]{2,1,0:T(1,128)}), f32[32,1,1536]{2,1,0:T(1,128)}, u32[]{:S(2)}, u32[]{:S(2)}) async-start(f32[32,1,1536]{2,1,0:T(1,128)} %broadcast_in_dim.53), calls=%async_computation.7 | async-start | bytes 393216 | tf_op jit(solution)/shard_map/all_to_all | solution.py:14
  165.7 1.6 reduce_sum.196
  167.3 3.7 %copy.46 = f32[32,12,1024]{2,1,0:T(8,128)} copy(f32[32,12,1024]{2,0,1:T(8,128)} %reduce_sum.196) | data formatting | bytes 3145728 | tf_op jit(solution)/shard_map/reduce_sum | solution.py:48
  171.0 6.4 %all-to-all-done.7 = f32[32,1,1536]{2,1,0:T(1,128)} async-done(((f32[32,1,1536]{2,1,0:T(1,128)}), f32[32,1,1536]{2,1,0:T(1,128)}, u32[]{:S(2)}, u32[]{:S(2)}) %all-to-all-start.7) | async-done | bytes 196640 | tf_op jit(solution)/shard_map/all_to_all | solution.py:14
  177.4 4.1 %all-to-all-start.9 = ((f32[32,12,1024]{2,1,0:T(8,128)}), f32[32,12,1024]{2,1,0:T(8,128)S(1)}, u32[]{:S(2)}, u32[]{:S(2)}) async-start(f32[32,12,1024]{2,1,0:T(8,128)} %copy.46), calls=%async_computation.9 | async-start | bytes 4194304 | tf_op jit(solution)/shard_map/all_to_all | solution.py:55
  181.6 0.9 fusion.1
  182.5 1.1 reduce_sum.195
  183.5 47.5 %all-to-all-done.9 = f32[32,12,1024]{2,1,0:T(8,128)S(1)} async-done(((f32[32,12,1024]{2,1,0:T(8,128)}), f32[32,12,1024]{2,1,0:T(8,128)S(1)}, u32[]{:S(2)}, u32[]{:S(2)}) %all-to-all-start.9) | async-done | bytes 1572896 | tf_op jit(solution)/shard_map/all_to_all | solution.py:55
  231.2 0.6 broadcast_in_dim.55
  231.8 7.2 %all-to-all-start.11 = ((bf16[8,12,256]{2,1,0:T(8,128)(2,1)}), bf16[8,12,256]{2,1,0:T(8,128)(2,1)S(1)}, u32[]{:S(2)}, u32[]{:S(2)}) async-start(bf16[8,12,256]{2,1,0:T(8,128)(2,1)} %broadcast_in_dim.55), calls=%async_computation.11 | async-start | bytes 131072 | tf_op jit(solution)/shard_map/all_to_all | solution.py:14
  239.0 6.9 %all-to-all-done.11 = bf16[8,12,256]{2,1,0:T(8,128)(2,1)S(1)} async-done(((bf16[8,12,256]{2,1,0:T(8,128)(2,1)}), bf16[8,12,256]{2,1,0:T(8,128)(2,1)S(1)}, u32[]{:S(2)}, u32[]{:S(2)}) %all-to-all-start.11) | async-done | bytes 49184 | tf_op jit(solution)/shard_map/all_to_all | solution.py:14
  245.9 0.7 broadcast_in_dim.54
  246.6 4.8 %all-to-all-start.10 = ((bf16[8,12,768]{2,1,0:T(8,128)(2,1)}), bf16[8,12,768]{2,1,0:T(8,128)(2,1)S(1)}, u32[]{:S(2)}, u32[]{:S(2)}) async-start(bf16[8,12,768]{2,1,0:T(8,128)(2,1)} %broadcast_in_dim.54), calls=%async_computation.10 | async-start | bytes 393216 | tf_op jit(solution)/shard_map/all_to_all | solution.py:14
  251.4 0.8 fusion.35
  252.2 0.6 convert_reduce_fusion.2
  252.9 6.7 %all-to-all-done.10 = bf16[8,12,768]{2,1,0:T(8,128)(2,1)S(1)} async-done(((bf16[8,12,768]{2,1,0:T(8,128)(2,1)}), bf16[8,12,768]{2,1,0:T(8,128)(2,1)S(1)}, u32[]{:S(2)}, u32[]{:S(2)}) %all-to-all-start.10) | async-done | bytes 147488 | tf_op jit(solution)/shard_map/all_to_all | solution.py:14
  259.6 0.7 convert_reduce_fusion.1
  (68 shorter events, 1.5 us)
Async XLA Ops:
  0.6 92.4 %copy-start = (bf16[256,768]{1,0:T(8,128)(2,1)S(1)}, bf16[256,768]{1,0:T(8,128)(2,1)}, u32[]{:S(2)}) copy-start(bf16[256,768]{1,0:T(8,128)(2,1)} %param.11) | copy-start | bytes 1179652
  18.7 33.5 %copy-start.7 = (bf16[768,768]{1,0:T(8,128)(2,1)S(1)}, bf16[768,768]{1,0:T(8,128)(2,1)}, u32[]{:S(2)}) copy-start(bf16[768,768]{1,0:T(8,128)(2,1)} %param.10) | copy-start | bytes 3538948
  43.3 49.8 %copy-start.5 = (bf16[1,128,768]{2,1,0:T(8,128)(2,1)S(1)}, bf16[1,128,768]{2,1,0:T(8,128)(2,1)}, u32[]{:S(2)}) copy-start(bf16[1,128,768]{2,1,0:T(8,128)(2,1)} %param.9) | copy-start | bytes 589828
  43.3 49.8 %copy-start.16 = (f32[256]{0:T(256)S(1)}, f32[256]{0:T(256)}, u32[]{:S(2)}) copy-start(f32[256]{0:T(256)} %param.14) | copy-start | bytes 3076
  43.3 49.8 %copy-start.18 = (f32[256]{0:T(256)S(1)}, f32[256]{0:T(256)}, u32[]{:S(2)}) copy-start(f32[256]{0:T(256)} %param.15) | copy-start | bytes 3076
  43.3 8.8 %collective-permute-start = (bf16[1,128,768]{2,1,0:T(8,128)(2,1)S(1)}, bf16[1,128,768]{2,1,0:T(8,128)(2,1)S(1)}, u32[]{:S(2)}, u32[]{:S(2)}) collective-permute-start(bf16[1,128,768]{2,1,0:T(8,128)(2,1)S(1)} %fusion.15), channel_id=1, source_target_pairs={{0,64},{8,72},{16,80},{24,88},{32,96},{40,104},{48,112},{56,120},{... | collective-permute-start | bytes 589832 | tf_op jit(solution)/shard_map/ppermute | solution.py:37
  47.1 15.6 %collective-permute-start.1 = (bf16[1,128,768]{2,1,0:T(8,128)(2,1)S(1)}, bf16[1,128,768]{2,1,0:T(8,128)(2,1)S(1)}, u32[]{:S(2)}, u32[]{:S(2)}) collective-permute-start(bf16[1,128,768]{2,1,0:T(8,128)(2,1)S(1)} %fusion.15), channel_id=1, source_target_pairs={{64,0},{72,8},{80,16},{88,24},{96,32},{104,40},{112,48},{120,56},{... | collective-permute-start | bytes 589832 | tf_op jit(solution)/shard_map/ppermute | solution.py:37
  62.9 67.4 %copy-start.3 = (f32[128,256]{1,0:T(8,128)}, f32[128,256]{1,0:T(8,128)S(1)}, u32[]{:S(2)}) copy-start(f32[128,256]{1,0:T(8,128)S(1)} %get-tuple-element.18) | copy-start | bytes 393220
  62.9 66.0 %copy-start.1 = (bf16[1,128,768]{2,1,0:T(8,128)(2,1)S(1)}, bf16[1,128,768]{2,1,0:T(8,128)(2,1)}, u32[]{:S(2)}) copy-start(bf16[1,128,768]{2,1,0:T(8,128)(2,1)} %param.8) | copy-start | bytes 589828
  62.9 66.0 %copy-start.9 = (f32[768]{0:T(1024)S(1)}, f32[768]{0:T(1024)}, u32[]{:S(2)}) copy-start(f32[768]{0:T(1024)} %param.12) | copy-start | bytes 9220
  62.9 66.0 %copy-start.15 = (f32[768]{0:T(1024)S(1)}, f32[768]{0:T(1024)}, u32[]{:S(2)}) copy-start(f32[768]{0:T(1024)} %param.13) | copy-start | bytes 9220
  93.0 37.3 %copy-start.11 = (f32[256]{0:T(256)}, f32[256]{0:T(256)S(1)}, u32[]{:S(2)}) copy-start(f32[256]{0:T(256)S(1)} %get-tuple-element.16) | copy-start | bytes 3076
  93.1 37.2 %copy-start.13 = (f32[256]{0:T(256)}, f32[256]{0:T(256)S(1)}, u32[]{:S(2)}) copy-start(f32[256]{0:T(256)S(1)} %get-tuple-element.17) | copy-start | bytes 3076
  117.0 10.1 %collective-permute-start.2 = (bf16[1,128,256]{2,1,0:T(8,128)(2,1)S(1)}, bf16[1,128,256]{2,1,0:T(8,128)(2,1)S(1)}, u32[]{:S(2)}, u32[]{:S(2)}) collective-permute-start(bf16[1,128,256]{2,1,0:T(8,128)(2,1)S(1)} %fusion.41), channel_id=1, source_target_pairs={{64,0},{72,8},{80,16},{88,24},{96,32},{104,40},{112,48},{120,56},{... | collective-permute-start | bytes 196616 | tf_op jit(solution)/shard_map/ppermute | solution.py:37
  118.3 10.6 %collective-permute-start.3 = (bf16[1,128,256]{2,1,0:T(8,128)(2,1)S(1)}, bf16[1,128,256]{2,1,0:T(8,128)(2,1)S(1)}, u32[]{:S(2)}, u32[]{:S(2)}) collective-permute-start(bf16[1,128,256]{2,1,0:T(8,128)(2,1)S(1)} %fusion.41), channel_id=1, source_target_pairs={{0,64},{8,72},{16,80},{24,88},{32,96},{40,104},{48,112},{56,120},{... | collective-permute-start | bytes 196616 | tf_op jit(solution)/shard_map/ppermute | solution.py:37
  131.0 17.5 %all-to-all-start.6 = ((f32[16,1,1536]{2,1,0:T(1,128)}), f32[16,1,1536]{2,1,0:T(1,128)}, u32[]{:S(2)}, u32[]{:S(2)}) async-start(f32[16,1,1536]{2,1,0:T(1,128)} %broadcast_in_dim.52), calls=%async_computation.6 | async-start | bytes 196608 | tf_op jit(solution)/shard_map/all_to_all | solution.py:14
  148.5 7.6 %all-to-all-start.8 = ((f32[2,32,12,1024]{3,1,2,0:T(8,128)}), f32[2,32,12,1024]{3,1,2,0:T(8,128)S(1)}, u32[]{:S(2)}, u32[]{:S(2)}) async-start(f32[2,32,12,1024]{3,1,2,0:T(8,128)} %copy.45), calls=%async_computation.8 | async-start | bytes 6291456 | tf_op jit(solution)/shard_map/all_to_all | solution.py:47
  156.8 20.5 %all-to-all-start.7 = ((f32[32,1,1536]{2,1,0:T(1,128)}), f32[32,1,1536]{2,1,0:T(1,128)}, u32[]{:S(2)}, u32[]{:S(2)}) async-start(f32[32,1,1536]{2,1,0:T(1,128)} %broadcast_in_dim.53), calls=%async_computation.7 | async-start | bytes 393216 | tf_op jit(solution)/shard_map/all_to_all | solution.py:14
  171.0 10.5 %copy-start.2 = (bf16[1,128,768]{2,1,0:T(8,128)(2,1)S(1)}, bf16[1,128,768]{2,1,0:T(8,128)(2,1)}, u32[]{:S(2)}) copy-start(bf16[1,128,768]{2,1,0:T(8,128)(2,1)} %param.8) | copy-start | bytes 589828
  171.0 10.5 %copy-start.4 = (f32[128,256]{1,0:T(8,128)S(1)}, f32[128,256]{1,0:T(8,128)}, u32[]{:S(2)}) copy-start(f32[128,256]{1,0:T(8,128)} %copy-done.3) | copy-start | bytes 393220
  171.0 10.5 %copy-start.12 = (f32[256]{0:T(256)S(1)}, f32[256]{0:T(256)}, u32[]{:S(2)}) copy-start(f32[256]{0:T(256)} %copy-done.11) | copy-start | bytes 3076
  171.0 10.5 %copy-start.14 = (f32[256]{0:T(256)S(1)}, f32[256]{0:T(256)}, u32[]{:S(2)}) copy-start(f32[256]{0:T(256)} %copy-done.13) | copy-start | bytes 3076
  171.0 10.5 %copy-start.17 = (f32[256]{0:T(256)S(1)}, f32[256]{0:T(256)}, u32[]{:S(2)}) copy-start(f32[256]{0:T(256)} %param.14) | copy-start | bytes 3076
  171.0 10.5 %copy-start.19 = (f32[256]{0:T(256)S(1)}, f32[256]{0:T(256)}, u32[]{:S(2)}) copy-start(f32[256]{0:T(256)} %param.15) | copy-start | bytes 3076
  177.4 53.7 %all-to-all-start.9 = ((f32[32,12,1024]{2,1,0:T(8,128)}), f32[32,12,1024]{2,1,0:T(8,128)S(1)}, u32[]{:S(2)}, u32[]{:S(2)}) async-start(f32[32,12,1024]{2,1,0:T(8,128)} %copy.46), calls=%async_computation.9 | async-start | bytes 4194304 | tf_op jit(solution)/shard_map/all_to_all | solution.py:55
  181.5 69.9 %copy-start.6 = (bf16[1,128,768]{2,1,0:T(8,128)(2,1)S(1)}, bf16[1,128,768]{2,1,0:T(8,128)(2,1)}, u32[]{:S(2)}) copy-start(bf16[1,128,768]{2,1,0:T(8,128)(2,1)} %param.9) | copy-start | bytes 589828
  181.5 69.9 %copy-start.8 = (f32[128,768]{1,0:T(8,128)S(1)}, f32[128,768]{1,0:T(8,128)}, u32[]{:S(2)}) copy-start(f32[128,768]{1,0:T(8,128)} %get-tuple-element.20) | copy-start | bytes 1179652
  181.5 69.9 %copy-start.10 = (f32[768]{0:T(1024)S(1)}, f32[768]{0:T(1024)}, u32[]{:S(2)}) copy-start(f32[768]{0:T(1024)} %param.12) | copy-start | bytes 9220
  231.8 14.1 %all-to-all-start.11 = ((bf16[8,12,256]{2,1,0:T(8,128)(2,1)}), bf16[8,12,256]{2,1,0:T(8,128)(2,1)S(1)}, u32[]{:S(2)}, u32[]{:S(2)}) async-start(bf16[8,12,256]{2,1,0:T(8,128)(2,1)} %broadcast_in_dim.55), calls=%async_computation.11 | async-start | bytes 131072 | tf_op jit(solution)/shard_map/all_to_all | solution.py:14
  246.6 13.0 %all-to-all-start.10 = ((bf16[8,12,768]{2,1,0:T(8,128)(2,1)}), bf16[8,12,768]{2,1,0:T(8,128)(2,1)S(1)}, u32[]{:S(2)}, u32[]{:S(2)}) async-start(bf16[8,12,768]{2,1,0:T(8,128)(2,1)} %broadcast_in_dim.54), calls=%async_computation.10 | async-start | bytes 393216 | tf_op jit(solution)/shard_map/all_to_all | solution.py:14
where the time goes:
time: 262 us; the launch traced here: 260 us
  blocking collectives  92.3 us (35%)
  waiting for transfers between devices  84.5 us (32%)
  starting transfers between devices  48.6 us (19%)
  local copies, waits for them, and re-layouts  17.1 us (7%)
  other arithmetic  11.5 us (4%)
  matrix products  5.39 us (2%)
    all_to_all x6, blocking collectives, copy_for_each(): return lax.all_to_all(copies, axis, split_axis=0, concat_axis=0, tiled=True)  92.3 us
    all_to_all x1, waiting for transfers between devices, sum_by_axis(): lax.all_to_all(nearer, far, split_axis=0, concat_axis=0, tiled=True)  47.5 us
    all_to_all x4, starting transfers between devices, copy_for_each(): return lax.all_to_all(copies, axis, split_axis=0, concat_axis=0, tiled=True)  25.8 us
    all_to_all x4, waiting for transfers between devices, copy_for_each(): return lax.all_to_all(copies, axis, split_axis=0, concat_axis=0, tiled=True)  20 us
    ppermute x4, starting transfers between devices, passed_along(): lax.ppermute(value, axis, [(source, source + steps) for source in range(f...  14.8 us
    ppermute x4, waiting for transfers between devices, passed_along(): lax.ppermute(value, axis, [(source, source + steps) for source in range(f...  14.3 us
    transpose x1, local copies, waits for them, and re-layouts, in_blocks(): return jnp.moveaxis(x.reshape(*before, devices, -1, *after), dim, 0)  5.69 us
  transfers between devices with their start and end apart: 10, of which 8 were waited for; matrix products, arithmetic and copies ran while one was open for 9% of the time, Pallas kernels for 0%

commit v1 on v0

v1 whole, which is shorter than its diff:
```python
import math

import jax
import jax.numpy as jnp
from jax import lax
from jax.sharding import Mesh
from jax.sharding import PartitionSpec as P

SEQ = ("x", "z_hi", "z_lo", "core")
CHAIN = ("x", "z_hi")
PLANE = ("x", "z_hi", "z_lo")
LINE = ("core", "dp")
BF16, F32 = jnp.bfloat16, jnp.float32


def exchange(pieces, axes):
    return lax.all_to_all(pieces, axes, split_axis=0, concat_axis=0, tiled=True)


def over_copies(x, axes):
    count = lax.axis_size(axes)
    return exchange(jnp.broadcast_to(x, (count, *x.shape)), axes).sum(axis=0)


def over_all(x):
    return over_copies(over_copies(x, LINE), PLANE)


def inner_tanh(value):
    coeff = math.sqrt(2.0 / math.pi)
    return jnp.tanh(coeff * (value + 0.044715 * value * value * value))


def gelu_tanh(value):
    return 0.5 * value * (1.0 + inner_tanh(value))


def gelu_slope(value):
    coeff = math.sqrt(2.0 / math.pi)
    inner = inner_tanh(value)
    return 0.5 * (1.0 + inner) + 0.5 * value * (1.0 - inner * inner) * coeff * (
        1.0 + 3.0 * 0.044715 * value * value
    )


def sums(a, b):
    return jnp.concatenate([jnp.sum(a, axis=0), jnp.sum(b, axis=0)])[None]


def moments(total, counted):
    center, second = jnp.split(total[0] / counted, 2)
    return center, jnp.sqrt(second - center * center + 1e-05)


def later(x, rows):
    return jnp.concatenate([jnp.zeros_like(x[:rows]), x[:-rows]], axis=0)


def earlier(x, rows):
    return jnp.concatenate([x[rows:], jnp.zeros_like(x[:rows])], axis=0)


def matmul(a, b, dims):
    return lax.dot_general(a, b, (dims, ((), ())), preferred_element_type=F32)


def per_device(inputs, cotangent, conv_weight, proj_weight, gain_in, bias_in, gain_mid, bias_mid):
    samples, places, width = inputs.shape
    rows = samples * places
    mid = proj_weight.shape[0]
    links = lax.axis_size(CHAIN)
    step = rows // links
    counted = rows * lax.axis_size(SEQ) * lax.axis_size("dp")
    own_in = inputs.reshape(rows, width)
    own_cot = cotangent.reshape(rows, width)

    with jax.named_scope("spread"):
        both = jnp.concatenate([own_in, own_cot], axis=1).reshape(links, step, 2 * width)
        both = exchange(both, CHAIN).reshape(rows, 2 * width)
    stream = own_in.astype(F32)
    with jax.named_scope("stat_in"):
        center_in, spread_in = moments(over_all(sums(stream, stream * stream)), counted)

    x, cot = both[:, :width], both[:, width:]
    normed_in = (x.astype(F32) - center_in) / spread_in
    pre_in = gain_in * normed_in + bias_in
    act_in = gelu_tanh(pre_in).astype(BF16)
    terms = matmul(act_in, conv_weight, ((1,), (0,)))
    conv = later(terms[:, :mid], step) + terms[:, mid : 2 * mid] + earlier(terms[:, 2 * mid :], step)
    with jax.named_scope("stat_mid"):
        center_mid, spread_mid = moments(over_all(sums(conv, conv * conv)), counted)
    normed_mid = (conv - center_mid) / spread_mid
    pre_mid = gain_mid * normed_mid + bias_mid
    act_mid = gelu_tanh(pre_mid).astype(BF16)
    dact_mid = matmul(cot, proj_weight, ((1,), (1,)))
    dpre_mid = dact_mid * gelu_slope(pre_mid)
    with jax.named_scope("back_mid"):
        total = over_all(sums(dpre_mid, dpre_mid * normed_mid))
        first, second = jnp.split(total[0] / counted, 2)
    dconv = (gain_mid * (dpre_mid - first - normed_mid * second) / spread_mid).astype(BF16)
    stacked = jnp.concatenate([earlier(dconv, step), dconv, later(dconv, step)], axis=1)

    part_conv = matmul(act_in, stacked, ((0,), (0,)))
    part_proj = matmul(cot, act_mid, ((0,), (0,)))
    half = (3 * mid + mid) // 2
    with jax.named_scope("grad_core"):
        parts = jnp.concatenate([part_conv, part_proj], axis=1).astype(BF16)
        parts = jnp.stack([parts[:, :half], parts[:, half:]])
        parts = exchange(parts, "core").astype(F32).sum(axis=0)
    with jax.named_scope("grad_plane"):
        planes = lax.axis_size(PLANE)
        block = exchange(parts.astype(BF16).reshape(planes, width // planes, half), PLANE)

    dact_in = matmul(stacked, conv_weight, ((1,), (1,)))
    dpre_in = dact_in * gelu_slope(pre_in)
    with jax.named_scope("gather"):
        back = jnp.concatenate([dpre_in.astype(BF16), act_mid], axis=1)
        back = exchange(back.reshape(links, step, width + mid), CHAIN).reshape(rows, width + mid)
    with jax.named_scope("back_in"):
        total = over_all(sums(dpre_in, dpre_in * normed_in))
        first, second = jnp.split(total[0] / counted, 2)
    normed = (stream - center_in) / spread_in
    dpre = back[:, :width].astype(F32)
    change = gain_in * (dpre - first - normed * second) / spread_in
    input_grad = (own_cot.astype(F32) + change).astype(BF16)
    block_out = (stream + matmul(back[:, width:], proj_weight, ((1,), (0,)))).astype(BF16)

    with jax.named_scope("grad_line"):
        cores, batch = lax.axis_size("core"), lax.axis_size("dp")
        block = block.astype(F32).sum(axis=0).astype(BF16).reshape(cores, 1, -1, half)
        block = jnp.broadcast_to(block, (cores, batch, *block.shape[2:]))
        block = exchange(block.reshape(cores * batch, -1, half), LINE)
        block = block.reshape(cores, batch, -1, half).astype(F32).sum(axis=1)
    grads = jnp.concatenate([block[0], block[1]], axis=1)
    return (
        block_out.reshape(inputs.shape),
        input_grad.reshape(inputs.shape),
        grads[:, : 3 * mid],
        grads[:, 3 * mid :],
    )


def solution(mesh):
    split = Mesh(
        mesh.devices.reshape(4, 2, 4, 2, mesh.shape["dp"]), ("x", "z_hi", "z_lo", "core", "dp")
    )
    rows = P("dp", SEQ, None)
    return jax.shard_map(
        per_device,
        mesh=split,
        in_specs=(rows, rows, P(), P(), P(), P(), P(), P()),
        out_specs=(rows, rows, P(SEQ, None), P(SEQ, None)),
        check_vma=False,
    )
```

time: 262 us -> 210 us (0.80)
  blocking collectives: 92.3 us -> 67 us
  local copies, waits for them, and re-layouts: 17.1 us -> 6.22 us
  starting transfers between devices: 48.6 us -> 42.2 us
  waiting for transfers between devices: 84.5 us -> 80 us
    all_to_all x6 -> x5, blocking collectives: 92.3 us -> 67 us  [exchange(): return lax.all_to_all(pieces, axes, split_axis=0, concat_axis=0, tiled=True)]
    ppermute x4 -> x0, starting transfers between devices: 14.8 us -> none  [passed_along(): lax.ppermute(value, axis, [(source, source + steps) for source in range(f...]
    ppermute x4 -> x0, waiting for transfers between devices: 14.3 us -> none  [passed_along(): lax.ppermute(value, axis, [(source, source + steps) for source in range(f...]
    all_to_all x6 -> x8, waiting for transfers between devices: 70.1 us -> 80 us  [exchange(): return lax.all_to_all(pieces, axes, split_axis=0, concat_axis=0, tiled=True)]
    all_to_all x6 -> x8, starting transfers between devices: 33.8 us -> 42.2 us  [exchange(): return lax.all_to_all(pieces, axes, split_axis=0, concat_axis=0, tiled=True)]
    transpose x1 -> x0, local copies, waits for them, and re-layouts: 5.69 us -> none  [in_blocks(): return jnp.moveaxis(x.reshape(*before, devices, -1, *after), dim, 0)]
    reduce_sum x14, other arithmetic: 7.5 us -> 4.47 us  [the longest x3 2.11 us: sums(): return jnp.concatenate([jnp.sum(a, axis=0), jnp.sum(b, axis=0)])[None]]
    dot_general x8 -> x6, matrix products: 5.39 us -> 3.84 us  [matmul(): return lax.dot_general(a, b, (dims, ((), ())), preferred_element_type=F32)]
  transfers between devices with their start and end apart: 10 -> 8, of which waited for: 8 -> 8; matrix products, arithmetic and copies ran while one was open for 9% -> 3% of each run, Pallas kernels for 0% -> 0%
where the time goes in v1:
time: 210 us; the launch traced here: 209 us
  waiting for transfers between devices  80 us (38%)
  blocking collectives  67 us (32%)
  starting transfers between devices  42.2 us (20%)
  other arithmetic  8.99 us (4%)
  local copies, waits for them, and re-layouts  6.22 us (3%)
  matrix products  3.84 us (2%)
    all_to_all x8, waiting for transfers between devices, exchange(): return lax.all_to_all(pieces, axes, split_axis=0, concat_axis=0, tiled=True)  80 us
    all_to_all x5, blocking collectives, exchange(): return lax.all_to_all(pieces, axes, split_axis=0, concat_axis=0, tiled=True)  67 us
    all_to_all x8, starting transfers between devices, exchange(): return lax.all_to_all(pieces, axes, split_axis=0, concat_axis=0, tiled=True)  42.2 us
  transfers between devices with their start and end apart: 8, of which 8 were waited for; matrix products, arithmetic and copies ran while one was open for 3% of the time, Pallas kernels for 0%

profile of v1, /device:TPU:8, one launch (start us, length us, event | category | flops | bytes accessed | tf_op | source)
XLA Modules:
  0.0 209.3 jit_solution(11213209208596754237)
XLA Ops:
  0.7 1.1 convert_reduce_fusion
  1.8 1.0 fusion.5
  2.8 15.8 %all_to_all.65 = f32[16,1,1536]{2,1,0:T(1,128)S(1)} all-to-all(f32[16,1,1536]{2,1,0:T(1,128)S(1)} %broadcast_in_dim.20), channel_id=1, replica_groups=mesh['x'=4,'z_hi'=2,'z_lo'=4,'core'=2,'dp'=8] {'core','dp'}, dimensions={0} | all-to-all | bytes 196608 | tf_op jit(solution)/shard_map/stat_in/all_to_all | solution.py:17
  18.7 0.8 broadcast_in_dim.21
  19.5 12.3 %all-to-all-start.2 = ((f32[32,1,1536]{2,1,0:T(1,128)}), f32[32,1,1536]{2,1,0:T(1,128)S(1)}, u32[]{:S(2)}, u32[]{:S(2)}) async-start(f32[32,1,1536]{2,1,0:T(1,128)} %broadcast_in_dim.21), calls=%async_computation.2 | async-start | bytes 393216 | tf_op jit(solution)/shard_map/stat_in/all_to_all | solution.py:17
  31.8 0.8 pad_maximum_fusion.2
  32.6 10.3 %all-to-all-done.2 = f32[32,1,1536]{2,1,0:T(1,128)S(1)} async-done(((f32[32,1,1536]{2,1,0:T(1,128)}), f32[32,1,1536]{2,1,0:T(1,128)S(1)}, u32[]{:S(2)}, u32[]{:S(2)}) %all-to-all-start.2) | async-done | bytes 196640 | tf_op jit(solution)/shard_map/stat_in/all_to_all | solution.py:17
  42.9 3.7 %all-to-all-start = ((bf16[8,16,1536]{2,1,0:T(8,128)(2,1)}), bf16[8,16,1536]{2,1,0:T(8,128)(2,1)S(1)}, u32[]{:S(2)}, u32[]{:S(2)}) async-start(bf16[8,16,1536]{2,1,0:T(8,128)(2,1)} %pad_maximum_fusion.2), calls=%async_computation | async-start | bytes 786432 | tf_op jit(solution)/shard_map/spread/all_to_all | solution.py:17
  46.5 0.1 reduce_sum.180
  46.7 12.0 %all-to-all-done = bf16[8,16,1536]{2,1,0:T(8,128)(2,1)S(1)} async-done(((bf16[8,16,1536]{2,1,0:T(8,128)(2,1)}), bf16[8,16,1536]{2,1,0:T(8,128)(2,1)S(1)}, u32[]{:S(2)}, u32[]{:S(2)}) %all-to-all-start) | async-done | bytes 393248 | tf_op jit(solution)/shard_map/spread/all_to_all | solution.py:17
  58.7 0.4 fusion.36
  59.3 10.1 %all_to_all.66 = f32[16,1,512]{2,1,0:T(1,128)S(1)} all-to-all(f32[16,1,512]{2,1,0:T(1,128)S(1)} %broadcast_in_dim.22), channel_id=1, replica_groups=mesh['x'=4,'z_hi'=2,'z_lo'=4,'core'=2,'dp'=8] {'core','dp'}, dimensions={0} | all-to-all | bytes 65536 | tf_op jit(solution)/shard_map/stat_mid/all_to_all | solution.py:17
  69.5 17.8 %all_to_all.67 = f32[32,1,512]{2,1,0:T(1,128)S(1)} all-to-all(f32[32,1,512]{2,1,0:T(1,128)S(1)} %broadcast_in_dim.23), channel_id=1, replica_groups=mesh['x'=4,'z_hi'=2,'z_lo'=4,'core'=2,'dp'=8] {'x','z_hi','z_lo'}, dimensions={0} | all-to-all | bytes 131072 | tf_op jit(solution)/shard_map/stat_mid/all_to_all | solution.py:17
  87.4 0.3 fusion.38
  87.8 10.2 %all_to_all.68 = f32[16,1,512]{2,1,0:T(1,128)S(1)} all-to-all(f32[16,1,512]{2,1,0:T(1,128)S(1)} %broadcast_in_dim.24), channel_id=1, replica_groups=mesh['x'=4,'z_hi'=2,'z_lo'=4,'core'=2,'dp'=8] {'core','dp'}, dimensions={0} | all-to-all | bytes 65536 | tf_op jit(solution)/shard_map/back_mid/all_to_all | solution.py:17
  98.1 13.2 %all_to_all.69 = f32[32,1,512]{2,1,0:T(1,128)S(1)} all-to-all(f32[32,1,512]{2,1,0:T(1,128)S(1)} %broadcast_in_dim.25), channel_id=1, replica_groups=mesh['x'=4,'z_hi'=2,'z_lo'=4,'core'=2,'dp'=8] {'x','z_hi','z_lo'}, dimensions={0} | all-to-all | bytes 131072 | tf_op jit(solution)/shard_map/back_mid/all_to_all | solution.py:17
  111.3 0.1 divide_convert_fusion
  111.4 1.3 fusion.37
  112.7 0.6 convolution_convert_fusion
  113.3 0.3 convolution_convert_fusion.1
  113.6 0.1 slice_bitcast_fusion
  113.7 1.3 pad_maximum_fusion
  115.0 3.8 %all-to-all-start.10 = ((bf16[2,768,512]{1,2,0:T(8,128)(2,1)}), bf16[2,768,512]{1,2,0:T(8,128)(2,1)S(1)}, u32[]{:S(2)}, u32[]{:S(2)}) async-start(bf16[2,768,512]{1,2,0:T(8,128)(2,1)} %pad_maximum_fusion), calls=%async_computation.10 | async-start | bytes 3145728 | tf_op jit(solution)/shard_map/grad_core/all_to_all | solution.py:17
  118.8 2.5 %all-to-all-done.10 = bf16[2,768,512]{1,2,0:T(8,128)(2,1)S(1)} async-done(((bf16[2,768,512]{1,2,0:T(8,128)(2,1)}), bf16[2,768,512]{1,2,0:T(8,128)(2,1)S(1)}, u32[]{:S(2)}, u32[]{:S(2)}) %all-to-all-start.10) | async-done | bytes 1572896 | tf_op jit(solution)/shard_map/grad_core/all_to_all | solution.py:17
  121.3 0.7 broadcast_in_dim.26
  122.0 4.5 %all-to-all-start.8 = ((f32[16,1,1536]{2,1,0:T(1,128)}), f32[16,1,1536]{2,1,0:T(1,128)S(1)}, u32[]{:S(2)}, u32[]{:S(2)}) async-start(f32[16,1,1536]{2,1,0:T(1,128)} %broadcast_in_dim.26), calls=%async_computation.8 | async-start | bytes 196608 | tf_op jit(solution)/shard_map/back_in/all_to_all | solution.py:17
  126.6 0.7 pad_maximum_fusion.3
  127.3 6.9 %all-to-all-done.8 = f32[16,1,1536]{2,1,0:T(1,128)S(1)} async-done(((f32[16,1,1536]{2,1,0:T(1,128)}), f32[16,1,1536]{2,1,0:T(1,128)S(1)}, u32[]{:S(2)}, u32[]{:S(2)}) %all-to-all-start.8) | async-done | bytes 98336 | tf_op jit(solution)/shard_map/back_in/all_to_all | solution.py:17
  134.2 3.4 %all-to-all-start.7 = ((bf16[8,16,1024]{2,1,0:T(8,128)(2,1)}), bf16[8,16,1024]{2,1,0:T(8,128)(2,1)S(1)}, u32[]{:S(2)}, u32[]{:S(2)}) async-start(bf16[8,16,1024]{2,1,0:T(8,128)(2,1)} %bitcast.4), calls=%async_computation.7 | async-start | bytes 524288 | tf_op jit(solution)/shard_map/gather/all_to_all | solution.py:17
  137.6 0.1 reduce_sum.191
  137.7 11.2 %all-to-all-done.7 = bf16[8,16,1024]{2,1,0:T(8,128)(2,1)S(1)} async-done(((bf16[8,16,1024]{2,1,0:T(8,128)(2,1)}), bf16[8,16,1024]{2,1,0:T(8,128)(2,1)S(1)}, u32[]{:S(2)}, u32[]{:S(2)}) %all-to-all-start.7) | async-done | bytes 262176 | tf_op jit(solution)/shard_map/gather/all_to_all | solution.py:17
  148.8 0.8 broadcast_in_dim.27
  149.6 6.5 %all-to-all-start.9 = ((f32[32,1,1536]{2,1,0:T(1,128)}), f32[32,1,1536]{2,1,0:T(1,128)S(1)}, u32[]{:S(2)}, u32[]{:S(2)}) async-start(f32[32,1,1536]{2,1,0:T(1,128)} %broadcast_in_dim.27), calls=%async_computation.9 | async-start | bytes 393216 | tf_op jit(solution)/shard_map/back_in/all_to_all | solution.py:17
  156.1 1.4 reduce_sum.193
  157.5 2.3 %copy.25 = bf16[768,512]{1,0:T(8,128)(2,1)} copy(bf16[768,512]{0,1:T(8,128)(2,1)} %reduce_sum.193) | data formatting | bytes 1572864 | tf_op jit(solution)/shard_map/grad_core/reduce_sum | solution.py:109
  159.8 7.0 %all-to-all-done.9 = f32[32,1,1536]{2,1,0:T(1,128)S(1)} async-done(((f32[32,1,1536]{2,1,0:T(1,128)}), f32[32,1,1536]{2,1,0:T(1,128)S(1)}, u32[]{:S(2)}, u32[]{:S(2)}) %all-to-all-start.9) | async-done | bytes 196640 | tf_op jit(solution)/shard_map/back_in/all_to_all | solution.py:17
  166.9 4.0 %all-to-all-start.11 = ((bf16[32,24,512]{2,1,0:T(8,128)(2,1)}), bf16[32,24,512]{2,1,0:T(8,128)(2,1)S(1)}, u32[]{:S(2)}, u32[]{:S(2)}) async-start(bf16[32,24,512]{2,1,0:T(8,128)(2,1)} %bitcast.11), calls=%async_computation.11 | async-start | bytes 1572864 | tf_op jit(solution)/shard_map/grad_plane/all_to_all | solution.py:17
  170.9 0.9 fusion.1
  171.8 0.1 reduce_sum.192
  171.9 20.0 %all-to-all-done.11 = bf16[32,24,512]{2,1,0:T(8,128)(2,1)S(1)} async-done(((bf16[32,24,512]{2,1,0:T(8,128)(2,1)}), bf16[32,24,512]{2,1,0:T(8,128)(2,1)S(1)}, u32[]{:S(2)}, u32[]{:S(2)}) %all-to-all-start.11) | async-done | bytes 786464 | tf_op jit(solution)/shard_map/grad_plane/all_to_all | solution.py:17
  191.9 0.1 reduce_sum.194
  192.1 0.7 broadcast_in_dim.29
  192.8 4.0 %all-to-all-start.12 = ((bf16[16,12,512]{2,1,0:T(8,128)(2,1)}), bf16[16,12,512]{2,1,0:T(8,128)(2,1)S(1)}, u32[]{:S(2)}, u32[]{:S(2)}) async-start(bf16[16,12,512]{2,1,0:T(8,128)(2,1)} %bitcast.12), calls=%async_computation.12 | async-start | bytes 524288 | tf_op jit(solution)/shard_map/grad_line/all_to_all | solution.py:17
  196.8 0.8 fusion.22
  197.6 10.1 %all-to-all-done.12 = bf16[16,12,512]{2,1,0:T(8,128)(2,1)S(1)} async-done(((bf16[16,12,512]{2,1,0:T(8,128)(2,1)}), bf16[16,12,512]{2,1,0:T(8,128)(2,1)S(1)}, u32[]{:S(2)}, u32[]{:S(2)}) %all-to-all-start.12) | async-done | bytes 196640 | tf_op jit(solution)/shard_map/grad_line/all_to_all | solution.py:17
  207.7 0.3 convert_reduce_fusion.1
  208.1 0.6 slice.77
  208.7 0.6 pad_maximum_fusion.4
  (50 shorter events, 0.8 us)
Async XLA Ops:
  0.6 58.1 %copy-start = (bf16[768,768]{1,0:T(8,128)(2,1)S(1)}, bf16[768,768]{1,0:T(8,128)(2,1)}, u32[]{:S(2)}) copy-start(bf16[768,768]{1,0:T(8,128)(2,1)} %param.10) | copy-start | bytes 3538948
  0.6 31.1 %copy-start.1 = (bf16[1,128,768]{2,1,0:T(8,128)(2,1)S(1)}, bf16[1,128,768]{2,1,0:T(8,128)(2,1)}, u32[]{:S(2)}) copy-start(bf16[1,128,768]{2,1,0:T(8,128)(2,1)} %param.8) | copy-start | bytes 589828
  0.7 31.1 %copy-start.2 = (bf16[1,128,768]{2,1,0:T(8,128)(2,1)S(1)}, bf16[1,128,768]{2,1,0:T(8,128)(2,1)}, u32[]{:S(2)}) copy-start(bf16[1,128,768]{2,1,0:T(8,128)(2,1)} %param.9) | copy-start | bytes 589828
  18.7 40.0 %copy-start.7 = (f32[768]{0:T(1024)S(1)}, f32[768]{0:T(1024)}, u32[]{:S(2)}) copy-start(f32[768]{0:T(1024)} %param.12) | copy-start | bytes 9220
  18.7 40.0 %copy-start.10 = (f32[768]{0:T(1024)S(1)}, f32[768]{0:T(1024)}, u32[]{:S(2)}) copy-start(f32[768]{0:T(1024)} %param.13) | copy-start | bytes 9220
  19.5 23.4 %all-to-all-start.2 = ((f32[32,1,1536]{2,1,0:T(1,128)}), f32[32,1,1536]{2,1,0:T(1,128)S(1)}, u32[]{:S(2)}, u32[]{:S(2)}) async-start(f32[32,1,1536]{2,1,0:T(1,128)} %broadcast_in_dim.21), calls=%async_computation.2 | async-start | bytes 393216 | tf_op jit(solution)/shard_map/stat_in/all_to_all | solution.py:17
  42.9 15.9 %all-to-all-start = ((bf16[8,16,1536]{2,1,0:T(8,128)(2,1)}), bf16[8,16,1536]{2,1,0:T(8,128)(2,1)S(1)}, u32[]{:S(2)}, u32[]{:S(2)}) async-start(bf16[8,16,1536]{2,1,0:T(8,128)(2,1)} %pad_maximum_fusion.2), calls=%async_computation | async-start | bytes 786432 | tf_op jit(solution)/shard_map/spread/all_to_all | solution.py:17
  59.2 28.2 %copy-start.4 = (bf16[256,768]{1,0:T(8,128)(2,1)S(1)}, bf16[256,768]{1,0:T(8,128)(2,1)}, u32[]{:S(2)}) copy-start(bf16[256,768]{1,0:T(8,128)(2,1)} %param.11) | copy-start | bytes 1179652
  59.2 28.2 %copy-start.8 = (f32[256]{0:T(256)S(1)}, f32[256]{0:T(256)}, u32[]{:S(2)}) copy-start(f32[256]{0:T(256)} %param.15) | copy-start | bytes 3076
  59.2 28.2 %copy-start.9 = (f32[256]{0:T(256)S(1)}, f32[256]{0:T(256)}, u32[]{:S(2)}) copy-start(f32[256]{0:T(256)} %param.14) | copy-start | bytes 3076
  115.0 11.5 %copy-start.6 = (bf16[128,768]{1,0:T(8,128)(2,1)S(1)}, bf16[128,768]{1,0:T(8,128)(2,1)}, u32[]{:S(2)}) copy-start(bf16[128,768]{1,0:T(8,128)(2,1)} %get-tuple-element.13) | copy-start | bytes 589828
  115.0 6.3 %all-to-all-start.10 = ((bf16[2,768,512]{1,2,0:T(8,128)(2,1)}), bf16[2,768,512]{1,2,0:T(8,128)(2,1)S(1)}, u32[]{:S(2)}, u32[]{:S(2)}) async-start(bf16[2,768,512]{1,2,0:T(8,128)(2,1)} %pad_maximum_fusion), calls=%async_computation.10 | async-start | bytes 3145728 | tf_op jit(solution)/shard_map/grad_core/all_to_all | solution.py:17
  122.0 12.2 %all-to-all-start.8 = ((f32[16,1,1536]{2,1,0:T(1,128)}), f32[16,1,1536]{2,1,0:T(1,128)S(1)}, u32[]{:S(2)}, u32[]{:S(2)}) async-start(f32[16,1,1536]{2,1,0:T(1,128)} %broadcast_in_dim.26), calls=%async_computation.8 | async-start | bytes 196608 | tf_op jit(solution)/shard_map/back_in/all_to_all | solution.py:17
  134.2 14.7 %all-to-all-start.7 = ((bf16[8,16,1024]{2,1,0:T(8,128)(2,1)}), bf16[8,16,1024]{2,1,0:T(8,128)(2,1)S(1)}, u32[]{:S(2)}, u32[]{:S(2)}) async-start(bf16[8,16,1024]{2,1,0:T(8,128)(2,1)} %bitcast.4), calls=%async_computation.7 | async-start | bytes 524288 | tf_op jit(solution)/shard_map/gather/all_to_all | solution.py:17
  149.6 17.2 %all-to-all-start.9 = ((f32[32,1,1536]{2,1,0:T(1,128)}), f32[32,1,1536]{2,1,0:T(1,128)S(1)}, u32[]{:S(2)}, u32[]{:S(2)}) async-start(f32[32,1,1536]{2,1,0:T(1,128)} %broadcast_in_dim.27), calls=%async_computation.9 | async-start | bytes 393216 | tf_op jit(solution)/shard_map/back_in/all_to_all | solution.py:17
  159.8 11.1 %copy-start.5 = (bf16[256,768]{1,0:T(8,128)(2,1)S(1)}, bf16[256,768]{1,0:T(8,128)(2,1)}, u32[]{:S(2)}) copy-start(bf16[256,768]{1,0:T(8,128)(2,1)} %param.11) | copy-start | bytes 1179652
  166.9 25.1 %all-to-all-start.11 = ((bf16[32,24,512]{2,1,0:T(8,128)(2,1)}), bf16[32,24,512]{2,1,0:T(8,128)(2,1)S(1)}, u32[]{:S(2)}, u32[]{:S(2)}) async-start(bf16[32,24,512]{2,1,0:T(8,128)(2,1)} %bitcast.11), calls=%async_computation.11 | async-start | bytes 1572864 | tf_op jit(solution)/shard_map/grad_plane/all_to_all | solution.py:17
  170.9 25.9 %copy-start.3 = (bf16[1,128,768]{2,1,0:T(8,128)(2,1)S(1)}, bf16[1,128,768]{2,1,0:T(8,128)(2,1)}, u32[]{:S(2)}) copy-start(bf16[1,128,768]{2,1,0:T(8,128)(2,1)} %param.9) | copy-start | bytes 589828
  192.8 15.0 %all-to-all-start.12 = ((bf16[16,12,512]{2,1,0:T(8,128)(2,1)}), bf16[16,12,512]{2,1,0:T(8,128)(2,1)S(1)}, u32[]{:S(2)}, u32[]{:S(2)}) async-start(bf16[16,12,512]{2,1,0:T(8,128)(2,1)} %bitcast.12), calls=%async_computation.12 | async-start | bytes 524288 | tf_op jit(solution)/shard_map/grad_line/all_to_all | solution.py:17

commit v2 on v1

v2 whole, which is shorter than its diff:
```python
import math

import jax
import jax.numpy as jnp
from jax import lax
from jax.experimental import pallas as pl
from jax.experimental.pallas import tpu as pltpu
from jax.sharding import Mesh
from jax.sharding import PartitionSpec as P

SEQ = ("x", "z_hi", "z_lo", "core")
PLANE = ("x", "z_hi", "z_lo")
LINE = ("core", "dp")
BF16, F32 = jnp.bfloat16, jnp.float32
CH, MID = 768, 256
ROWS, SHIFT = 128, 16
PLANES, LINES, BATCH = 32, 16, 8
HALF = 512
COUNTED = 8.0 * 8192.0
COEFF = math.sqrt(2.0 / math.pi)


def exchange(pieces, axes):
    return lax.all_to_all(pieces, axes, split_axis=0, concat_axis=0, tiled=True)


def kernel(body, *outs, name):
    shapes = tuple(jax.ShapeDtypeStruct(shape, dtype) for shape, dtype in outs)
    whole = pl.BlockSpec(memory_space=pltpu.VMEM)

    def call(*args):
        return pl.pallas_call(
            body,
            out_shape=shapes,
            in_specs=[whole] * len(args),
            out_specs=(whole,) * len(shapes),
            name=name,
        )(*args)

    return call


def matmul(a, b, dims):
    return lax.dot_general(a, b, (dims, ((), ())), preferred_element_type=F32)


def later(x):
    return jnp.concatenate([jnp.zeros_like(x[:SHIFT]), x[:-SHIFT]], axis=0)


def earlier(x):
    return jnp.concatenate([x[SHIFT:], jnp.zeros_like(x[:SHIFT])], axis=0)


def upper(shape):
    return lax.broadcasted_iota(jnp.int32, shape, 1) < shape[1] // 2


def woven(a, b):
    a, b = (v.astype(F32).reshape(ROWS // 8, 8, v.shape[1]) for v in (a, b))
    first = upper(a.shape)
    even = jnp.where(first, a, pltpu.roll(b, 4, axis=1))
    odd = jnp.where(first, pltpu.roll(a, 4, axis=1), b)
    pieces = jnp.stack([even, odd], axis=1)
    return pieces.reshape(PLANES, 8, a.shape[2]).astype(BF16)


def unwoven(pieces):
    pairs = pieces.astype(F32).reshape(ROWS // 8, 2, 8, pieces.shape[2])
    even, odd = pairs[:, 0], pairs[:, 1]
    first = upper(even.shape)
    a = jnp.where(first, even, pltpu.roll(odd, 4, axis=1))
    b = jnp.where(first, pltpu.roll(even, 4, axis=1), odd)
    return a.reshape(ROWS, -1), b.reshape(ROWS, -1)


def split_up(value, parts, width):
    pieces = []
    for _ in range(parts):
        rounded = value.astype(BF16).astype(F32)
        pieces += [rounded[:, k : k + width] for k in range(0, value.shape[1], width)]
        value = value - rounded
    row = lax.broadcasted_iota(jnp.int32, (8, width), 0)
    tile = jnp.zeros((8, width), F32)
    for k, piece in enumerate(pieces):
        tile = jnp.where(row == k, piece, tile)
    return tile.astype(BF16)


def put_together(tile, parts, count):
    rows = [tile[k : k + 1] for k in range(parts * count)]
    return [sum(rows[k::count][1:], rows[k]) for k in range(count)]


def sum_rows(value):
    return jnp.sum(value, axis=0, keepdims=True)


def copies(ref, index, row):
    ref[:, :, index] = jnp.broadcast_to(row, (ref.shape[0], 1, row.shape[1]))


def tanh_of(value):
    return jnp.tanh(COEFF * (value + 0.044715 * value * value * value))


def gelu_of(value, inner):
    return 0.5 * value * (1.0 + inner)


def slope_of(value, inner):
    return 0.5 * (1.0 + inner) + 0.5 * value * (1.0 - inner * inner) * COEFF * (
        1.0 + 3.0 * 0.044715 * value * value
    )


def moments(totals, squares):
    center = totals * (1.0 / COUNTED)
    return center, jnp.sqrt(squares * (1.0 / COUNTED) - center * center + 1e-05)


def first_sums(x_ref, out_ref):
    x = x_ref[...].astype(F32)
    copies(out_ref, slice(0, CH), sum_rows(x))
    copies(out_ref, slice(CH, 2 * CH), sum_rows(x * x))


def spread_data(x_ref, cot_ref, out_ref):
    out_ref[...] = woven(x_ref[...], cot_ref[...])


def spread_all(data_ref, sums_ref, out_ref):
    total = jnp.sum(sums_ref[...], axis=0)
    tile = split_up(total, 3, CH)
    out_ref[:, 0:8, :] = data_ref[...]
    out_ref[:, 8:16, :] = jnp.broadcast_to(tile[None], (PLANES, 8, CH))


def forward_conv(
    got_ref, weight_ref, gain_ref, bias_ref, act_ref, conv_ref, sums_ref, stat_ref
):
    tile = jnp.sum(got_ref[:, 8:16, :].astype(F32), axis=0)
    center, spread = moments(*put_together(tile, 3, 2))
    stat_ref[0:1, :] = center
    stat_ref[1:2, :] = spread
    x, _ = unwoven(got_ref[:, 0:8, :])
    pre = gain_ref[...] * ((x - center) / spread) + bias_ref[...]
    act = gelu_of(pre, tanh_of(pre)).astype(BF16)
    act_ref[...] = act
    terms = matmul(act, weight_ref[...], ((1,), (0,)))
    conv = later(terms[:, :MID]) + terms[:, MID : 2 * MID] + earlier(terms[:, 2 * MID :])
    conv_ref[...] = conv
    copies(sums_ref, slice(0, MID), sum_rows(conv))
    copies(sums_ref, slice(MID, 2 * MID), sum_rows(conv * conv))


def beside_conv(got_ref, stat_ref, gain_ref, bias_ref, proj_ref, normed_ref, slope_ref, cot_ref, dact_ref):
    x, cot = unwoven(got_ref[:, 0:8, :])
    normed = (x - stat_ref[0:1, :]) / stat_ref[1:2, :]
    pre = gain_ref[...] * normed + bias_ref[...]
    normed_ref[...] = normed
    slope_ref[...] = slope_of(pre, tanh_of(pre))
    cot_ref[...] = cot.astype(BF16)
    dact_ref[...] = matmul(cot.astype(BF16), proj_ref[...], ((1,), (1,)))


def middle(got_ref, conv_ref, dact_ref, gain_ref, bias_ref, act_ref, normed_ref, dpre_ref, sums_ref, stat_ref):
    total = jnp.sum(got_ref[...], axis=0)
    center, spread = moments(total[:, :MID], total[:, MID:])
    stat_ref[...] = spread
    normed = (conv_ref[...] - center) / spread
    pre = gain_ref[...] * normed + bias_ref[...]
    inner = tanh_of(pre)
    act_ref[...] = gelu_of(pre, inner).astype(BF16)
    dpre = dact_ref[...] * slope_of(pre, inner)
    normed_ref[...] = normed
    dpre_ref[...] = dpre
    copies(sums_ref, slice(0, MID), sum_rows(dpre))
    copies(sums_ref, slice(MID, 2 * MID), sum_rows(dpre * normed))


def filter_parts(
    got_ref, dpre_ref, normed_ref, spread_ref, gain_ref, act_in_ref, act_ref, cot_ref, stacked_ref, parts_ref
):
    total = jnp.sum(got_ref[...], axis=0) * (1.0 / COUNTED)
    first, second = total[:, :MID], total[:, MID:]
    dconv = gain_ref[...] * (dpre_ref[...] - first - normed_ref[...] * second) / spread_ref[...]
    stacked = jnp.concatenate([earlier(dconv), dconv, later(dconv)], axis=1).astype(BF16)
    stacked_ref[...] = stacked
    conv_part = matmul(act_in_ref[...], stacked, ((0,), (0,)))
    parts_ref[0] = conv_part[:, :HALF].astype(BF16)
    parts_ref[1, :, : HALF - MID] = conv_part[:, HALF:].astype(BF16)
    proj_part = matmul(cot_ref[...], act_ref[...], ((0,), (0,)))
    parts_ref[1, :, HALF - MID :] = proj_part.astype(BF16)


def back_rows(stacked_ref, weight_ref, slope_ref, normed_ref, act_ref, out_ref, sums_ref):
    dpre = matmul(stacked_ref[...], weight_ref[...], ((1,), (1,))) * slope_ref[...]
    sums = jnp.concatenate([sum_rows(dpre), sum_rows(dpre * normed_ref[...])], axis=1)
    sums_ref[...] = split_up(sums, 2, HALF)
    tail = jnp.concatenate([dpre[:, HALF:], act_ref[...].astype(F32)], axis=1)
    out_ref[...] = woven(dpre[:, :HALF], tail)


def to_plane(parts_ref, rows_ref, sums_ref, out_ref):
    both = parts_ref[0].astype(F32) + parts_ref[1].astype(F32)
    out_ref[:, 0:24, :] = both.astype(BF16).reshape(PLANES, 24, HALF)
    out_ref[:, 24:32, :] = rows_ref[...]
    out_ref[:, 32:40, :] = jnp.broadcast_to(sums_ref[...][None], (PLANES, 8, HALF))


def to_line(got_ref, out_ref):
    block = jnp.sum(got_ref[:, 0:24, :].astype(F32), axis=0)
    tile = jnp.sum(got_ref[:, 32:40, :].astype(F32), axis=0)
    tile = split_up(jnp.concatenate(put_together(tile, 2, 3), axis=1), 2, HALF)
    own = (block[:16], pltpu.roll(block, 12, axis=0)[:16])
    for core in range(2):
        piece = own[core].astype(BF16)
        out_ref[core * BATCH : (core + 1) * BATCH, 0:16, :] = jnp.broadcast_to(
            piece[None], (BATCH, 16, HALF)
        )
    out_ref[:, 16:24, :] = jnp.broadcast_to(tile[None], (LINES, 8, HALF))


def block_rows(got_ref, x_ref, proj_ref, out_ref, dpre_ref):
    low, tail = unwoven(got_ref[:, 24:32, :])
    dpre_ref[:, :HALF] = low
    dpre_ref[:, HALF:] = tail[:, :MID]
    update = matmul(tail[:, MID:].astype(BF16), proj_ref[...], ((1,), (0,)))
    out_ref[...] = (x_ref[...].astype(F32) + update).astype(BF16)


def last_rows(got_ref, dpre_ref, x_ref, cot_ref, stat_ref, gain_ref, grad_ref, conv_ref, proj_ref):
    tile = jnp.sum(got_ref[:, 16:24, :].astype(F32), axis=0)
    total = jnp.concatenate(put_together(tile, 2, 3), axis=1) * (1.0 / COUNTED)
    first, second = total[:, :CH], total[:, CH:]
    center, spread = stat_ref[0:1, :], stat_ref[1:2, :]
    normed = (x_ref[...].astype(F32) - center) / spread
    change = gain_ref[...] * (dpre_ref[...] - first - normed * second) / spread
    grad_ref[...] = (cot_ref[...].astype(F32) + change).astype(BF16)
    left = jnp.sum(got_ref[0:BATCH, 0:16, :].astype(F32), axis=0)
    right = jnp.sum(got_ref[BATCH:LINES, 0:16, :].astype(F32), axis=0)
    conv_ref[:, :HALF] = left[:12]
    conv_ref[:, HALF:] = right[:12, : CH - HALF]
    proj_ref[...] = right[:12, CH - HALF :]


def per_device(inputs, cotangent, conv_weight, proj_weight, gain_in, bias_in, gain_mid, bias_mid):
    x = inputs.reshape(ROWS, CH)
    cot = cotangent.reshape(ROWS, CH)
    gain_in, bias_in, gain_mid, bias_mid = (v[None] for v in (gain_in, bias_in, gain_mid, bias_mid))
    rows, rows_mid = (ROWS, CH), (ROWS, MID)

    (sums,) = kernel(first_sums, ((LINES, 1, 2 * CH), F32), name="first_sums")(x)
    (data,) = kernel(spread_data, ((PLANES, 8, CH), BF16), name="spread_data")(x, cot)
    sums = exchange(sums, LINE)
    (both,) = kernel(spread_all, ((PLANES, 16, CH), BF16), name="spread_all")(data, sums)
    both = exchange(both, PLANE)

    act_in, conv, sums, stat_in = kernel(
        forward_conv,
        (rows, BF16),
        (rows_mid, F32),
        ((LINES, 1, 2 * MID), F32),
        ((8, CH), F32),
        name="forward_conv",
    )(both, conv_weight, gain_in, bias_in)
    normed_in, slope_in, far_cot, dact_mid = kernel(
        beside_conv, (rows, F32), (rows, F32), (rows, BF16), (rows_mid, F32), name="beside_conv"
    )(both, stat_in, gain_in, bias_in, proj_weight)
    sums = exchange(sums, LINE).sum(axis=0)
    sums = exchange(jnp.broadcast_to(sums, (PLANES, 1, 2 * MID)), PLANE)

    act_mid, normed_mid, dpre_mid, sums, spread_mid = kernel(
        middle,
        (rows_mid, BF16),
        (rows_mid, F32),
        (rows_mid, F32),
        ((LINES, 1, 2 * MID), F32),
        ((1, MID), F32),
        name="middle",
    )(sums, conv, dact_mid, gain_mid, bias_mid)
    sums = exchange(sums, LINE).sum(axis=0)
    sums = exchange(jnp.broadcast_to(sums, (PLANES, 1, 2 * MID)), PLANE)

    stacked, parts = kernel(
        filter_parts, (rows, BF16), ((2, CH, HALF), BF16), name="filter_parts"
    )(sums, dpre_mid, normed_mid, spread_mid, gain_mid, act_in, act_mid, far_cot)
    parts = exchange(parts, "core")
    back, sums = kernel(
        back_rows, ((PLANES, 8, HALF), BF16), ((8, HALF), BF16), name="back_rows"
    )(stacked, conv_weight, slope_in, normed_in, act_mid)
    (plane,) = kernel(to_plane, ((PLANES, 40, HALF), BF16), name="to_plane")(parts, back, sums)
    plane = exchange(plane, PLANE)
    (line,) = kernel(to_line, ((LINES, 24, HALF), BF16), name="to_line")(plane)
    line = exchange(line, LINE)
    block_out, dpre_in = kernel(block_rows, (rows, BF16), (rows, F32), name="block_rows")(
        plane, x, proj_weight
    )
    input_grad, conv_grad, proj_grad = kernel(
        last_rows, (rows, BF16), ((12, CH), F32), ((12, MID), F32), name="last_rows"
    )(line, dpre_in, x, cot, stat_in, gain_in)
    return (
        block_out.reshape(inputs.shape),
        input_grad.reshape(inputs.shape),
        conv_grad,
        proj_grad,
    )


def solution(mesh):
    split = Mesh(mesh.devices.reshape(4, 2, 4, 2, 8), ("x", "z_hi", "z_lo", "core", "dp"))
    rows = P("dp", SEQ, None)
    return jax.shard_map(
        per_device,
        mesh=split,
        in_specs=(rows, rows, P(), P(), P(), P(), P(), P()),
        out_specs=(rows, rows, P(SEQ, None), P(SEQ, None)),
        check_vma=False,
    )
```

time: 210 us -> 191 us (0.910)
  waiting for transfers between devices: 80 us -> 46.2 us
  Pallas kernels: 0 us -> 28.3 us
  other arithmetic: 8.99 us -> 0.08 us
  starting transfers between devices: 42.2 us -> 33.7 us
  blocking collectives: 67 us -> 74.8 us
  matrix products: 3.84 us -> 0 us
    all_to_all x8 -> x5, waiting for transfers between devices: 80 us -> 46.2 us  [exchange(): return lax.all_to_all(pieces, axes, split_axis=0, concat_axis=0, tiled=True)]
    pallas_call x0 -> x12, Pallas kernels: none -> 28.3 us  [call(): pl.pallas_call(body, out_shape=shapes, in_specs=[whole] * len(args), out_...]
    all_to_all x8 -> x5, starting transfers between devices: 42.2 us -> 33.7 us  [exchange(): return lax.all_to_all(pieces, axes, split_axis=0, concat_axis=0, tiled=True)]
    all_to_all x5 -> x4, blocking collectives: 67 us -> 74.8 us  [exchange(): return lax.all_to_all(pieces, axes, split_axis=0, concat_axis=0, tiled=True)]
    reduce_sum x14 -> x2, other arithmetic: 4.47 us -> 0.08 us  [per_device(): sums = exchange(sums, LINE).sum(axis=0)]
    unnamed x22 -> x14, local copies, waits for them, and re-layouts: 0.07 us -> 4.09 us
    dot_general x6 -> x0, matrix products: 3.84 us -> none  [matmul(): return lax.dot_general(a, b, (dims, ((), ())), preferred_element_type=F32)]
    reduce_sum x1 -> x0, local copies, waits for them, and re-layouts: 2.32 us -> none  [per_device(): parts = exchange(parts, 'core').astype(F32).sum(axis=0)]
  transfers between devices with their start and end apart: 8 -> 5, of which waited for: 8 -> 4; matrix products, arithmetic and copies ran while one was open for 3% -> 1% of each run, Pallas kernels for 0% -> 5%
where the time goes in v2:
time: 191 us; the launch traced here: 190 us
  blocking collectives  74.8 us (39%)
  waiting for transfers between devices  46.2 us (24%)
  starting transfers between devices  33.7 us (18%)
  Pallas kernels  28.3 us (15%)
  local copies, waits for them, and re-layouts  5.97 us (3%)
    all_to_all x4, blocking collectives, exchange(): return lax.all_to_all(pieces, axes, split_axis=0, concat_axis=0, tiled=True)  74.8 us
    all_to_all x5, waiting for transfers between devices, exchange(): return lax.all_to_all(pieces, axes, split_axis=0, concat_axis=0, tiled=True)  46.2 us
    all_to_all x5, starting transfers between devices, exchange(): return lax.all_to_all(pieces, axes, split_axis=0, concat_axis=0, tiled=True)  33.7 us
    pallas_call x12, Pallas kernels, call(): pl.pallas_call(body, out_shape=shapes, in_specs=[whole] * len(args), out_...  28.3 us
    unnamed x14, local copies, waits for them, and re-layouts  4.09 us
  transfers between devices with their start and end apart: 5, of which 4 were waited for; matrix products, arithmetic and copies ran while one was open for 1% of the time, Pallas kernels for 5%

profile of v2, /device:TPU:8, one launch (start us, length us, event | category | flops | bytes accessed | tf_op | source)
XLA Modules:
  0.0 189.8 jit_solution(8855882688166307074)
XLA Ops:
  0.6 1.6 first_sums.1
  2.3 9.1 %all-to-all-start = ((f32[16,1,1536]{2,1,0:T(1,128)}), f32[16,1,1536]{2,1,0:T(1,128)S(1)}, u32[]{:S(2)}, u32[]{:S(2)}) async-start(f32[16,1,1536]{2,1,0:T(1,128)} %first_sums.1), calls=%async_computation | async-start | bytes 196608 | tf_op jit(solution)/shard_map/all_to_all | solution.py:24
  11.3 1.9 spread_data.1.data_ref
  13.2 0.0 copy-start.5
  13.2 0.0 copy-start.6
  13.2 5.7 %all-to-all-done.sums_ref = f32[16,1,1536]{2,1,0:T(1,128)S(1)} async-done(((f32[16,1,1536]{2,1,0:T(1,128)}), f32[16,1,1536]{2,1,0:T(1,128)S(1)}, u32[]{:S(2)}, u32[]{:S(2)}) %all-to-all-start) | async-done | bytes 98336 | tf_op jit(solution)/shard_map/all_to_all | solution.py:24
  19.0 0.0 copy-start.3
  19.0 0.6 copy-done.3
  19.6 2.0 %spread_all.1 = bf16[32,16,768]{2,1,0:T(8,128)(2,1)} custom-call(bf16[32,8,768]{2,1,0:T(8,128)(2,1)} %spread_data.1.data_ref, f32[16,1,1536]{2,1,0:T(1,128)} %copy-done.3), custom_call_target="tpu_custom_call" | custom-call | tf_op jit(solution)/shard_map/spread_all/pallas_call | solution.py:32
  21.6 11.6 %all-to-all-start.1 = ((bf16[32,16,768]{2,1,0:T(8,128)(2,1)}), bf16[32,16,768]{2,1,0:T(8,128)(2,1)S(1)}, u32[]{:S(2)}, u32[]{:S(2)}) async-start(bf16[32,16,768]{2,1,0:T(8,128)(2,1)} %spread_all.1), calls=%async_computation.1 | async-start | bytes 1572864 | tf_op jit(solution)/shard_map/all_to_all | solution.py:24
  33.2 0.0 copy-done.5
  33.2 0.6 broadcast_in_dim.18.gain_ref
  33.8 0.0 copy-done.6
  33.8 0.6 broadcast_in_dim.19.bias_ref
  34.4 22.0 %all-to-all-done.1.got_ref = bf16[32,16,768]{2,1,0:T(8,128)(2,1)S(1)} async-done(((bf16[32,16,768]{2,1,0:T(8,128)(2,1)}), bf16[32,16,768]{2,1,0:T(8,128)(2,1)S(1)}, u32[]{:S(2)}, u32[]{:S(2)}) %all-to-all-start.1) | async-done | bytes 786464 | tf_op jit(solution)/shard_map/all_to_all | solution.py:24
  56.4 0.0 copy-start
  56.4 0.9 copy-done
  57.3 2.7 %forward_conv.1 = (bf16[128,768]{1,0:T(8,128)(2,1)}, f32[128,256]{1,0:T(8,128)}, f32[16,1,512]{2,1,0:T(1,128)}, f32[8,768]{1,0:T(8,128)}) custom-call(bf16[32,16,768]{2,1,0:T(8,128)(2,1)} %copy-done, bf16[768,768]{1,0:T(8,128)(2,1)} %weight_ref.3, f32[1,768]{1,0:T(1,128)} %broadcast_in_dim.18.gain_ref, f32[1,768]{1,0:T(1,128)} %broadcast_in_dim.19.bias_ref), custom_call_target="tpu_custom_call" | custom-call | tf_op jit(solution)/shard_map/forward_conv/pallas_call | solution.py:32
  60.0 10.5 %all_to_all.45 = f32[16,1,512]{2,1,0:T(1,128)S(1)} all-to-all(f32[16,1,512]{2,1,0:T(1,128)} %get-tuple-element.26), channel_id=1, replica_groups=mesh['x'=4,'z_hi'=2,'z_lo'=4,'core'=2,'dp'=8] {'core','dp'}, dimensions={0} | all-to-all | bytes 65536 | tf_op jit(solution)/shard_map/all_to_all | solution.py:24
  70.5 0.7 broadcast_in_dim.20
  71.2 4.7 %all-to-all-start.3 = ((f32[32,1,512]{2,1,0:T(1,128)}), f32[32,1,512]{2,1,0:T(1,128)S(1)}, u32[]{:S(2)}, u32[]{:S(2)}) async-start(f32[32,1,512]{2,1,0:T(1,128)} %broadcast_in_dim.20), calls=%async_computation.3 | async-start | bytes 131072 | tf_op jit(solution)/shard_map/all_to_all | solution.py:24
  76.0 2.6 %beside_conv.1 = (f32[128,768]{1,0:T(8,128)}, f32[128,768]{1,0:T(8,128)}, bf16[128,768]{1,0:T(8,128)(2,1)}, f32[128,256]{1,0:T(8,128)}) custom-call(bf16[32,16,768]{2,1,0:T(8,128)(2,1)} %copy-done, f32[8,768]{1,0:T(8,128)} %get-tuple-element.28.stat_ref, f32[1,768]{1,0:T(1,128)} %broadcast_in_dim.18.gain_ref, f32[1,768]{1,0:T(1,128)} %broadcast_in_dim.19.bias_ref, ...), custom_call_target="tpu_custom_call" | custom-call | tf_op jit(solution)/shard_map/beside_conv/pallas_call | solution.py:32
  78.6 7.4 %all-to-all-done.3.got_ref = f32[32,1,512]{2,1,0:T(1,128)S(1)} async-done(((f32[32,1,512]{2,1,0:T(1,128)}), f32[32,1,512]{2,1,0:T(1,128)S(1)}, u32[]{:S(2)}, u32[]{:S(2)}) %all-to-all-start.3) | async-done | bytes 65568 | tf_op jit(solution)/shard_map/all_to_all | solution.py:24
  86.0 0.0 copy-start.4
  86.0 0.6 copy-done.4
  86.6 1.9 %middle.1 = (bf16[128,256]{1,0:T(8,128)(2,1)}, f32[128,256]{1,0:T(8,128)}, f32[128,256]{1,0:T(8,128)}, f32[16,1,512]{2,1,0:T(1,128)}, f32[1,256]{1,0:T(1,128)}) custom-call(f32[32,1,512]{2,1,0:T(1,128)} %copy-done.4, f32[128,256]{1,0:T(8,128)} %get-tuple-element.27.conv_ref, f32[128,256]{1,0:T(8,128)} %get-tuple-element.29.dact_ref, f32[1,256]{1,0:T(1,128)} %bitcast.12, ...), custom_call_target="tpu_custom_call" | custom-call | tf_op jit(solution)/shard_map/middle/pallas_call | solution.py:32
  88.5 11.1 %all_to_all.46 = f32[16,1,512]{2,1,0:T(1,128)S(1)} all-to-all(f32[16,1,512]{2,1,0:T(1,128)} %get-tuple-element.30), channel_id=1, replica_groups=mesh['x'=4,'z_hi'=2,'z_lo'=4,'core'=2,'dp'=8] {'core','dp'}, dimensions={0} | all-to-all | bytes 65536 | tf_op jit(solution)/shard_map/all_to_all | solution.py:24
  99.7 13.7 %all_to_all.47.got_ref = f32[32,1,512]{2,1,0:T(1,128)} all-to-all(f32[32,1,512]{2,1,0:T(1,128)S(1)} %broadcast_in_dim.23), channel_id=1, replica_groups=mesh['x'=4,'z_hi'=2,'z_lo'=4,'core'=2,'dp'=8] {'x','z_hi','z_lo'}, dimensions={0} | all-to-all | bytes 131072 | tf_op jit(solution)/shard_map/all_to_all | solution.py:24
  113.3 3.0 %filter_parts.1 = (bf16[128,768]{1,0:T(8,128)(2,1)}, bf16[2,768,512]{2,1,0:T(8,128)(2,1)}) custom-call(f32[32,1,512]{2,1,0:T(1,128)} %all_to_all.47.got_ref, f32[128,256]{1,0:T(8,128)} %get-tuple-element.31.dpre_ref, f32[128,256]{1,0:T(8,128)} %get-tuple-element.32.normed_ref, f32[1,256]{1,0:T(1,128)} %get-tuple-element.33.spread_ref, f32[1,256]{1,0:T(1,128)} %bitcast.13, ...), custom_call_target="tpu_custom_call" | custom-call | tf_op jit(solution)/shard_map/filter_parts/pallas_call | solution.py:32
  116.4 3.7 %all-to-all-start.6 = ((bf16[2,768,512]{2,1,0:T(8,128)(2,1)}), bf16[2,768,512]{2,1,0:T(8,128)(2,1)S(1)}, u32[]{:S(2)}, u32[]{:S(2)}) async-start(bf16[2,768,512]{2,1,0:T(8,128)(2,1)} %get-tuple-element.37), calls=%async_computation.6 | async-start | bytes 3145728 | tf_op jit(solution)/shard_map/all_to_all | solution.py:24
  120.0 2.8 %back_rows.1 = (bf16[32,8,512]{2,1,0:T(8,128)(2,1)}, bf16[8,512]{1,0:T(8,128)(2,1)}) custom-call(bf16[128,768]{1,0:T(8,128)(2,1)} %get-tuple-element.38.stacked_ref, bf16[768,768]{1,0:T(8,128)(2,1)} %weight_ref.3, f32[128,768]{1,0:T(8,128)} %get-tuple-element.39.slope_ref, f32[128,768]{1,0:T(8,128)} %get-tuple-element.40.normed_ref, ...), custom_call_target="tpu_custom_call" | custom-call | tf_op jit(solution)/shard_map/back_rows/pallas_call | solution.py:32
  122.8 0.0 all-to-all-done.6.parts_ref
  122.9 0.0 copy-start.1
  122.9 1.2 copy-done.1
  124.0 2.8 %to_plane.1 = bf16[32,40,512]{2,1,0:T(8,128)(2,1)} custom-call(bf16[2,768,512]{2,1,0:T(8,128)(2,1)} %copy-done.1, bf16[32,8,512]{2,1,0:T(8,128)(2,1)} %get-tuple-element.41.rows_ref, bf16[8,512]{1,0:T(8,128)(2,1)} %get-tuple-element.42.sums_ref), custom_call_target="tpu_custom_call" | custom-call | tf_op jit(solution)/shard_map/to_plane/pallas_call | solution.py:32
  126.8 39.6 %all_to_all.48.got_ref = bf16[32,40,512]{2,1,0:T(8,128)(2,1)} all-to-all(bf16[32,40,512]{2,1,0:T(8,128)(2,1)} %to_plane.1), channel_id=1, replica_groups=mesh['x'=4,'z_hi'=2,'z_lo'=4,'core'=2,'dp'=8] {'x','z_hi','z_lo'}, dimensions={0} | all-to-all | bytes 2621440 | tf_op jit(solution)/shard_map/all_to_all | solution.py:24
  166.4 2.3 %to_line.1 = bf16[16,24,512]{2,1,0:T(8,128)(2,1)} custom-call(bf16[32,40,512]{2,1,0:T(8,128)(2,1)} %all_to_all.48.got_ref), custom_call_target="tpu_custom_call" | custom-call | tf_op jit(solution)/shard_map/to_line/pallas_call | solution.py:32
  168.7 4.6 %all-to-all-start.8 = ((bf16[16,24,512]{2,1,0:T(8,128)(2,1)}), bf16[16,24,512]{2,1,0:T(8,128)(2,1)S(1)}, u32[]{:S(2)}, u32[]{:S(2)}) async-start(bf16[16,24,512]{2,1,0:T(8,128)(2,1)} %to_line.1), calls=%async_computation.8 | async-start | bytes 786432 | tf_op jit(solution)/shard_map/all_to_all | solution.py:24
  173.2 2.5 %block_rows.1 = (bf16[128,768]{1,0:T(8,128)(2,1)}, f32[128,768]{1,0:T(8,128)}) custom-call(bf16[32,40,512]{2,1,0:T(8,128)(2,1)} %all_to_all.48.got_ref, bf16[128,768]{1,0:T(8,128)(2,1)} %bitcast.8, bf16[256,768]{1,0:T(8,128)(2,1)} %proj_ref.3), custom_call_target="tpu_custom_call" | custom-call | tf_op jit(solution)/shard_map/block_rows/pallas_call | solution.py:32
  175.7 11.2 %all-to-all-done.8.got_ref = bf16[16,24,512]{2,1,0:T(8,128)(2,1)S(1)} async-done(((bf16[16,24,512]{2,1,0:T(8,128)(2,1)}), bf16[16,24,512]{2,1,0:T(8,128)(2,1)S(1)}, u32[]{:S(2)}, u32[]{:S(2)}) %all-to-all-start.8) | async-done | bytes 393248 | tf_op jit(solution)/shard_map/all_to_all | solution.py:24
  186.9 0.0 copy-start.2
  186.9 0.8 copy-done.2
  187.6 2.1 %last_rows.1 = (bf16[128,768]{1,0:T(8,128)(2,1)}, f32[12,768]{1,0:T(8,128)}, f32[12,256]{1,0:T(8,128)}) custom-call(bf16[16,24,512]{2,1,0:T(8,128)(2,1)} %copy-done.2, f32[128,768]{1,0:T(8,128)} %get-tuple-element.44.dpre_ref, bf16[128,768]{1,0:T(8,128)(2,1)} %bitcast.9, bf16[128,768]{1,0:T(8,128)(2,1)} %bitcast.11, f32[8,768]{1,0:T(8,128)} %get-tuple-element.28.stat_ref, ...), custom_call_target="tpu_custom_call" | custom-call | tf_op jit(solution)/shard_map/last_rows/pallas_call | solution.py:32
  (3 shorter events, 0.1 us)
Async XLA Ops:
  2.3 16.7 %all-to-all-start = ((f32[16,1,1536]{2,1,0:T(1,128)}), f32[16,1,1536]{2,1,0:T(1,128)S(1)}, u32[]{:S(2)}, u32[]{:S(2)}) async-start(f32[16,1,1536]{2,1,0:T(1,128)} %first_sums.1), calls=%async_computation | async-start | bytes 196608 | tf_op jit(solution)/shard_map/all_to_all | solution.py:24
  13.2 20.0 %copy-start.5 = (f32[768]{0:T(1024)S(1)}, f32[768]{0:T(1024)}, u32[]{:S(2)}) copy-start(f32[768]{0:T(1024)} %param.12) | copy-start | bytes 9220
  13.2 20.6 %copy-start.6 = (f32[768]{0:T(1024)S(1)}, f32[768]{0:T(1024)}, u32[]{:S(2)}) copy-start(f32[768]{0:T(1024)} %param.13) | copy-start | bytes 9220
  19.0 0.6 copy-start.3
  21.6 34.7 %all-to-all-start.1 = ((bf16[32,16,768]{2,1,0:T(8,128)(2,1)}), bf16[32,16,768]{2,1,0:T(8,128)(2,1)S(1)}, u32[]{:S(2)}, u32[]{:S(2)}) async-start(bf16[32,16,768]{2,1,0:T(8,128)(2,1)} %spread_all.1), calls=%async_computation.1 | async-start | bytes 1572864 | tf_op jit(solution)/shard_map/all_to_all | solution.py:24
  56.4 0.9 copy-start
  71.2 14.8 %all-to-all-start.3 = ((f32[32,1,512]{2,1,0:T(1,128)}), f32[32,1,512]{2,1,0:T(1,128)S(1)}, u32[]{:S(2)}, u32[]{:S(2)}) async-start(f32[32,1,512]{2,1,0:T(1,128)} %broadcast_in_dim.20), calls=%async_computation.3 | async-start | bytes 131072 | tf_op jit(solution)/shard_map/all_to_all | solution.py:24
  86.0 0.6 copy-start.4
  116.4 6.5 %all-to-all-start.6 = ((bf16[2,768,512]{2,1,0:T(8,128)(2,1)}), bf16[2,768,512]{2,1,0:T(8,128)(2,1)S(1)}, u32[]{:S(2)}, u32[]{:S(2)}) async-start(bf16[2,768,512]{2,1,0:T(8,128)(2,1)} %get-tuple-element.37), calls=%async_computation.6 | async-start | bytes 3145728 | tf_op jit(solution)/shard_map/all_to_all | solution.py:24
  122.9 1.2 copy-start.1
  168.7 18.2 %all-to-all-start.8 = ((bf16[16,24,512]{2,1,0:T(8,128)(2,1)}), bf16[16,24,512]{2,1,0:T(8,128)(2,1)S(1)}, u32[]{:S(2)}, u32[]{:S(2)}) async-start(bf16[16,24,512]{2,1,0:T(8,128)(2,1)} %to_line.1), calls=%async_computation.8 | async-start | bytes 786432 | tf_op jit(solution)/shard_map/all_to_all | solution.py:24
  186.9 0.8 copy-start.2

commit v3 on v2

v3 whole, which is shorter than its diff:
```python
import math

import jax
import jax.numpy as jnp
from jax import lax
from jax.experimental import pallas as pl
from jax.experimental.pallas import tpu as pltpu
from jax.sharding import Mesh
from jax.sharding import PartitionSpec as P

SEQ = ("x", "z_hi", "z_lo", "core")
PLANE = ("x", "z_hi", "z_lo")
LINE = ("core", "dp")
BF16, F32 = jnp.bfloat16, jnp.float32
CH, MID = 768, 256
ROWS, SHIFT = 128, 16
PLANES, LINES, BATCH = 32, 16, 8
HALF = 512
COUNTED = 8.0 * 8192.0
COEFF = math.sqrt(2.0 / math.pi)


def exchange(pieces, axes):
    return lax.all_to_all(pieces, axes, split_axis=0, concat_axis=0, tiled=True)


def kernel(body, *outs, name):
    shapes = tuple(jax.ShapeDtypeStruct(shape, dtype) for shape, dtype in outs)
    whole = pl.BlockSpec(memory_space=pltpu.VMEM)

    def call(*args, near=()):
        near = tuple(pltpu.with_memory_space_constraint(a, pltpu.VMEM) for a in near)
        args = (*near, *args)
        return pl.pallas_call(
            body,
            out_shape=shapes,
            in_specs=[whole] * len(args),
            out_specs=(whole,) * len(shapes),
            name=name,
            compiler_params=pltpu.CompilerParams(vmem_limit_bytes=24 << 20),
        )(*args)

    return call


def matmul(a, b, dims):
    return lax.dot_general(a, b, (dims, ((), ())), preferred_element_type=F32)


def later(x):
    return jnp.concatenate([jnp.zeros_like(x[:SHIFT]), x[:-SHIFT]], axis=0)


def earlier(x):
    return jnp.concatenate([x[SHIFT:], jnp.zeros_like(x[:SHIFT])], axis=0)


def woven(value):
    width = value.shape[1] // 2
    tiles = value.astype(F32).reshape(ROWS // 8, 8, 2 * width)
    a, b = tiles[:, :, :width], tiles[:, :, width:]
    upper = lax.broadcasted_iota(jnp.int32, a.shape, 1) < 4
    even = jnp.where(upper, a, pltpu.roll(b, 4, axis=1))
    odd = jnp.where(upper, pltpu.roll(a, 4, axis=1), b)
    return jnp.stack([even, odd], axis=1).reshape(PLANES, 8, width).astype(BF16)


def unwoven(pieces):
    width = pieces.shape[2]
    pairs = pieces.astype(F32).reshape(ROWS // 8, 2, 8, width)
    even, odd = pairs[:, 0], pairs[:, 1]
    upper = lax.broadcasted_iota(jnp.int32, even.shape, 1) < 4
    a = jnp.where(upper, even, pltpu.roll(odd, 4, axis=1))
    b = jnp.where(upper, pltpu.roll(even, 4, axis=1), odd)
    return jnp.concatenate([a.reshape(ROWS, width), b.reshape(ROWS, width)], axis=1)


def rounded(value):
    return value.astype(BF16).astype(F32)


def tile_of(pieces, width):
    row = lax.broadcasted_iota(jnp.int32, (8, width), 0)
    tile = jnp.zeros((8, width), F32)
    for k, piece in enumerate(pieces):
        tile = jnp.where(row == k, piece, tile)
    return tile


def in_two(value, width):
    high = rounded(value)
    return [
        part[:, k : k + width] for part in (high, value - high) for k in range(0, value.shape[1], width)
    ]


def row_of(tile, rows):
    return jnp.concatenate([tile[k : k + 1] for k in rows], axis=1)


def sum_rows(value):
    return jnp.sum(value, axis=0, keepdims=True)


def copies(ref, index, row):
    ref[:, :, index] = jnp.broadcast_to(row, (ref.shape[0], 1, row.shape[1]))


def tanh_of(value):
    return jnp.tanh(COEFF * (value + 0.044715 * value * value * value))


def gelu_of(value, inner):
    return 0.5 * value * (1.0 + inner)


def slope_of(value, inner):
    return 0.5 * (1.0 + inner) + 0.5 * value * (1.0 - inner * inner) * COEFF * (
        1.0 + 3.0 * 0.044715 * value * value
    )


def first_sums(x_ref, out_ref):
    x = x_ref[...].astype(F32)
    mean = sum_rows(x) * (1.0 / ROWS)
    apart = x - mean
    copies(out_ref, slice(0, CH), mean)
    copies(out_ref, slice(CH, 2 * CH), sum_rows(apart * apart))


def spread_data(x_ref, cot_ref, proj_ref, out_ref):
    out_ref[:, :, : CH // 2] = woven(x_ref[...])
    out_ref[:, :, CH // 2 :] = woven(matmul(cot_ref[...], proj_ref[...], ((1,), (1,))))


def spread_all(sums_ref, data_ref, out_ref):
    sums = sums_ref[...]
    means = sums[:, :, :CH]
    mean = jnp.sum(means, axis=0) * (1.0 / LINES)
    apart = means - mean[None]
    squares = jnp.sum(sums[:, :, CH:] + float(ROWS) * (apart * apart), axis=0)
    tile = tile_of(in_two(mean, CH // 2) + in_two(squares, CH // 2), CH // 2).astype(BF16)
    out_ref[:, :, :HALF] = data_ref[...]
    out_ref[:, :, HALF:] = jnp.broadcast_to(tile[None], (PLANES, 8, CH // 2))


def forward_conv(got_ref, weight_ref, gain_ref, bias_ref, act_ref, conv_ref, sums_ref, stat_ref):
    parts = got_ref[:, :, HALF:].astype(F32)
    parts = parts + pltpu.roll(parts, 6, axis=1)
    total = jnp.sum(parts, axis=0)
    mean = total * (1.0 / PLANES)
    apart = parts - mean[None]
    between = jnp.sum(apart * apart, axis=0) * float(ROWS * LINES)
    center = row_of(mean, (0, 1))
    variance = (row_of(total, (4, 5)) + row_of(between, (0, 1))) * (1.0 / COUNTED)
    spread = jnp.sqrt(variance + 1e-05)
    stat_ref[0:1, :] = center
    stat_ref[1:2, :] = spread
    x = unwoven(got_ref[:, :, : CH // 2])
    pre = gain_ref[...] * ((x - center) / spread) + bias_ref[...]
    act = gelu_of(pre, tanh_of(pre)).astype(BF16)
    act_ref[...] = act
    terms = matmul(act, weight_ref[...], ((1,), (0,)))
    conv = later(terms[:, :MID]) + terms[:, MID : 2 * MID] + earlier(terms[:, 2 * MID :])
    conv_ref[...] = conv
    copies(sums_ref, slice(0, MID), sum_rows(conv))
    copies(sums_ref, slice(MID, 2 * MID), sum_rows(conv * conv))


def beside_conv(got_ref, stat_ref, gain_ref, bias_ref, normed_ref, slope_ref, dact_ref):
    normed = (unwoven(got_ref[:, :, : CH // 2]) - stat_ref[0:1, :]) / stat_ref[1:2, :]
    pre = gain_ref[...] * normed + bias_ref[...]
    normed_ref[...] = normed
    slope_ref[...] = slope_of(pre, tanh_of(pre))
    dact_ref[...] = unwoven(got_ref[:, :, CH // 2 : HALF])


def middle(got_ref, conv_ref, dact_ref, gain_ref, bias_ref, act_ref, normed_ref, dpre_ref, sums_ref, spread_ref):
    total = jnp.sum(got_ref[...], axis=0) * (1.0 / COUNTED)
    center = total[:, :MID]
    spread = jnp.sqrt(total[:, MID:] - center * center + 1e-05)
    spread_ref[...] = spread
    normed = (conv_ref[...] - center) / spread
    pre = gain_ref[...] * normed + bias_ref[...]
    inner = tanh_of(pre)
    dpre = dact_ref[...] * slope_of(pre, inner)
    copies(sums_ref, slice(0, MID), sum_rows(dpre))
    copies(sums_ref, slice(MID, 2 * MID), sum_rows(dpre * normed))
    normed_ref[...] = normed
    dpre_ref[...] = dpre
    act_ref[...] = woven(gelu_of(pre, inner))


def middle_plane(sums_ref, act_ref, out_ref):
    tile = tile_of(in_two(jnp.sum(sums_ref[...], axis=0), 128), 128).astype(BF16)
    out_ref[:, :, :128] = act_ref[...]
    out_ref[:, :, 128:] = jnp.broadcast_to(tile[None], (PLANES, 8, 128))


def filter_parts(
    got_ref, dpre_ref, normed_ref, spread_ref, gain_ref, act_in_ref, cot_ref, stacked_ref, parts_ref, act_ref
):
    tile = jnp.sum(got_ref[:, :, 128:].astype(F32), axis=0) * (1.0 / COUNTED)
    tile = tile + pltpu.roll(tile, 4, axis=0)
    first, second = row_of(tile, (0, 1)), row_of(tile, (2, 3))
    dconv = gain_ref[...] * (dpre_ref[...] - first - normed_ref[...] * second) / spread_ref[...]
    stacked = jnp.concatenate([earlier(dconv), dconv, later(dconv)], axis=1).astype(BF16)
    stacked_ref[...] = stacked
    conv_part = matmul(act_in_ref[...], stacked, ((0,), (0,)))
    parts_ref[0] = conv_part[:, :HALF].astype(BF16)
    parts_ref[1, :, : HALF - MID] = conv_part[:, HALF:].astype(BF16)
    act = unwoven(got_ref[:, :, :128]).astype(BF16)
    act_ref[...] = act
    proj_part = matmul(cot_ref[...], act, ((0,), (0,)))
    parts_ref[1, :, HALF - MID :] = proj_part.astype(BF16)


def back_rows(weight_ref, stacked_ref, slope_ref, normed_ref, out_ref):
    dpre = matmul(stacked_ref[...], weight_ref[...], ((1,), (1,))) * slope_ref[...]
    sums = jnp.concatenate([sum_rows(dpre), sum_rows(dpre * normed_ref[...])], axis=1)
    rows = [sums[:, k : k + 128] for k in range(0, 2 * CH, 128)]
    out_ref[:, :, : CH // 2] = woven(dpre)
    for k in range(2):
        tile = tile_of(rows[6 * k : 6 * k + 6], 128).astype(BF16)
        lanes = slice(CH // 2 + 128 * k, CH // 2 + 128 * (k + 1))
        out_ref[:, :, lanes] = jnp.broadcast_to(tile[None], (PLANES, 8, 128))


def to_plane(parts_ref, back_ref, out_ref):
    both = (parts_ref[0].astype(F32) + parts_ref[1].astype(F32)).astype(BF16)
    both = both.reshape(PLANES, 3, 8, HALF)
    for k in range(3):
        out_ref[:, :, HALF * k : HALF * (k + 1)] = both[:, k]
    out_ref[:, :, 3 * HALF :] = back_ref[...]


def to_line(got_ref, out_ref):
    tiles = [
        jnp.sum(got_ref[:, :, HALF * k : HALF * (k + 1)].astype(F32), axis=0) for k in range(3)
    ]
    sums = jnp.sum(got_ref[:, :, 3 * HALF + CH // 2 :].astype(F32), axis=0)
    sums = [row_of(sums[:, 128 * k : 128 * (k + 1)], range(6)) for k in range(2)]
    sums = jnp.concatenate(sums, axis=1)
    low = pltpu.roll(tile_of([sums[:, k : k + HALF] for k in range(0, 2 * CH, HALF)], HALF), 4, axis=0)
    upper = lax.broadcasted_iota(jnp.int32, (8, HALF), 0) < 4
    turned = [pltpu.roll(tile, 4, axis=0) for tile in tiles]
    own = (
        (tiles[0], jnp.where(upper, tiles[1], low)),
        (jnp.where(upper, turned[1], turned[2]), jnp.where(upper, turned[2], low)),
    )
    for core in range(2):
        for k in range(2):
            out_ref[core * BATCH : (core + 1) * BATCH, :, HALF * k : HALF * (k + 1)] = (
                jnp.broadcast_to(own[core][k].astype(BF16)[None], (BATCH, 8, HALF))
            )


def block_rows(act_ref, x_ref, proj_ref, out_ref):
    update = matmul(act_ref[...], proj_ref[...], ((1,), (0,)))
    out_ref[...] = (x_ref[...].astype(F32) + update).astype(BF16)


def beside_line(got_ref, x_ref, cot_ref, stat_ref, gain_ref, base_ref, normed_ref):
    dpre = unwoven(got_ref[:, :, 3 * HALF : 3 * HALF + CH // 2])
    spread = stat_ref[1:2, :]
    normed_ref[...] = (x_ref[...].astype(F32) - stat_ref[0:1, :]) / spread
    base_ref[...] = cot_ref[...].astype(F32) + dpre * (gain_ref[...] / spread)


def last_rows(got_ref, base_ref, normed_ref, stat_ref, gain_ref, grad_ref, conv_ref, proj_ref):
    left, right = (
        jnp.sum(got_ref[BATCH * k : BATCH * (k + 1)].astype(F32), axis=0) for k in range(2)
    )
    tile = left[4:8, HALF:] + right[4:8, HALF:]
    total = row_of(tile, range(3)) * (1.0 / COUNTED)
    scale = gain_ref[...] / stat_ref[1:2, :]
    grad = base_ref[...] - scale * total[:, :CH] - normed_ref[...] * (scale * total[:, CH:])
    grad_ref[...] = grad.astype(BF16)
    for rows, lanes, count in ((slice(0, 8), 0, 8), (slice(8, 12), HALF, 4)):
        conv_ref[rows, :HALF] = left[:count, lanes : lanes + HALF]
        conv_ref[rows, HALF:] = right[:count, lanes : lanes + CH - HALF]
        proj_ref[rows, :] = right[:count, lanes + CH - HALF : lanes + HALF]


def per_device(inputs, cotangent, conv_weight, proj_weight, gain_in, bias_in, gain_mid, bias_mid):
    x = inputs.reshape(ROWS, CH)
    cot = cotangent.reshape(ROWS, CH)
    gain_in, bias_in, gain_mid, bias_mid = (v[None] for v in (gain_in, bias_in, gain_mid, bias_mid))
    rows, rows_mid = (ROWS, CH), (ROWS, MID)

    (sums,) = kernel(first_sums, ((LINES, 1, 2 * CH), F32), name="first_sums")(x)
    (data,) = kernel(spread_data, ((PLANES, 8, HALF), BF16), name="spread_data")(x, cot, proj_weight)
    sums = exchange(sums, LINE)
    (both,) = kernel(spread_all, ((PLANES, 8, HALF + CH // 2), BF16), name="spread_all")(
        near=(sums, data)
    )
    both = exchange(both, PLANE)

    act_in, conv, sums, stat_in = kernel(
        forward_conv,
        (rows, BF16),
        (rows_mid, F32),
        ((LINES, 1, 2 * MID), F32),
        ((8, CH), F32),
        name="forward_conv",
    )(near=(both, conv_weight, gain_in, bias_in))
    normed_in, slope_in, dact_mid = kernel(
        beside_conv, (rows, F32), (rows, F32), (rows_mid, F32), name="beside_conv"
    )(stat_in, gain_in, bias_in, near=(both,))
    sums = exchange(sums, LINE).sum(axis=0)
    sums = exchange(jnp.broadcast_to(sums, (PLANES, 1, 2 * MID)), PLANE)

    act_mid, normed_mid, dpre_mid, sums, spread_mid = kernel(
        middle,
        ((PLANES, 8, 128), BF16),
        (rows_mid, F32),
        (rows_mid, F32),
        ((LINES, 1, 2 * MID), F32),
        ((1, MID), F32),
        name="middle",
    )(conv, dact_mid, gain_mid, bias_mid, near=(sums,))
    sums = exchange(sums, LINE)
    (both,) = kernel(middle_plane, ((PLANES, 8, 256), BF16), name="middle_plane")(
        act_mid, near=(sums,)
    )
    both = exchange(both, PLANE)

    stacked, parts, act_mid = kernel(
        filter_parts, (rows, BF16), ((2, CH, HALF), BF16), (rows_mid, BF16), name="filter_parts"
    )(dpre_mid, normed_mid, spread_mid, gain_mid, act_in, cot, near=(both,))
    parts = exchange(parts, "core")
    (back,) = kernel(back_rows, ((PLANES, 8, CH // 2 + 256), BF16), name="back_rows")(
        stacked, slope_in, normed_in, near=(conv_weight,)
    )
    (plane,) = kernel(to_plane, ((PLANES, 8, 3 * HALF + CH // 2 + 256), BF16), name="to_plane")(
        back, near=(parts,)
    )
    plane = exchange(plane, PLANE)
    (line,) = kernel(to_line, ((LINES, 8, 2 * HALF), BF16), name="to_line")(near=(plane,))
    line = exchange(line, LINE)
    (block_out,) = kernel(block_rows, (rows, BF16), name="block_rows")(act_mid, x, proj_weight)
    base, normed = kernel(beside_line, (rows, F32), (rows, F32), name="beside_line")(
        x, cot, stat_in, gain_in, near=(plane,)
    )
    input_grad, conv_grad, proj_grad = kernel(
        last_rows, (rows, BF16), ((12, CH), F32), ((12, MID), F32), name="last_rows"
    )(stat_in, gain_in, near=(line, base, normed))
    return (
        block_out.reshape(inputs.shape),
        input_grad.reshape(inputs.shape),
        conv_grad,
        proj_grad,
    )


def solution(mesh):
    split = Mesh(mesh.devices.reshape(4, 2, 4, 2, 8), ("x", "z_hi", "z_lo", "core", "dp"))
    rows = P("dp", SEQ, None)
    return jax.shard_map(
        per_device,
        mesh=split,
        in_specs=(rows, rows, P(), P(), P(), P(), P(), P()),
        out_specs=(rows, rows, P(SEQ, None), P(SEQ, None)),
        check_vma=False,
    )
```

time: 191 us -> 161 us (0.84)
  Pallas kernels: 28.3 us -> 7.25 us
  waiting for transfers between devices: 46.2 us -> 37.9 us
  blocking collectives: 74.8 us -> 69.6 us
  local copies, waits for them, and re-layouts: 5.97 us -> 9.78 us
    pallas_call x12 -> x14, Pallas kernels: 28.3 us -> 7.25 us  [call(): pl.pallas_call(body, out_shape=shapes, in_specs=[whole] * len(args), out_...]
    all_to_all x5, waiting for transfers between devices: 46.2 us -> 37.9 us  [exchange(): return lax.all_to_all(pieces, axes, split_axis=0, concat_axis=0, tiled=True)]
    all_to_all x4, blocking collectives: 74.8 us -> 69.6 us  [exchange(): return lax.all_to_all(pieces, axes, split_axis=0, concat_axis=0, tiled=True)]
    unnamed x14 -> x38, local copies, waits for them, and re-layouts: 4.09 us -> 9.11 us
  transfers between devices with their start and end apart: 5 -> 5, of which waited for: 4 -> 4; matrix products, arithmetic and copies ran while one was open for 1% -> 0% of each run, Pallas kernels for 5% -> 1%
where the time goes in v3:
time: 161 us; the launch traced here: 160 us
  blocking collectives  69.6 us (43%)
  waiting for transfers between devices  37.9 us (24%)
  starting transfers between devices  34.5 us (21%)
  local copies, waits for them, and re-layouts  9.78 us (6%)
  Pallas kernels  7.25 us (5%)
    all_to_all x4, blocking collectives, exchange(): return lax.all_to_all(pieces, axes, split_axis=0, concat_axis=0, tiled=True)  69.6 us
    all_to_all x5, waiting for transfers between devices, exchange(): return lax.all_to_all(pieces, axes, split_axis=0, concat_axis=0, tiled=True)  37.9 us
    all_to_all x5, starting transfers between devices, exchange(): return lax.all_to_all(pieces, axes, split_axis=0, concat_axis=0, tiled=True)  34.5 us
    unnamed x38, local copies, waits for them, and re-layouts  9.11 us
    pallas_call x14, Pallas kernels, call(): pl.pallas_call(body, out_shape=shapes, in_specs=[whole] * len(args), out_...  7.25 us
  transfers between devices with their start and end apart: 5, of which 4 were waited for; matrix products, arithmetic and copies ran while one was open for 0% of the time, Pallas kernels for 1%

profile of v3, /device:TPU:8, one launch (start us, length us, event | category | flops | bytes accessed | tf_op | source)
XLA Modules:
  0.0 159.9 jit_solution(10599561024663651501)
XLA Ops:
  0.6 0.0 copy-start.1
  0.6 0.9 copy-done.1
  1.6 0.8 first_sums.1
  2.3 9.1 %all-to-all-start = ((f32[16,1,1536]{2,1,0:T(1,128)}), f32[16,1,1536]{2,1,0:T(1,128)S(1)}, u32[]{:S(2)}, u32[]{:S(2)}) async-start(f32[16,1,1536]{2,1,0:T(1,128)} %first_sums.1), calls=%async_computation | async-start | bytes 196608 | tf_op jit(solution)/shard_map/all_to_all | solution.py:24
  11.4 0.9 copy-done.2
  12.3 0.9 copy-done.4
  13.3 1.0 copy-done.7
  14.3 0.3 spread_data.1.data_ref
  14.6 4.5 %all-to-all-done.sums_ref = f32[16,1,1536]{2,1,0:T(1,128)S(1)} async-done(((f32[16,1,1536]{2,1,0:T(1,128)}), f32[16,1,1536]{2,1,0:T(1,128)S(1)}, u32[]{:S(2)}, u32[]{:S(2)}) %all-to-all-start) | async-done | bytes 98336 | tf_op jit(solution)/shard_map/all_to_all | solution.py:24
  19.0 0.9 spread_all.1
  19.9 11.6 %all-to-all-start.1 = ((bf16[32,8,896]{2,1,0:T(8,128)(2,1)}), bf16[32,8,896]{2,1,0:T(8,128)(2,1)S(1)}, u32[]{:S(2)}, u32[]{:S(2)}) async-start(bf16[32,8,896]{2,1,0:T(8,128)(2,1)} %spread_all.1), calls=%async_computation.1 | async-start | bytes 917504 | tf_op jit(solution)/shard_map/all_to_all | solution.py:24
  31.5 0.0 copy-done.17
  31.5 0.0 copy-done.18
  31.6 0.0 copy-start.15
  31.6 0.0 copy-start.16
  31.6 15.3 %all-to-all-done.1.got_ref = bf16[32,8,896]{2,1,0:T(8,128)(2,1)S(1)} async-done(((bf16[32,8,896]{2,1,0:T(8,128)(2,1)}), bf16[32,8,896]{2,1,0:T(8,128)(2,1)S(1)}, u32[]{:S(2)}, u32[]{:S(2)}) %all-to-all-start.1) | async-done | bytes 458784 | tf_op jit(solution)/shard_map/all_to_all | solution.py:24
  46.9 0.0 copy-done
  46.9 0.7 forward_conv.1
  47.6 0.0 copy-start.5
  47.6 9.9 %all_to_all.45 = f32[16,1,512]{2,1,0:T(1,128)S(1)} all-to-all(f32[16,1,512]{2,1,0:T(1,128)S(1)} %get-tuple-element.24), channel_id=1, replica_groups=mesh['x'=4,'z_hi'=2,'z_lo'=4,'core'=2,'dp'=8] {'core','dp'}, dimensions={0} | all-to-all | bytes 65536 | tf_op jit(solution)/shard_map/all_to_all | solution.py:24
  57.5 0.7 broadcast_in_dim.17
  58.2 5.8 %all-to-all-start.3 = ((f32[32,1,512]{2,1,0:T(1,128)}), f32[32,1,512]{2,1,0:T(1,128)S(1)}, u32[]{:S(2)}, u32[]{:S(2)}) async-start(f32[32,1,512]{2,1,0:T(1,128)} %broadcast_in_dim.17), calls=%async_computation.3 | async-start | bytes 131072 | tf_op jit(solution)/shard_map/all_to_all | solution.py:24
  64.0 0.3 beside_conv.1
  64.4 0.0 copy-start.9
  64.4 0.7 copy-done.9
  65.1 0.8 copy-done.11
  65.9 8.2 %all-to-all-done.3.got_ref = f32[32,1,512]{2,1,0:T(1,128)S(1)} async-done(((f32[32,1,512]{2,1,0:T(1,128)}), f32[32,1,512]{2,1,0:T(1,128)S(1)}, u32[]{:S(2)}, u32[]{:S(2)}) %all-to-all-start.3) | async-done | bytes 65568 | tf_op jit(solution)/shard_map/all_to_all | solution.py:24
  74.0 0.2 middle.1
  74.3 10.2 %all_to_all.46.sums_ref = f32[16,1,512]{2,1,0:T(1,128)S(1)} all-to-all(f32[16,1,512]{2,1,0:T(1,128)S(1)} %get-tuple-element.28), channel_id=1, replica_groups=mesh['x'=4,'z_hi'=2,'z_lo'=4,'core'=2,'dp'=8] {'core','dp'}, dimensions={0} | all-to-all | bytes 65536 | tf_op jit(solution)/shard_map/all_to_all | solution.py:24
  84.5 0.1 middle_plane.1
  84.5 13.7 %all_to_all.47.got_ref = bf16[32,8,256]{2,1,0:T(8,128)(2,1)S(1)} all-to-all(bf16[32,8,256]{2,1,0:T(8,128)(2,1)S(1)} %middle_plane.1), channel_id=1, replica_groups=mesh['x'=4,'z_hi'=2,'z_lo'=4,'core'=2,'dp'=8] {'x','z_hi','z_lo'}, dimensions={0} | all-to-all | bytes 262144 | tf_op jit(solution)/shard_map/all_to_all | solution.py:24
  98.2 0.6 filter_parts.1
  98.8 0.0 copy-start.6
  98.8 1.2 copy-done.6
  100.0 0.6 copy-done.13
  100.6 3.7 %all-to-all-start.6 = ((bf16[2,768,512]{2,1,0:T(8,128)(2,1)}), bf16[2,768,512]{2,1,0:T(8,128)(2,1)S(1)}, u32[]{:S(2)}, u32[]{:S(2)}) async-start(bf16[2,768,512]{2,1,0:T(8,128)(2,1)} %copy-done.6), calls=%async_computation.6 | async-start | bytes 3145728 | tf_op jit(solution)/shard_map/all_to_all | solution.py:24
  104.3 1.0 copy-done.10
  105.3 1.0 copy-done.12
  106.3 0.6 back_rows.1.back_ref
  106.9 0.0 all-to-all-done.6.parts_ref
  106.9 0.2 to_plane.1
  107.1 35.8 %all_to_all.48.got_ref = bf16[32,8,2176]{2,1,0:T(8,128)(2,1)S(1)} all-to-all(bf16[32,8,2176]{2,1,0:T(8,128)(2,1)S(1)} %to_plane.1), channel_id=1, replica_groups=mesh['x'=4,'z_hi'=2,'z_lo'=4,'core'=2,'dp'=8] {'x','z_hi','z_lo'}, dimensions={0} | all-to-all | bytes 2228224 | tf_op jit(solution)/shard_map/all_to_all | solution.py:24
  142.9 0.8 to_line.1
  143.7 4.4 %all-to-all-start.8 = ((bf16[16,8,1024]{2,1,0:T(8,128)(2,1)}), bf16[16,8,1024]{2,1,0:T(8,128)(2,1)S(1)}, u32[]{:S(2)}, u32[]{:S(2)}) async-start(bf16[16,8,1024]{2,1,0:T(8,128)(2,1)} %to_line.1), calls=%async_computation.8 | async-start | bytes 524288 | tf_op jit(solution)/shard_map/all_to_all | solution.py:24
  148.1 0.9 block_rows.1
  149.0 0.1 beside_line.1
  149.2 9.9 %all-to-all-done.8.got_ref = bf16[16,8,1024]{2,1,0:T(8,128)(2,1)S(1)} async-done(((bf16[16,8,1024]{2,1,0:T(8,128)(2,1)}), bf16[16,8,1024]{2,1,0:T(8,128)(2,1)S(1)}, u32[]{:S(2)}, u32[]{:S(2)}) %all-to-all-start.8) | async-done | bytes 262176 | tf_op jit(solution)/shard_map/all_to_all | solution.py:24
  159.1 0.8 last_rows.1
  (22 shorter events, 0.1 us)
Async XLA Ops:
  0.6 0.9 copy-start.1
  2.3 16.7 %all-to-all-start = ((f32[16,1,1536]{2,1,0:T(1,128)}), f32[16,1,1536]{2,1,0:T(1,128)S(1)}, u32[]{:S(2)}, u32[]{:S(2)}) async-start(f32[16,1,1536]{2,1,0:T(1,128)} %first_sums.1), calls=%async_computation | async-start | bytes 196608 | tf_op jit(solution)/shard_map/all_to_all | solution.py:24
  11.4 0.9 copy-start.2
  12.3 0.9 copy-start.4
  13.3 1.0 copy-start.7
  14.3 17.3 %copy-start.17 = (f32[768]{0:T(1024)S(1)}, f32[768]{0:T(1024)}, u32[]{:S(2)}) copy-start(f32[768]{0:T(1024)} %param.12) | copy-start | bytes 9220
  14.3 17.3 %copy-start.18 = (f32[768]{0:T(1024)S(1)}, f32[768]{0:T(1024)}, u32[]{:S(2)}) copy-start(f32[768]{0:T(1024)} %param.13) | copy-start | bytes 9220
  14.3 32.7 %copy-start = (bf16[768,768]{1,0:T(8,128)(2,1)S(1)}, bf16[768,768]{1,0:T(8,128)(2,1)}, u32[]{:S(2)}) copy-start(bf16[768,768]{1,0:T(8,128)(2,1)} %weight_ref.3) | copy-start | bytes 3538948
  19.9 27.0 %all-to-all-start.1 = ((bf16[32,8,896]{2,1,0:T(8,128)(2,1)}), bf16[32,8,896]{2,1,0:T(8,128)(2,1)S(1)}, u32[]{:S(2)}, u32[]{:S(2)}) async-start(bf16[32,8,896]{2,1,0:T(8,128)(2,1)} %spread_all.1), calls=%async_computation.1 | async-start | bytes 917504 | tf_op jit(solution)/shard_map/all_to_all | solution.py:24
  31.6 42.5 %copy-start.15 = (f32[256]{0:T(256)S(1)}, f32[256]{0:T(256)}, u32[]{:S(2)}) copy-start(f32[256]{0:T(256)} %param.14) | copy-start | bytes 3076
  31.6 42.5 %copy-start.16 = (f32[256]{0:T(256)S(1)}, f32[256]{0:T(256)}, u32[]{:S(2)}) copy-start(f32[256]{0:T(256)} %param.15) | copy-start | bytes 3076
  47.6 50.6 %copy-start.5 = (bf16[1,128,768]{2,1,0:T(8,128)(2,1)S(1)}, bf16[1,128,768]{2,1,0:T(8,128)(2,1)}, u32[]{:S(2)}) copy-start(bf16[1,128,768]{2,1,0:T(8,128)(2,1)} %param.9) | copy-start | bytes 589828
  58.2 15.8 %all-to-all-start.3 = ((f32[32,1,512]{2,1,0:T(1,128)}), f32[32,1,512]{2,1,0:T(1,128)S(1)}, u32[]{:S(2)}, u32[]{:S(2)}) async-start(f32[32,1,512]{2,1,0:T(1,128)} %broadcast_in_dim.17), calls=%async_computation.3 | async-start | bytes 131072 | tf_op jit(solution)/shard_map/all_to_all | solution.py:24
  64.4 0.8 copy-start.9
  65.1 0.8 copy-start.11
  98.8 1.2 copy-start.6
  100.0 0.6 copy-start.13
  100.6 6.3 %all-to-all-start.6 = ((bf16[2,768,512]{2,1,0:T(8,128)(2,1)}), bf16[2,768,512]{2,1,0:T(8,128)(2,1)S(1)}, u32[]{:S(2)}, u32[]{:S(2)}) async-start(bf16[2,768,512]{2,1,0:T(8,128)(2,1)} %copy-done.6), calls=%async_computation.6 | async-start | bytes 3145728 | tf_op jit(solution)/shard_map/all_to_all | solution.py:24
  104.3 1.0 copy-start.10
  105.3 1.0 copy-start.12
  142.9 5.2 %copy-start.3 = (bf16[1,128,768]{2,1,0:T(8,128)(2,1)S(1)}, bf16[1,128,768]{2,1,0:T(8,128)(2,1)}, u32[]{:S(2)}) copy-start(bf16[1,128,768]{2,1,0:T(8,128)(2,1)} %param.8) | copy-start | bytes 589828
  142.9 5.2 %copy-start.8 = (bf16[256,768]{1,0:T(8,128)(2,1)S(1)}, bf16[256,768]{1,0:T(8,128)(2,1)}, u32[]{:S(2)}) copy-start(bf16[256,768]{1,0:T(8,128)(2,1)} %proj_ref.3) | copy-start | bytes 1179652
  142.9 5.2 %copy-start.14 = (bf16[128,256]{1,0:T(8,128)(2,1)S(1)}, bf16[128,256]{1,0:T(8,128)(2,1)}, u32[]{:S(2)}) copy-start(bf16[128,256]{1,0:T(8,128)(2,1)} %copy-done.13) | copy-start | bytes 196612
  143.7 15.4 %all-to-all-start.8 = ((bf16[16,8,1024]{2,1,0:T(8,128)(2,1)}), bf16[16,8,1024]{2,1,0:T(8,128)(2,1)S(1)}, u32[]{:S(2)}, u32[]{:S(2)}) async-start(bf16[16,8,1024]{2,1,0:T(8,128)(2,1)} %to_line.1), calls=%async_computation.8 | async-start | bytes 524288 | tf_op jit(solution)/shard_map/all_to_all | solution.py:24

commit v4 on v3

--- a/solution.py
+++ b/solution.py
@@ -102,6 +102,10 @@
     return jnp.sum(value, axis=0, keepdims=True)
 
 
+def flat(ref):
+    return ref[...].reshape(1, ref.shape[0])
+
+
 def copies(ref, index, row):
     ref[:, :, index] = jnp.broadcast_to(row, (ref.shape[0], 1, row.shape[1]))
 
@@ -120,17 +124,21 @@
     )
 
 
-def first_sums(x_ref, out_ref):
+def opening(x_hbm, cot_hbm, proj_hbm, sums_ref, data_ref, x_ref, cot_ref, proj_ref, sems):
+    pairs = ((x_hbm, x_ref), (cot_hbm, cot_ref), (proj_hbm, proj_ref))
+    loads = [pltpu.make_async_copy(*pair, sems.at[k]) for k, pair in enumerate(pairs)]
+    for load in loads:
+        load.start()
+    loads[0].wait()
     x = x_ref[...].astype(F32)
     mean = sum_rows(x) * (1.0 / ROWS)
     apart = x - mean
-    copies(out_ref, slice(0, CH), mean)
-    copies(out_ref, slice(CH, 2 * CH), sum_rows(apart * apart))
-
-
-def spread_data(x_ref, cot_ref, proj_ref, out_ref):
-    out_ref[:, :, : CH // 2] = woven(x_ref[...])
-    out_ref[:, :, CH // 2 :] = woven(matmul(cot_ref[...], proj_ref[...], ((1,), (1,))))
+    copies(sums_ref, slice(0, CH), mean)
+    copies(sums_ref, slice(CH, 2 * CH), sum_rows(apart * apart))
+    data_ref[:, :, : CH // 2] = woven(x)
+    loads[1].wait()
+    loads[2].wait()
+    data_ref[:, :, CH // 2 :] = woven(matmul(cot_ref[...], proj_ref[...], ((1,), (1,))))
 
 
 def spread_all(sums_ref, data_ref, out_ref):
@@ -144,7 +152,7 @@
     out_ref[:, :, HALF:] = jnp.broadcast_to(tile[None], (PLANES, 8, CH // 2))
 
 
-def forward_conv(got_ref, weight_ref, gain_ref, bias_ref, act_ref, conv_ref, sums_ref, stat_ref):
+def forward_conv(got_ref, weight_ref, gain_ref, bias_ref, act_ref, x_ref, conv_ref, dact_ref, sums_ref, stat_ref):
     parts = got_ref[:, :, HALF:].astype(F32)
     parts = parts + pltpu.roll(parts, 6, axis=1)
     total = jnp.sum(parts, axis=0)
@@ -157,7 +165,8 @@
     stat_ref[0:1, :] = center
     stat_ref[1:2, :] = spread
     x = unwoven(got_ref[:, :, : CH // 2])
-    pre = gain_ref[...] * ((x - center) / spread) + bias_ref[...]
+    x_ref[...] = x.astype(BF16)
+    pre = flat(gain_ref) * ((x - center) / spread) + flat(bias_ref)
     act = gelu_of(pre, tanh_of(pre)).astype(BF16)
     act_ref[...] = act
     terms = matmul(act, weight_ref[...], ((1,), (0,)))
@@ -165,23 +174,16 @@
     conv_ref[...] = conv
     copies(sums_ref, slice(0, MID), sum_rows(conv))
     copies(sums_ref, slice(MID, 2 * MID), sum_rows(conv * conv))
-
-
-def beside_conv(got_ref, stat_ref, gain_ref, bias_ref, normed_ref, slope_ref, dact_ref):
-    normed = (unwoven(got_ref[:, :, : CH // 2]) - stat_ref[0:1, :]) / stat_ref[1:2, :]
-    pre = gain_ref[...] * normed + bias_ref[...]
-    normed_ref[...] = normed
-    slope_ref[...] = slope_of(pre, tanh_of(pre))
     dact_ref[...] = unwoven(got_ref[:, :, CH // 2 : HALF])
 
 
-def middle(got_ref, conv_ref, dact_ref, gain_ref, bias_ref, act_ref, normed_ref, dpre_ref, sums_ref, spread_ref):
+def middle(got_ref, gain_ref, bias_ref, conv_ref, dact_ref, act_ref, normed_ref, dpre_ref, sums_ref, spread_ref):
     total = jnp.sum(got_ref[...], axis=0) * (1.0 / COUNTED)
     center = total[:, :MID]
     spread = jnp.sqrt(total[:, MID:] - center * center + 1e-05)
-    spread_ref[...] = spread
+    spread_ref[0:1, :] = spread
     normed = (conv_ref[...] - center) / spread
-    pre = gain_ref[...] * normed + bias_ref[...]
+    pre = flat(gain_ref) * normed + flat(bias_ref)
     inner = tanh_of(pre)
     dpre = dact_ref[...] * slope_of(pre, inner)
     copies(sums_ref, slice(0, MID), sum_rows(dpre))
@@ -198,12 +200,13 @@
 
 
 def filter_parts(
-    got_ref, dpre_ref, normed_ref, spread_ref, gain_ref, act_in_ref, cot_ref, stacked_ref, parts_ref, act_ref
+    got_ref, gain_ref, cot_ref, dpre_ref, normed_ref, spread_ref, act_in_ref, stacked_ref, parts_ref, act_ref
 ):
     tile = jnp.sum(got_ref[:, :, 128:].astype(F32), axis=0) * (1.0 / COUNTED)
     tile = tile + pltpu.roll(tile, 4, axis=0)
     first, second = row_of(tile, (0, 1)), row_of(tile, (2, 3))
-    dconv = gain_ref[...] * (dpre_ref[...] - first - normed_ref[...] * second) / spread_ref[...]
+    dconv = dpre_ref[...] - first - normed_ref[...] * second
+    dconv = flat(gain_ref) * dconv / spread_ref[0:1, :]
     stacked = jnp.concatenate([earlier(dconv), dconv, later(dconv)], axis=1).astype(BF16)
     stacked_ref[...] = stacked
     conv_part = matmul(act_in_ref[...], stacked, ((0,), (0,)))
@@ -215,23 +218,23 @@
     parts_ref[1, :, HALF - MID :] = proj_part.astype(BF16)
 
 
-def back_rows(weight_ref, stacked_ref, slope_ref, normed_ref, out_ref):
-    dpre = matmul(stacked_ref[...], weight_ref[...], ((1,), (1,))) * slope_ref[...]
-    sums = jnp.concatenate([sum_rows(dpre), sum_rows(dpre * normed_ref[...])], axis=1)
+def to_plane(parts_ref, weight_ref, gain_ref, bias_ref, stacked_ref, x_ref, stat_ref, out_ref):
+    normed = (x_ref[...].astype(F32) - stat_ref[0:1, :]) / stat_ref[1:2, :]
+    pre = flat(gain_ref) * normed + flat(bias_ref)
+    dpre = matmul(stacked_ref[...], weight_ref[...], ((1,), (1,))) * slope_of(pre, tanh_of(pre))
+    sums = jnp.concatenate([sum_rows(dpre), sum_rows(dpre * normed)], axis=1)
     rows = [sums[:, k : k + 128] for k in range(0, 2 * CH, 128)]
-    out_ref[:, :, : CH // 2] = woven(dpre)
-    for k in range(2):
-        tile = tile_of(rows[6 * k : 6 * k + 6], 128).astype(BF16)
-        lanes = slice(CH // 2 + 128 * k, CH // 2 + 128 * (k + 1))
-        out_ref[:, :, lanes] = jnp.broadcast_to(tile[None], (PLANES, 8, 128))
-
-
-def to_plane(parts_ref, back_ref, out_ref):
     both = (parts_ref[0].astype(F32) + parts_ref[1].astype(F32)).astype(BF16)
     both = both.reshape(PLANES, 3, 8, HALF)
     for k in range(3):
         out_ref[:, :, HALF * k : HALF * (k + 1)] = both[:, k]
-    out_ref[:, :, 3 * HALF :] = back_ref[...]
+    begin = 3 * HALF + CH // 2
+    out_ref[:, :, 3 * HALF : begin] = woven(dpre)
+    for k in range(2):
+        tile = tile_of(rows[6 * k : 6 * k + 6], 128).astype(BF16)
+        out_ref[:, :, begin + 128 * k : begin + 128 * (k + 1)] = jnp.broadcast_to(
+            tile[None], (PLANES, 8, 128)
+        )
 
 
 def to_line(got_ref, out_ref):
@@ -255,58 +258,66 @@
             )
 
 
-def block_rows(act_ref, x_ref, proj_ref, out_ref):
+def last_rows(
+    got_ref, plane_ref, x_ref, cot_ref, proj_ref, gain_ref, act_ref, stat_ref, out_ref, grad_ref, conv_ref, proj_grad_ref
+):
+    x = x_ref[...].astype(F32)
     update = matmul(act_ref[...], proj_ref[...], ((1,), (0,)))
-    out_ref[...] = (x_ref[...].astype(F32) + update).astype(BF16)
-
-
-def beside_line(got_ref, x_ref, cot_ref, stat_ref, gain_ref, base_ref, normed_ref):
-    dpre = unwoven(got_ref[:, :, 3 * HALF : 3 * HALF + CH // 2])
-    spread = stat_ref[1:2, :]
-    normed_ref[...] = (x_ref[...].astype(F32) - stat_ref[0:1, :]) / spread
-    base_ref[...] = cot_ref[...].astype(F32) + dpre * (gain_ref[...] / spread)
-
-
-def last_rows(got_ref, base_ref, normed_ref, stat_ref, gain_ref, grad_ref, conv_ref, proj_ref):
+    out_ref[...] = (x + update).astype(BF16)
     left, right = (
         jnp.sum(got_ref[BATCH * k : BATCH * (k + 1)].astype(F32), axis=0) for k in range(2)
     )
-    tile = left[4:8, HALF:] + right[4:8, HALF:]
-    total = row_of(tile, range(3)) * (1.0 / COUNTED)
-    scale = gain_ref[...] / stat_ref[1:2, :]
-    grad = base_ref[...] - scale * total[:, :CH] - normed_ref[...] * (scale * total[:, CH:])
-    grad_ref[...] = grad.astype(BF16)
+    total = row_of(left[4:8, HALF:] + right[4:8, HALF:], range(3)) * (1.0 / COUNTED)
+    spread = stat_ref[1:2, :]
+    normed = (x - stat_ref[0:1, :]) / spread
+    dpre = unwoven(plane_ref[:, :, 3 * HALF : 3 * HALF + CH // 2])
+    change = flat(gain_ref) * (dpre - total[:, :CH] - normed * total[:, CH:]) / spread
+    grad_ref[...] = (cot_ref[...].astype(F32) + change).astype(BF16)
     for rows, lanes, count in ((slice(0, 8), 0, 8), (slice(8, 12), HALF, 4)):
         conv_ref[rows, :HALF] = left[:count, lanes : lanes + HALF]
         conv_ref[rows, HALF:] = right[:count, lanes : lanes + CH - HALF]
-        proj_ref[rows, :] = right[:count, lanes + CH - HALF : lanes + HALF]
+        proj_grad_ref[rows, :] = right[:count, lanes + CH - HALF : lanes + HALF]
 
 
 def per_device(inputs, cotangent, conv_weight, proj_weight, gain_in, bias_in, gain_mid, bias_mid):
     x = inputs.reshape(ROWS, CH)
     cot = cotangent.reshape(ROWS, CH)
-    gain_in, bias_in, gain_mid, bias_mid = (v[None] for v in (gain_in, bias_in, gain_mid, bias_mid))
     rows, rows_mid = (ROWS, CH), (ROWS, MID)
 
-    (sums,) = kernel(first_sums, ((LINES, 1, 2 * CH), F32), name="first_sums")(x)
-    (data,) = kernel(spread_data, ((PLANES, 8, HALF), BF16), name="spread_data")(x, cot, proj_weight)
+    far, near = pl.BlockSpec(memory_space=pltpu.HBM), pl.BlockSpec(memory_space=pltpu.VMEM)
+    sums, data = pl.pallas_call(
+        opening,
+        out_shape=(
+            jax.ShapeDtypeStruct((LINES, 1, 2 * CH), F32),
+            jax.ShapeDtypeStruct((PLANES, 8, HALF), BF16),
+        ),
+        in_specs=[far] * 3,
+        out_specs=(near, near),
+        scratch_shapes=[
+            pltpu.VMEM(rows, BF16),
+            pltpu.VMEM(rows, BF16),
+            pltpu.VMEM((MID, CH), BF16),
+            pltpu.SemaphoreType.DMA((3,)),
+        ],
+        name="opening",
+        compiler_params=pltpu.CompilerParams(vmem_limit_bytes=24 << 20),
+    )(*(pltpu.with_memory_space_constraint(v, pltpu.HBM) for v in (x, cot, proj_weight)))
     sums = exchange(sums, LINE)
     (both,) = kernel(spread_all, ((PLANES, 8, HALF + CH // 2), BF16), name="spread_all")(
-        near=(sums, data)
+        data, near=(sums,)
     )
     both = exchange(both, PLANE)
 
-    act_in, conv, sums, stat_in = kernel(
+    act_in, far_x, conv, dact_mid, sums, stat_in = kernel(
         forward_conv,
         (rows, BF16),
+        (rows, BF16),
+        (rows_mid, F32),
         (rows_mid, F32),
         ((LINES, 1, 2 * MID), F32),
         ((8, CH), F32),
         name="forward_conv",
     )(near=(both, conv_weight, gain_in, bias_in))
-    normed_in, slope_in, dact_mid = kernel(
-        beside_conv, (rows, F32), (rows, F32), (rows_mid, F32), name="beside_conv"
-    )(stat_in, gain_in, bias_in, near=(both,))
     sums = exchange(sums, LINE).sum(axis=0)
     sums = exchange(jnp.broadcast_to(sums, (PLANES, 1, 2 * MID)), PLANE)
 
@@ -316,9 +327,9 @@
         (rows_mid, F32),
         (rows_mid, F32),
         ((LINES, 1, 2 * MID), F32),
-        ((1, MID), F32),
+        ((8, MID), F32),
         name="middle",
-    )(conv, dact_mid, gain_mid, bias_mid, near=(sums,))
+    )(conv, dact_mid, near=(sums, gain_mid, bias_mid))
     sums = exchange(sums, LINE)
     (both,) = kernel(middle_plane, ((PLANES, 8, 256), BF16), name="middle_plane")(
         act_mid, near=(sums,)
@@ -327,24 +338,17 @@
 
     stacked, parts, act_mid = kernel(
         filter_parts, (rows, BF16), ((2, CH, HALF), BF16), (rows_mid, BF16), name="filter_parts"
-    )(dpre_mid, normed_mid, spread_mid, gain_mid, act_in, cot, near=(both,))
+    )(dpre_mid, normed_mid, spread_mid, act_in, near=(both, gain_mid, cot))
     parts = exchange(parts, "core")
-    (back,) = kernel(back_rows, ((PLANES, 8, CH // 2 + 256), BF16), name="back_rows")(
-        stacked, slope_in, normed_in, near=(conv_weight,)
-    )
     (plane,) = kernel(to_plane, ((PLANES, 8, 3 * HALF + CH // 2 + 256), BF16), name="to_plane")(
-        back, near=(parts,)
+        stacked, far_x, stat_in, near=(parts, conv_weight, gain_in, bias_in)
     )
     plane = exchange(plane, PLANE)
     (line,) = kernel(to_line, ((LINES, 8, 2 * HALF), BF16), name="to_line")(near=(plane,))
     line = exchange(line, LINE)
-    (block_out,) = kernel(block_rows, (rows, BF16), name="block_rows")(act_mid, x, proj_weight)
-    base, normed = kernel(beside_line, (rows, F32), (rows, F32), name="beside_line")(
-        x, cot, stat_in, gain_in, near=(plane,)
-    )
-    input_grad, conv_grad, proj_grad = kernel(
-        last_rows, (rows, BF16), ((12, CH), F32), ((12, MID), F32), name="last_rows"
-    )(stat_in, gain_in, near=(line, base, normed))
+    block_out, input_grad, conv_grad, proj_grad = kernel(
+        last_rows, (rows, BF16), (rows, BF16), ((12, CH), F32), ((12, MID), F32), name="last_rows"
+    )(act_mid, stat_in, near=(line, plane, x, cot, proj_weight, gain_in))
     return (
         block_out.reshape(inputs.shape),
         input_grad.reshape(inputs.shape),

time: 161 us -> 155 us (0.963)
  blocking collectives: 69.6 us -> 148 us
  waiting for transfers between devices: 37.9 us -> 0 us
  starting transfers between devices: 34.5 us -> 0 us
  local copies, waits for them, and re-layouts: 9.78 us -> 0.08 us
  Pallas kernels: 7.25 us -> 5.58 us
    all_to_all x4 -> x9, blocking collectives: 69.6 us -> 148 us  [exchange(): return lax.all_to_all(pieces, axes, split_axis=0, concat_axis=0, tiled=True)]
    all_to_all x5 -> x0, waiting for transfers between devices: 37.9 us -> none  [exchange(): return lax.all_to_all(pieces, axes, split_axis=0, concat_axis=0, tiled=True)]
    all_to_all x5 -> x0, starting transfers between devices: 34.5 us -> none  [exchange(): return lax.all_to_all(pieces, axes, split_axis=0, concat_axis=0, tiled=True)]
    unnamed x38 -> x16, local copies, waits for them, and re-layouts: 9.11 us -> 0.04 us
    pallas_call x14 -> x8, Pallas kernels: 7.25 us -> 3.98 us  [call(): pl.pallas_call(body, out_shape=shapes, in_specs=[whole] * len(args), out_...]
  transfers between devices with their start and end apart: 5 -> 0, of which waited for: 4 -> 0; matrix products, arithmetic and copies ran while one was open for 0% -> 0% of each run, Pallas kernels for 1% -> 0%
where the time goes in v4:
time: 155 us; the launch traced here: 154 us
  blocking collectives  148 us (95%)
  Pallas kernels  5.58 us (4%)
    all_to_all x9, blocking collectives, exchange(): return lax.all_to_all(pieces, axes, split_axis=0, concat_axis=0, tiled=True)  148 us
    pallas_call x8, Pallas kernels, call(): pl.pallas_call(body, out_shape=shapes, in_specs=[whole] * len(args), out_...  3.98 us

profile of v4, /device:TPU:8, one launch (start us, length us, event | category | flops | bytes accessed | tf_op | source)
XLA Modules:
  0.0 154.1 jit_solution(12676291954470513407)
XLA Ops:
  0.6 0.0 copy-start
  0.6 0.0 copy-start.4
  0.7 0.0 copy-start.5
  0.7 1.6 %opening.1 = (f32[16,1,1536]{2,1,0:T(1,128)S(1)}, bf16[32,8,512]{2,1,0:T(8,128)(2,1)S(1)}) custom-call(bf16[128,768]{1,0:T(8,128)(2,1)} %bitcast.7, bf16[128,768]{1,0:T(8,128)(2,1)} %bitcast.4, bf16[256,768]{1,0:T(8,128)(2,1)} %proj_ref.1), custom_call_target="tpu_custom_call" | custom-call | tf_op jit(solution)/shard_map/opening/pallas_call | solution.py:288
  2.3 15.8 %all_to_all.45.sums_ref = f32[16,1,1536]{2,1,0:T(1,128)S(1)} all-to-all(f32[16,1,1536]{2,1,0:T(1,128)S(1)} %get-tuple-element.24), channel_id=1, replica_groups=mesh['x'=4,'z_hi'=2,'z_lo'=4,'core'=2,'dp'=8] {'core','dp'}, dimensions={0} | all-to-all | bytes 196608 | tf_op jit(solution)/shard_map/all_to_all | solution.py:24
  18.1 0.1 spread_all.1
  18.2 27.5 %all_to_all.46.got_ref = bf16[32,8,896]{2,1,0:T(8,128)(2,1)S(1)} all-to-all(bf16[32,8,896]{2,1,0:T(8,128)(2,1)S(1)} %spread_all.1), channel_id=1, replica_groups=mesh['x'=4,'z_hi'=2,'z_lo'=4,'core'=2,'dp'=8] {'x','z_hi','z_lo'}, dimensions={0} | all-to-all | bytes 917504 | tf_op jit(solution)/shard_map/all_to_all | solution.py:24
  45.7 0.0 copy-done
  45.7 0.0 copy-done.4
  45.7 0.0 copy-done.5
  45.7 0.0 copy-start.6
  45.7 0.0 copy-start.7
  45.7 0.0 copy-start.1
  45.7 0.6 forward_conv.1
  46.4 9.8 %all_to_all.47 = f32[16,1,512]{2,1,0:T(1,128)S(1)} all-to-all(f32[16,1,512]{2,1,0:T(1,128)S(1)} %get-tuple-element.26), channel_id=1, replica_groups=mesh['x'=4,'z_hi'=2,'z_lo'=4,'core'=2,'dp'=8] {'core','dp'}, dimensions={0} | all-to-all | bytes 65536 | tf_op jit(solution)/shard_map/all_to_all | solution.py:24
  56.2 15.6 %all_to_all.48.got_ref = f32[32,1,512]{2,1,0:T(1,128)S(1)} all-to-all(f32[32,1,512]{2,1,0:T(1,128)S(1)} %broadcast_in_dim.3), channel_id=1, replica_groups=mesh['x'=4,'z_hi'=2,'z_lo'=4,'core'=2,'dp'=8] {'x','z_hi','z_lo'}, dimensions={0} | all-to-all | bytes 131072 | tf_op jit(solution)/shard_map/all_to_all | solution.py:24
  71.8 0.0 copy-done.6
  71.8 0.0 copy-done.7
  71.9 0.2 middle.1
  72.1 10.2 %all_to_all.49.sums_ref = f32[16,1,512]{2,1,0:T(1,128)S(1)} all-to-all(f32[16,1,512]{2,1,0:T(1,128)S(1)} %get-tuple-element.29), channel_id=1, replica_groups=mesh['x'=4,'z_hi'=2,'z_lo'=4,'core'=2,'dp'=8] {'core','dp'}, dimensions={0} | all-to-all | bytes 65536 | tf_op jit(solution)/shard_map/all_to_all | solution.py:24
  82.3 0.1 middle_plane.1
  82.3 13.7 %all_to_all.50.got_ref = bf16[32,8,256]{2,1,0:T(8,128)(2,1)S(1)} all-to-all(bf16[32,8,256]{2,1,0:T(8,128)(2,1)S(1)} %middle_plane.1), channel_id=1, replica_groups=mesh['x'=4,'z_hi'=2,'z_lo'=4,'core'=2,'dp'=8] {'x','z_hi','z_lo'}, dimensions={0} | all-to-all | bytes 262144 | tf_op jit(solution)/shard_map/all_to_all | solution.py:24
  96.0 0.0 copy-done.1
  96.0 0.6 filter_parts.1
  96.6 5.0 %all_to_all.51.parts_ref = bf16[2,768,512]{2,1,0:T(8,128)(2,1)S(1)} all-to-all(bf16[2,768,512]{2,1,0:T(8,128)(2,1)S(1)} %get-tuple-element.35), channel_id=1, replica_groups=mesh['x'=4,'z_hi'=2,'z_lo'=4,'core'=2,'dp'=8] {'core'}, dimensions={0} | all-to-all | bytes 3145728 | tf_op jit(solution)/shard_map/all_to_all | solution.py:24
  101.6 1.1 to_plane.1
  102.7 35.6 %all_to_all.52.got_ref.plane_ref = bf16[32,8,2176]{2,1,0:T(8,128)(2,1)S(1)} all-to-all(bf16[32,8,2176]{2,1,0:T(8,128)(2,1)S(1)} %to_plane.1), channel_id=1, replica_groups=mesh['x'=4,'z_hi'=2,'z_lo'=4,'core'=2,'dp'=8] {'x','z_hi','z_lo'}, dimensions={0} | all-to-all | bytes 2228224 | tf_op jit(solution)/shard_map/all_to_all | solution.py:24
  138.3 0.0 copy-start.2
  138.3 0.0 copy-start.3
  138.3 0.1 to_line.1
  138.4 14.6 %all_to_all.53.got_ref = bf16[16,8,1024]{2,1,0:T(8,128)(2,1)S(1)} all-to-all(bf16[16,8,1024]{2,1,0:T(8,128)(2,1)S(1)} %to_line.1), channel_id=1, replica_groups=mesh['x'=4,'z_hi'=2,'z_lo'=4,'core'=2,'dp'=8] {'core','dp'}, dimensions={0} | all-to-all | bytes 524288 | tf_op jit(solution)/shard_map/all_to_all | solution.py:24
  153.0 0.0 copy-done.2
  153.0 0.0 copy-done.3
  153.0 1.1 last_rows.1
  (2 shorter events, 0.1 us)
Async XLA Ops:
  0.6 45.0 %copy-start = (bf16[768,768]{1,0:T(8,128)(2,1)S(1)}, bf16[768,768]{1,0:T(8,128)(2,1)}, u32[]{:S(2)}) copy-start(bf16[768,768]{1,0:T(8,128)(2,1)} %weight_ref.3) | copy-start | bytes 3538948
  0.6 45.0 %copy-start.4 = (f32[768]{0:T(1024)S(1)}, f32[768]{0:T(1024)}, u32[]{:S(2)}) copy-start(f32[768]{0:T(1024)} %gain_ref.9) | copy-start | bytes 9220
  0.7 45.0 %copy-start.5 = (f32[768]{0:T(1024)S(1)}, f32[768]{0:T(1024)}, u32[]{:S(2)}) copy-start(f32[768]{0:T(1024)} %bias_ref.5) | copy-start | bytes 9220
  45.7 26.2 %copy-start.6 = (f32[256]{0:T(256)S(1)}, f32[256]{0:T(256)}, u32[]{:S(2)}) copy-start(f32[256]{0:T(256)} %gain_ref.7) | copy-start | bytes 3076
  45.7 26.1 %copy-start.7 = (f32[256]{0:T(256)S(1)}, f32[256]{0:T(256)}, u32[]{:S(2)}) copy-start(f32[256]{0:T(256)} %bias_ref.4) | copy-start | bytes 3076
  45.7 50.3 %copy-start.1 = (bf16[1,128,768]{2,1,0:T(8,128)(2,1)S(1)}, bf16[1,128,768]{2,1,0:T(8,128)(2,1)}, u32[]{:S(2)}) copy-start(bf16[1,128,768]{2,1,0:T(8,128)(2,1)} %param.9) | copy-start | bytes 589828
  138.3 14.7 %copy-start.2 = (bf16[256,768]{1,0:T(8,128)(2,1)S(1)}, bf16[256,768]{1,0:T(8,128)(2,1)}, u32[]{:S(2)}) copy-start(bf16[256,768]{1,0:T(8,128)(2,1)} %proj_ref.1) | copy-start | bytes 1179652
  138.3 14.7 %copy-start.3 = (bf16[1,128,768]{2,1,0:T(8,128)(2,1)S(1)}, bf16[1,128,768]{2,1,0:T(8,128)(2,1)}, u32[]{:S(2)}) copy-start(bf16[1,128,768]{2,1,0:T(8,128)(2,1)} %param.8) | copy-start | bytes 589828

commit v5 on v4

--- a/solution.py
+++ b/solution.py
@@ -199,8 +199,31 @@
     out_ref[:, :, 128:] = jnp.broadcast_to(tile[None], (PLANES, 8, 128))
 
 
+def in_four(value):
+    blank = jnp.zeros((1, HALF - CH // 2), F32)
+    return tile_of([jnp.concatenate([row, blank], axis=1) for row in in_two(value, CH // 2)], HALF)
+
+
+def from_four(tile):
+    return jnp.concatenate([tile[k : k + 1, : CH // 2] + tile[k + 2 : k + 3, : CH // 2] for k in range(2)], axis=1)
+
+
 def filter_parts(
-    got_ref, gain_ref, cot_ref, dpre_ref, normed_ref, spread_ref, act_in_ref, stacked_ref, parts_ref, act_ref
+    got_ref,
+    gain_ref,
+    cot_ref,
+    weight_ref,
+    gain_in_ref,
+    bias_in_ref,
+    dpre_ref,
+    normed_ref,
+    spread_ref,
+    act_in_ref,
+    x_ref,
+    stat_ref,
+    parts_ref,
+    act_ref,
+    back_ref,
 ):
     tile = jnp.sum(got_ref[:, :, 128:].astype(F32), axis=0) * (1.0 / COUNTED)
     tile = tile + pltpu.roll(tile, 4, axis=0)
@@ -208,33 +231,31 @@
     dconv = dpre_ref[...] - first - normed_ref[...] * second
     dconv = flat(gain_ref) * dconv / spread_ref[0:1, :]
     stacked = jnp.concatenate([earlier(dconv), dconv, later(dconv)], axis=1).astype(BF16)
-    stacked_ref[...] = stacked
     conv_part = matmul(act_in_ref[...], stacked, ((0,), (0,)))
-    parts_ref[0] = conv_part[:, :HALF].astype(BF16)
-    parts_ref[1, :, : HALF - MID] = conv_part[:, HALF:].astype(BF16)
+    parts_ref[0, :CH, :] = conv_part[:, :HALF].astype(BF16)
+    parts_ref[1, :CH, : HALF - MID] = conv_part[:, HALF:].astype(BF16)
     act = unwoven(got_ref[:, :, :128]).astype(BF16)
     act_ref[...] = act
     proj_part = matmul(cot_ref[...], act, ((0,), (0,)))
-    parts_ref[1, :, HALF - MID :] = proj_part.astype(BF16)
-
-
-def to_plane(parts_ref, weight_ref, gain_ref, bias_ref, stacked_ref, x_ref, stat_ref, out_ref):
+    parts_ref[1, :CH, HALF - MID :] = proj_part.astype(BF16)
     normed = (x_ref[...].astype(F32) - stat_ref[0:1, :]) / stat_ref[1:2, :]
-    pre = flat(gain_ref) * normed + flat(bias_ref)
-    dpre = matmul(stacked_ref[...], weight_ref[...], ((1,), (1,))) * slope_of(pre, tanh_of(pre))
-    sums = jnp.concatenate([sum_rows(dpre), sum_rows(dpre * normed)], axis=1)
-    rows = [sums[:, k : k + 128] for k in range(0, 2 * CH, 128)]
-    both = (parts_ref[0].astype(F32) + parts_ref[1].astype(F32)).astype(BF16)
-    both = both.reshape(PLANES, 3, 8, HALF)
+    pre = flat(gain_in_ref) * normed + flat(bias_in_ref)
+    dpre = matmul(stacked, weight_ref[...], ((1,), (1,))) * slope_of(pre, tanh_of(pre))
+    parts_ref[0, CH:, :] = in_four(sum_rows(dpre)).astype(BF16)
+    parts_ref[1, CH:, :] = in_four(sum_rows(dpre * normed)).astype(BF16)
+    back_ref[...] = woven(dpre)
+
+
+def to_plane(parts_ref, back_ref, out_ref):
+    both = parts_ref[0].astype(F32) + parts_ref[1].astype(F32)
+    pieces = both[:CH].astype(BF16).reshape(PLANES, 3, 8, HALF)
     for k in range(3):
-        out_ref[:, :, HALF * k : HALF * (k + 1)] = both[:, k]
+        out_ref[:, :, HALF * k : HALF * (k + 1)] = pieces[:, k]
     begin = 3 * HALF + CH // 2
-    out_ref[:, :, 3 * HALF : begin] = woven(dpre)
-    for k in range(2):
-        tile = tile_of(rows[6 * k : 6 * k + 6], 128).astype(BF16)
-        out_ref[:, :, begin + 128 * k : begin + 128 * (k + 1)] = jnp.broadcast_to(
-            tile[None], (PLANES, 8, 128)
-        )
+    out_ref[:, :, 3 * HALF : begin] = back_ref[...]
+    sums = from_four(both[CH:])
+    tile = tile_of([sums[:, k : k + 128] for k in range(0, CH, 128)], 128).astype(BF16)
+    out_ref[:, :, begin:] = jnp.broadcast_to(tile[None], (PLANES, 8, 128))
 
 
 def to_line(got_ref, out_ref):
@@ -242,9 +263,7 @@
         jnp.sum(got_ref[:, :, HALF * k : HALF * (k + 1)].astype(F32), axis=0) for k in range(3)
     ]
     sums = jnp.sum(got_ref[:, :, 3 * HALF + CH // 2 :].astype(F32), axis=0)
-    sums = [row_of(sums[:, 128 * k : 128 * (k + 1)], range(6)) for k in range(2)]
-    sums = jnp.concatenate(sums, axis=1)
-    low = pltpu.roll(tile_of([sums[:, k : k + HALF] for k in range(0, 2 * CH, HALF)], HALF), 4, axis=0)
+    low = pltpu.roll(in_four(row_of(sums, range(6))), 4, axis=0)
     upper = lax.broadcasted_iota(jnp.int32, (8, HALF), 0) < 4
     turned = [pltpu.roll(tile, 4, axis=0) for tile in tiles]
     own = (
@@ -267,11 +286,11 @@
     left, right = (
         jnp.sum(got_ref[BATCH * k : BATCH * (k + 1)].astype(F32), axis=0) for k in range(2)
     )
-    total = row_of(left[4:8, HALF:] + right[4:8, HALF:], range(3)) * (1.0 / COUNTED)
+    first, second = (from_four(half[4:8, HALF:]) * (1.0 / COUNTED) for half in (left, right))
     spread = stat_ref[1:2, :]
     normed = (x - stat_ref[0:1, :]) / spread
     dpre = unwoven(plane_ref[:, :, 3 * HALF : 3 * HALF + CH // 2])
-    change = flat(gain_ref) * (dpre - total[:, :CH] - normed * total[:, CH:]) / spread
+    change = flat(gain_ref) * (dpre - first - normed * second) / spread
     grad_ref[...] = (cot_ref[...].astype(F32) + change).astype(BF16)
     for rows, lanes, count in ((slice(0, 8), 0, 8), (slice(8, 12), HALF, 4)):
         conv_ref[rows, :HALF] = left[:count, lanes : lanes + HALF]
@@ -314,12 +333,12 @@
         (rows, BF16),
         (rows_mid, F32),
         (rows_mid, F32),
-        ((LINES, 1, 2 * MID), F32),
+        ((PLANES, 1, 2 * MID), F32),
         ((8, CH), F32),
         name="forward_conv",
     )(near=(both, conv_weight, gain_in, bias_in))
-    sums = exchange(sums, LINE).sum(axis=0)
-    sums = exchange(jnp.broadcast_to(sums, (PLANES, 1, 2 * MID)), PLANE)
+    sums = exchange(sums, PLANE).sum(axis=0)
+    sums = exchange(jnp.broadcast_to(sums, (LINES, 1, 2 * MID)), LINE)
 
     act_mid, normed_mid, dpre_mid, sums, spread_mid = kernel(
         middle,
@@ -336,12 +355,24 @@
     )
     both = exchange(both, PLANE)
 
-    stacked, parts, act_mid = kernel(
-        filter_parts, (rows, BF16), ((2, CH, HALF), BF16), (rows_mid, BF16), name="filter_parts"
-    )(dpre_mid, normed_mid, spread_mid, act_in, near=(both, gain_mid, cot))
+    parts, act_mid, back = kernel(
+        filter_parts,
+        ((2, CH + 8, HALF), BF16),
+        (rows_mid, BF16),
+        ((PLANES, 8, CH // 2), BF16),
+        name="filter_parts",
+    )(
+        dpre_mid,
+        normed_mid,
+        spread_mid,
+        act_in,
+        far_x,
+        stat_in,
+        near=(both, gain_mid, cot, conv_weight, gain_in, bias_in),
+    )
     parts = exchange(parts, "core")
-    (plane,) = kernel(to_plane, ((PLANES, 8, 3 * HALF + CH // 2 + 256), BF16), name="to_plane")(
-        stacked, far_x, stat_in, near=(parts, conv_weight, gain_in, bias_in)
+    (plane,) = kernel(to_plane, ((PLANES, 8, 3 * HALF + CH // 2 + 128), BF16), name="to_plane")(
+        back, near=(parts,)
     )
     plane = exchange(plane, PLANE)
     (line,) = kernel(to_line, ((LINES, 8, 2 * HALF), BF16), name="to_line")(near=(plane,))

time: 155 us -> 151 us (0.974)
  blocking collectives: 148 us -> 145 us
    all_to_all x9, blocking collectives: 148 us -> 145 us  [exchange(): return lax.all_to_all(pieces, axes, split_axis=0, concat_axis=0, tiled=True)]
where the time goes in v5:
time: 151 us
  blocking collectives  145 us (96%)
  Pallas kernels  5.17 us (3%)
    all_to_all x9, blocking collectives, exchange(): return lax.all_to_all(pieces, axes, split_axis=0, concat_axis=0, tiled=True)  145 us
    pallas_call x8, Pallas kernels, call(): pl.pallas_call(body, out_shape=shapes, in_specs=[whole] * len(args), out_...  3.57 us

profile of v5, /device:TPU:8, one launch (start us, length us, event | category | flops | bytes accessed | tf_op | source)
XLA Modules:
  0.0 150.6 jit_solution(3393233030904640980)
XLA Ops:
  0.6 0.0 copy-start.4
  0.6 0.0 copy-start.5
  0.7 0.0 copy-start
  0.7 1.6 %opening.1 = (f32[16,1,1536]{2,1,0:T(1,128)S(1)}, bf16[32,8,512]{2,1,0:T(8,128)(2,1)S(1)}) custom-call(bf16[128,768]{1,0:T(8,128)(2,1)} %bitcast.7, bf16[128,768]{1,0:T(8,128)(2,1)} %bitcast.4, bf16[256,768]{1,0:T(8,128)(2,1)} %proj_ref.1), custom_call_target="tpu_custom_call" | custom-call | tf_op jit(solution)/shard_map/opening/pallas_call | solution.py:307
  2.3 15.8 %all_to_all.45.sums_ref = f32[16,1,1536]{2,1,0:T(1,128)S(1)} all-to-all(f32[16,1,1536]{2,1,0:T(1,128)S(1)} %get-tuple-element.24), channel_id=1, replica_groups=mesh['x'=4,'z_hi'=2,'z_lo'=4,'core'=2,'dp'=8] {'core','dp'}, dimensions={0} | all-to-all | bytes 196608 | tf_op jit(solution)/shard_map/all_to_all | solution.py:24
  18.1 0.1 spread_all.1
  18.2 0.0 copy-start.6
  18.2 0.0 copy-start.7
  18.2 27.5 %all_to_all.46.got_ref = bf16[32,8,896]{2,1,0:T(8,128)(2,1)S(1)} all-to-all(bf16[32,8,896]{2,1,0:T(8,128)(2,1)S(1)} %spread_all.1), channel_id=1, replica_groups=mesh['x'=4,'z_hi'=2,'z_lo'=4,'core'=2,'dp'=8] {'x','z_hi','z_lo'}, dimensions={0} | all-to-all | bytes 917504 | tf_op jit(solution)/shard_map/all_to_all | solution.py:24
  45.7 0.0 copy-done.4
  45.7 0.0 copy-done.5
  45.7 0.0 copy-done
  45.7 0.0 copy-start.1
  45.7 0.7 forward_conv.1
  46.4 15.3 %all_to_all.47 = f32[32,1,512]{2,1,0:T(1,128)S(1)} all-to-all(f32[32,1,512]{2,1,0:T(1,128)S(1)} %get-tuple-element.26), channel_id=1, replica_groups=mesh['x'=4,'z_hi'=2,'z_lo'=4,'core'=2,'dp'=8] {'x','z_hi','z_lo'}, dimensions={0} | all-to-all | bytes 131072 | tf_op jit(solution)/shard_map/all_to_all | solution.py:24
  61.7 0.1 reduce_sum.9
  61.8 10.1 %all_to_all.48.got_ref = f32[16,1,512]{2,1,0:T(1,128)S(1)} all-to-all(f32[16,1,512]{2,1,0:T(1,128)S(1)} %broadcast_in_dim.3), channel_id=1, replica_groups=mesh['x'=4,'z_hi'=2,'z_lo'=4,'core'=2,'dp'=8] {'core','dp'}, dimensions={0} | all-to-all | bytes 65536 | tf_op jit(solution)/shard_map/all_to_all | solution.py:24
  71.9 0.0 copy-done.6
  71.9 0.0 copy-done.7
  71.9 0.2 middle.1
  72.1 10.2 %all_to_all.49.sums_ref = f32[16,1,512]{2,1,0:T(1,128)S(1)} all-to-all(f32[16,1,512]{2,1,0:T(1,128)S(1)} %get-tuple-element.29), channel_id=1, replica_groups=mesh['x'=4,'z_hi'=2,'z_lo'=4,'core'=2,'dp'=8] {'core','dp'}, dimensions={0} | all-to-all | bytes 65536 | tf_op jit(solution)/shard_map/all_to_all | solution.py:24
  82.3 0.1 middle_plane.1
  82.3 13.7 %all_to_all.50.got_ref = bf16[32,8,256]{2,1,0:T(8,128)(2,1)S(1)} all-to-all(bf16[32,8,256]{2,1,0:T(8,128)(2,1)S(1)} %middle_plane.1), channel_id=1, replica_groups=mesh['x'=4,'z_hi'=2,'z_lo'=4,'core'=2,'dp'=8] {'x','z_hi','z_lo'}, dimensions={0} | all-to-all | bytes 262144 | tf_op jit(solution)/shard_map/all_to_all | solution.py:24
  96.0 0.0 copy-done.1
  96.0 1.1 filter_parts.1
  97.1 5.0 %all_to_all.51.parts_ref = bf16[2,776,512]{2,1,0:T(8,128)(2,1)S(1)} all-to-all(bf16[2,776,512]{2,1,0:T(8,128)(2,1)S(1)} %get-tuple-element.37), channel_id=1, replica_groups=mesh['x'=4,'z_hi'=2,'z_lo'=4,'core'=2,'dp'=8] {'core'}, dimensions={0} | all-to-all | bytes 3178496 | tf_op jit(solution)/shard_map/all_to_all | solution.py:24
  102.1 0.2 to_plane.1
  102.3 0.0 copy-start.2
  102.3 0.0 copy-start.3
  102.3 32.6 %all_to_all.52.got_ref.plane_ref = bf16[32,8,2048]{2,1,0:T(8,128)(2,1)S(1)} all-to-all(bf16[32,8,2048]{2,1,0:T(8,128)(2,1)S(1)} %to_plane.1), channel_id=1, replica_groups=mesh['x'=4,'z_hi'=2,'z_lo'=4,'core'=2,'dp'=8] {'x','z_hi','z_lo'}, dimensions={0} | all-to-all | bytes 2097152 | tf_op jit(solution)/shard_map/all_to_all | solution.py:24
  134.9 0.1 to_line.1
  135.1 14.4 %all_to_all.53.got_ref = bf16[16,8,1024]{2,1,0:T(8,128)(2,1)S(1)} all-to-all(bf16[16,8,1024]{2,1,0:T(8,128)(2,1)S(1)} %to_line.1), channel_id=1, replica_groups=mesh['x'=4,'z_hi'=2,'z_lo'=4,'core'=2,'dp'=8] {'core','dp'}, dimensions={0} | all-to-all | bytes 524288 | tf_op jit(solution)/shard_map/all_to_all | solution.py:24
  149.5 0.0 copy-done.2
  149.5 0.0 copy-done.3
  149.5 1.1 last_rows.1
  (1 shorter events, 0.0 us)
Async XLA Ops:
  0.6 45.1 %copy-start.4 = (f32[768]{0:T(1024)S(1)}, f32[768]{0:T(1024)}, u32[]{:S(2)}) copy-start(f32[768]{0:T(1024)} %gain_ref.7) | copy-start | bytes 9220
  0.6 45.1 %copy-start.5 = (f32[768]{0:T(1024)S(1)}, f32[768]{0:T(1024)}, u32[]{:S(2)}) copy-start(f32[768]{0:T(1024)} %bias_in_ref.1) | copy-start | bytes 9220
  0.7 45.1 %copy-start = (bf16[768,768]{1,0:T(8,128)(2,1)S(1)}, bf16[768,768]{1,0:T(8,128)(2,1)}, u32[]{:S(2)}) copy-start(bf16[768,768]{1,0:T(8,128)(2,1)} %weight_ref.3) | copy-start | bytes 3538948
  18.2 53.6 %copy-start.6 = (f32[256]{0:T(256)S(1)}, f32[256]{0:T(256)}, u32[]{:S(2)}) copy-start(f32[256]{0:T(256)} %gain_ref.6) | copy-start | bytes 3076
  18.2 53.6 %copy-start.7 = (f32[256]{0:T(256)S(1)}, f32[256]{0:T(256)}, u32[]{:S(2)}) copy-start(f32[256]{0:T(256)} %bias_ref.3) | copy-start | bytes 3076
  45.7 50.3 %copy-start.1 = (bf16[1,128,768]{2,1,0:T(8,128)(2,1)S(1)}, bf16[1,128,768]{2,1,0:T(8,128)(2,1)}, u32[]{:S(2)}) copy-start(bf16[1,128,768]{2,1,0:T(8,128)(2,1)} %param.9) | copy-start | bytes 589828
  102.3 47.2 %copy-start.2 = (bf16[256,768]{1,0:T(8,128)(2,1)S(1)}, bf16[256,768]{1,0:T(8,128)(2,1)}, u32[]{:S(2)}) copy-start(bf16[256,768]{1,0:T(8,128)(2,1)} %proj_ref.1) | copy-start | bytes 1179652
  102.3 47.2 %copy-start.3 = (bf16[1,128,768]{2,1,0:T(8,128)(2,1)S(1)}, bf16[1,128,768]{2,1,0:T(8,128)(2,1)}, u32[]{:S(2)}) copy-start(bf16[1,128,768]{2,1,0:T(8,128)(2,1)} %param.8) | copy-start | bytes 589828

commit v6 on v5

--- a/solution.py
+++ b/solution.py
@@ -10,11 +10,13 @@
 
 SEQ = ("x", "z_hi", "z_lo", "core")
 PLANE = ("x", "z_hi", "z_lo")
+DEPTH = ("z_hi", "z_lo")
 LINE = ("core", "dp")
 BF16, F32 = jnp.bfloat16, jnp.float32
 CH, MID = 768, 256
 ROWS, SHIFT = 128, 16
 PLANES, LINES, BATCH = 32, 16, 8
+ACROSS, DEEP = 4, 8
 HALF = 512
 COUNTED = 8.0 * 8192.0
 COEFF = math.sqrt(2.0 / math.pi)
@@ -124,7 +126,7 @@
     )
 
 
-def opening(x_hbm, cot_hbm, proj_hbm, sums_ref, data_ref, x_ref, cot_ref, proj_ref, sems):
+def opening(x_hbm, cot_hbm, proj_hbm, sums_ref, data_ref, dact_ref, x_ref, cot_ref, proj_ref, sems):
     pairs = ((x_hbm, x_ref), (cot_hbm, cot_ref), (proj_hbm, proj_ref))
     loads = [pltpu.make_async_copy(*pair, sems.at[k]) for k, pair in enumerate(pairs)]
     for load in loads:
@@ -135,10 +137,10 @@
     apart = x - mean
     copies(sums_ref, slice(0, CH), mean)
     copies(sums_ref, slice(CH, 2 * CH), sum_rows(apart * apart))
-    data_ref[:, :, : CH // 2] = woven(x)
+    data_ref[...] = woven(x)
     loads[1].wait()
     loads[2].wait()
-    data_ref[:, :, CH // 2 :] = woven(matmul(cot_ref[...], proj_ref[...], ((1,), (1,))))
+    dact_ref[...] = woven(matmul(cot_ref[...], proj_ref[...], ((1,), (1,))))
 
 
 def spread_all(sums_ref, data_ref, out_ref):
@@ -148,20 +150,23 @@
     apart = means - mean[None]
     squares = jnp.sum(sums[:, :, CH:] + float(ROWS) * (apart * apart), axis=0)
     tile = tile_of(in_two(mean, CH // 2) + in_two(squares, CH // 2), CH // 2).astype(BF16)
-    out_ref[:, :, :HALF] = data_ref[...]
-    out_ref[:, :, HALF:] = jnp.broadcast_to(tile[None], (PLANES, 8, CH // 2))
-
-
-def forward_conv(got_ref, weight_ref, gain_ref, bias_ref, act_ref, x_ref, conv_ref, dact_ref, sums_ref, stat_ref):
-    parts = got_ref[:, :, HALF:].astype(F32)
+    out_ref[:, :, : CH // 2] = data_ref[...]
+    out_ref[:, :, CH // 2 :] = jnp.broadcast_to(tile[None], (PLANES, 8, CH // 2))
+
+
+def over_pieces(parts, count):
+    parts = parts.astype(F32)
     parts = parts + pltpu.roll(parts, 6, axis=1)
     total = jnp.sum(parts, axis=0)
     mean = total * (1.0 / PLANES)
     apart = parts - mean[None]
-    between = jnp.sum(apart * apart, axis=0) * float(ROWS * LINES)
-    center = row_of(mean, (0, 1))
-    variance = (row_of(total, (4, 5)) + row_of(between, (0, 1))) * (1.0 / COUNTED)
-    spread = jnp.sqrt(variance + 1e-05)
+    between = jnp.sum(apart * apart, axis=0) * float(count)
+    return row_of(mean, (0, 1)), row_of(total, (4, 5)) + row_of(between, (0, 1))
+
+
+def forward_conv(got_ref, weight_ref, gain_ref, bias_ref, dact_ref, act_ref, x_ref, conv_ref, out_ref, stat_ref):
+    center, squares = over_pieces(got_ref[:, :, CH // 2 :], ROWS * LINES)
+    spread = jnp.sqrt(squares * (1.0 / COUNTED) + 1e-05)
     stat_ref[0:1, :] = center
     stat_ref[1:2, :] = spread
     x = unwoven(got_ref[:, :, : CH // 2])
@@ -172,20 +177,30 @@
     terms = matmul(act, weight_ref[...], ((1,), (0,)))
     conv = later(terms[:, :MID]) + terms[:, MID : 2 * MID] + earlier(terms[:, 2 * MID :])
     conv_ref[...] = conv
-    copies(sums_ref, slice(0, MID), sum_rows(conv))
-    copies(sums_ref, slice(MID, 2 * MID), sum_rows(conv * conv))
-    dact_ref[...] = unwoven(got_ref[:, :, CH // 2 : HALF])
-
-
-def middle(got_ref, gain_ref, bias_ref, conv_ref, dact_ref, act_ref, normed_ref, dpre_ref, sums_ref, spread_ref):
-    total = jnp.sum(got_ref[...], axis=0) * (1.0 / COUNTED)
-    center = total[:, :MID]
-    spread = jnp.sqrt(total[:, MID:] - center * center + 1e-05)
+    mean = sum_rows(conv) * (1.0 / ROWS)
+    apart = conv - mean
+    tile = tile_of(in_two(mean, 128) + in_two(sum_rows(apart * apart), 128), 128).astype(BF16)
+    out_ref[:, :, :128] = dact_ref[...]
+    out_ref[:, :, 128:] = jnp.broadcast_to(tile[None], (PLANES, 8, 128))
+
+
+def middle_line(got_ref, out_ref):
+    mean, squares = over_pieces(got_ref[:, :, 128:], ROWS)
+    copies(out_ref, slice(0, MID), mean)
+    copies(out_ref, slice(MID, 2 * MID), squares)
+
+
+def middle(got_ref, plane_ref, gain_ref, bias_ref, conv_ref, act_ref, normed_ref, dpre_ref, sums_ref, spread_ref):
+    means = got_ref[:, :, :MID]
+    center = jnp.sum(means, axis=0) * (1.0 / LINES)
+    apart = means - center[None]
+    squares = jnp.sum(got_ref[:, :, MID:] + float(ROWS * PLANES) * (apart * apart), axis=0)
+    spread = jnp.sqrt(squares * (1.0 / COUNTED) + 1e-05)
     spread_ref[0:1, :] = spread
     normed = (conv_ref[...] - center) / spread
     pre = flat(gain_ref) * normed + flat(bias_ref)
     inner = tanh_of(pre)
-    dpre = dact_ref[...] * slope_of(pre, inner)
+    dpre = unwoven(plane_ref[:, :, :128]) * slope_of(pre, inner)
     copies(sums_ref, slice(0, MID), sum_rows(dpre))
     copies(sums_ref, slice(MID, 2 * MID), sum_rows(dpre * normed))
     normed_ref[...] = normed
@@ -258,11 +273,22 @@
     out_ref[:, :, begin:] = jnp.broadcast_to(tile[None], (PLANES, 8, 128))
 
 
+def to_depth(got_ref, out_ref):
+    sums = jnp.sum(got_ref[:, :, :, : 3 * HALF].astype(F32), axis=0)
+    out_ref[:, :, : 3 * HALF] = sums.astype(BF16)
+    begin = 3 * HALF + CH // 2
+    for k in range(ACROSS):
+        lanes = slice(3 * HALF + k * CH // 2, 3 * HALF + (k + 1) * CH // 2)
+        out_ref[:, :, lanes] = got_ref[k, :, :, 3 * HALF : begin]
+    sums = jnp.sum(got_ref[:, :, :, begin:].astype(F32), axis=0)
+    out_ref[:, :, 3 * HALF + 2 * CH :] = sums.astype(BF16)
+
+
 def to_line(got_ref, out_ref):
     tiles = [
         jnp.sum(got_ref[:, :, HALF * k : HALF * (k + 1)].astype(F32), axis=0) for k in range(3)
     ]
-    sums = jnp.sum(got_ref[:, :, 3 * HALF + CH // 2 :].astype(F32), axis=0)
+    sums = jnp.sum(got_ref[:, :, 3 * HALF + 2 * CH :].astype(F32), axis=0)
     low = pltpu.roll(in_four(row_of(sums, range(6))), 4, axis=0)
     upper = lax.broadcasted_iota(jnp.int32, (8, HALF), 0) < 4
     turned = [pltpu.roll(tile, 4, axis=0) for tile in tiles]
@@ -278,7 +304,7 @@
 
 
 def last_rows(
-    got_ref, plane_ref, x_ref, cot_ref, proj_ref, gain_ref, act_ref, stat_ref, out_ref, grad_ref, conv_ref, proj_grad_ref
+    got_ref, depth_ref, x_ref, cot_ref, proj_ref, gain_ref, act_ref, stat_ref, out_ref, grad_ref, conv_ref, proj_grad_ref
 ):
     x = x_ref[...].astype(F32)
     update = matmul(act_ref[...], proj_ref[...], ((1,), (0,)))
@@ -289,7 +315,8 @@
     first, second = (from_four(half[4:8, HALF:]) * (1.0 / COUNTED) for half in (left, right))
     spread = stat_ref[1:2, :]
     normed = (x - stat_ref[0:1, :]) / spread
-    dpre = unwoven(plane_ref[:, :, 3 * HALF : 3 * HALF + CH // 2])
+    begins = range(3 * HALF, 3 * HALF + 2 * CH, CH // 2)
+    dpre = unwoven(jnp.concatenate([depth_ref[:, :, k : k + CH // 2] for k in begins], axis=0))
     change = flat(gain_ref) * (dpre - first - normed * second) / spread
     grad_ref[...] = (cot_ref[...].astype(F32) + change).astype(BF16)
     for rows, lanes, count in ((slice(0, 8), 0, 8), (slice(8, 12), HALF, 4)):
@@ -304,14 +331,15 @@
     rows, rows_mid = (ROWS, CH), (ROWS, MID)
 
     far, near = pl.BlockSpec(memory_space=pltpu.HBM), pl.BlockSpec(memory_space=pltpu.VMEM)
-    sums, data = pl.pallas_call(
+    sums, data, dact = pl.pallas_call(
         opening,
         out_shape=(
             jax.ShapeDtypeStruct((LINES, 1, 2 * CH), F32),
-            jax.ShapeDtypeStruct((PLANES, 8, HALF), BF16),
+            jax.ShapeDtypeStruct((PLANES, 8, CH // 2), BF16),
+            jax.ShapeDtypeStruct((PLANES, 8, 128), BF16),
         ),
         in_specs=[far] * 3,
-        out_specs=(near, near),
+        out_specs=(near,) * 3,
         scratch_shapes=[
             pltpu.VMEM(rows, BF16),
             pltpu.VMEM(rows, BF16),
@@ -322,23 +350,23 @@
         compiler_params=pltpu.CompilerParams(vmem_limit_bytes=24 << 20),
     )(*(pltpu.with_memory_space_constraint(v, pltpu.HBM) for v in (x, cot, proj_weight)))
     sums = exchange(sums, LINE)
-    (both,) = kernel(spread_all, ((PLANES, 8, HALF + CH // 2), BF16), name="spread_all")(
+    (both,) = kernel(spread_all, ((PLANES, 8, CH), BF16), name="spread_all")(
         data, near=(sums,)
     )
     both = exchange(both, PLANE)
 
-    act_in, far_x, conv, dact_mid, sums, stat_in = kernel(
+    act_in, far_x, conv, both, stat_in = kernel(
         forward_conv,
         (rows, BF16),
         (rows, BF16),
         (rows_mid, F32),
-        (rows_mid, F32),
-        ((PLANES, 1, 2 * MID), F32),
+        ((PLANES, 8, 256), BF16),
         ((8, CH), F32),
         name="forward_conv",
-    )(near=(both, conv_weight, gain_in, bias_in))
-    sums = exchange(sums, PLANE).sum(axis=0)
-    sums = exchange(jnp.broadcast_to(sums, (LINES, 1, 2 * MID)), LINE)
+    )(dact, near=(both, conv_weight, gain_in, bias_in))
+    both = exchange(both, PLANE)
+    (sums,) = kernel(middle_line, ((LINES, 1, 2 * MID), F32), name="middle_line")(near=(both,))
+    sums = exchange(sums, LINE)
 
     act_mid, normed_mid, dpre_mid, sums, spread_mid = kernel(
         middle,
@@ -348,7 +376,7 @@
         ((LINES, 1, 2 * MID), F32),
         ((8, MID), F32),
         name="middle",
-    )(conv, dact_mid, near=(sums, gain_mid, bias_mid))
+    )(conv, near=(sums, both, gain_mid, bias_mid))
     sums = exchange(sums, LINE)
     (both,) = kernel(middle_plane, ((PLANES, 8, 256), BF16), name="middle_plane")(
         act_mid, near=(sums,)
@@ -374,12 +402,16 @@
     (plane,) = kernel(to_plane, ((PLANES, 8, 3 * HALF + CH // 2 + 128), BF16), name="to_plane")(
         back, near=(parts,)
     )
-    plane = exchange(plane, PLANE)
-    (line,) = kernel(to_line, ((LINES, 8, 2 * HALF), BF16), name="to_line")(near=(plane,))
+    plane = exchange(plane.reshape(ACROSS, DEEP, *plane.shape[1:]), "x")
+    (depth,) = kernel(to_depth, ((DEEP, 8, 3 * HALF + 2 * CH + 128), BF16), name="to_depth")(
+        near=(plane,)
+    )
+    depth = exchange(depth, DEPTH)
+    (line,) = kernel(to_line, ((LINES, 8, 2 * HALF), BF16), name="to_line")(near=(depth,))
     line = exchange(line, LINE)
     block_out, input_grad, conv_grad, proj_grad = kernel(
         last_rows, (rows, BF16), (rows, BF16), ((12, CH), F32), ((12, MID), F32), name="last_rows"
-    )(act_mid, stat_in, near=(line, plane, x, cot, proj_weight, gain_in))
+    )(act_mid, stat_in, near=(line, depth, x, cot, proj_weight, gain_in))
     return (
         block_out.reshape(inputs.shape),
         input_grad.reshape(inputs.shape),

time: 151 us -> 153 us (1.013)
    all_to_all x9 -> x10, blocking collectives: 145 us -> 146 us  [exchange(): return lax.all_to_all(pieces, axes, split_axis=0, concat_axis=0, tiled=True)]
    pallas_call x8 -> x10, Pallas kernels: 3.57 us -> 3.73 us  [call(): pl.pallas_call(body, out_shape=shapes, in_specs=[whole] * len(args), out_...]
where the time goes in v6:
time: 153 us
  blocking collectives  146 us (95%)
  Pallas kernels  5.33 us (3%)
    all_to_all x10, blocking collectives, exchange(): return lax.all_to_all(pieces, axes, split_axis=0, concat_axis=0, tiled=True)  146 us
    pallas_call x10, Pallas kernels, call(): pl.pallas_call(body, out_shape=shapes, in_specs=[whole] * len(args), out_...  3.73 us

profile of v6, /device:TPU:8, one launch (start us, length us, event | category | flops | bytes accessed | tf_op | source)
XLA Modules:
  0.0 152.6 jit_solution(1631892594645191356)
XLA Ops:
  0.6 0.0 copy-start.4
  0.6 0.0 copy-start.5
  0.7 0.0 copy-start
  0.7 1.6 %opening.1 = (f32[16,1,1536]{2,1,0:T(1,128)S(1)}, bf16[32,8,384]{2,1,0:T(8,128)(2,1)S(1)}, bf16[32,8,128]{2,1,0:T(8,128)(2,1)S(1)}) custom-call(bf16[128,768]{1,0:T(8,128)(2,1)} %bitcast.9, bf16[128,768]{1,0:T(8,128)(2,1)} %bitcast.6, bf16[256,768]{1,0:T(8,128)(2,1)} %proj_ref.1), custom_call_target="tpu_custom_call" | custom-call | tf_op jit(solution)/shard_map/opening/pallas_call | solution.py:334
  2.3 15.8 %all_to_all.50.sums_ref = f32[16,1,1536]{2,1,0:T(1,128)S(1)} all-to-all(f32[16,1,1536]{2,1,0:T(1,128)S(1)} %get-tuple-element.24), channel_id=1, replica_groups=mesh['x'=4,'z_hi'=2,'z_lo'=4,'core'=2,'dp'=8] {'core','dp'}, dimensions={0} | all-to-all | bytes 196608 | tf_op jit(solution)/shard_map/all_to_all | solution.py:26
  18.1 0.1 spread_all.1
  18.2 0.0 copy-start.6
  18.2 0.0 copy-start.7
  18.2 26.4 %all_to_all.51.got_ref = bf16[32,8,768]{2,1,0:T(8,128)(2,1)S(1)} all-to-all(bf16[32,8,768]{2,1,0:T(8,128)(2,1)S(1)} %spread_all.1), channel_id=1, replica_groups=mesh['x'=4,'z_hi'=2,'z_lo'=4,'core'=2,'dp'=8] {'x','z_hi','z_lo'}, dimensions={0} | all-to-all | bytes 786432 | tf_op jit(solution)/shard_map/all_to_all | solution.py:26
  44.7 0.0 copy-start.1
  44.7 0.0 copy-done.4
  44.7 0.0 copy-done.5
  44.7 0.0 copy-done
  44.7 0.7 forward_conv.1
  45.4 15.3 %all_to_all.52.got_ref.plane_ref = bf16[32,8,256]{2,1,0:T(8,128)(2,1)S(1)} all-to-all(bf16[32,8,256]{2,1,0:T(8,128)(2,1)S(1)} %get-tuple-element.27), channel_id=1, replica_groups=mesh['x'=4,'z_hi'=2,'z_lo'=4,'core'=2,'dp'=8] {'x','z_hi','z_lo'}, dimensions={0} | all-to-all | bytes 262144 | tf_op jit(solution)/shard_map/all_to_all | solution.py:26
  60.7 0.1 middle_line.1
  60.8 10.0 %all_to_all.53.got_ref = f32[16,1,512]{2,1,0:T(1,128)S(1)} all-to-all(f32[16,1,512]{2,1,0:T(1,128)S(1)} %middle_line.1), channel_id=1, replica_groups=mesh['x'=4,'z_hi'=2,'z_lo'=4,'core'=2,'dp'=8] {'core','dp'}, dimensions={0} | all-to-all | bytes 65536 | tf_op jit(solution)/shard_map/all_to_all | solution.py:26
  70.8 0.0 copy-done.6
  70.8 0.0 copy-done.7
  70.8 0.2 middle.1
  71.1 10.2 %all_to_all.54.sums_ref = f32[16,1,512]{2,1,0:T(1,128)S(1)} all-to-all(f32[16,1,512]{2,1,0:T(1,128)S(1)} %get-tuple-element.29), channel_id=1, replica_groups=mesh['x'=4,'z_hi'=2,'z_lo'=4,'core'=2,'dp'=8] {'core','dp'}, dimensions={0} | all-to-all | bytes 65536 | tf_op jit(solution)/shard_map/all_to_all | solution.py:26
  81.3 0.1 middle_plane.1
  81.3 13.8 %all_to_all.55.got_ref = bf16[32,8,256]{2,1,0:T(8,128)(2,1)S(1)} all-to-all(bf16[32,8,256]{2,1,0:T(8,128)(2,1)S(1)} %middle_plane.1), channel_id=1, replica_groups=mesh['x'=4,'z_hi'=2,'z_lo'=4,'core'=2,'dp'=8] {'x','z_hi','z_lo'}, dimensions={0} | all-to-all | bytes 262144 | tf_op jit(solution)/shard_map/all_to_all | solution.py:26
  95.2 0.0 copy-done.1
  95.2 1.1 filter_parts.1
  96.3 5.0 %all_to_all.56.parts_ref = bf16[2,776,512]{2,1,0:T(8,128)(2,1)S(1)} all-to-all(bf16[2,776,512]{2,1,0:T(8,128)(2,1)S(1)} %get-tuple-element.37), channel_id=1, replica_groups=mesh['x'=4,'z_hi'=2,'z_lo'=4,'core'=2,'dp'=8] {'core'}, dimensions={0} | all-to-all | bytes 3178496 | tf_op jit(solution)/shard_map/all_to_all | solution.py:26
  101.3 0.2 to_plane.1
  101.5 18.1 %all_to_all.57.got_ref = bf16[4,8,8,2048]{3,2,1,0:T(8,128)(2,1)S(1)} all-to-all(bf16[4,8,8,2048]{3,2,1,0:T(8,128)(2,1)S(1)} %bitcast.5), channel_id=1, replica_groups=mesh['x'=4,'z_hi'=2,'z_lo'=4,'core'=2,'dp'=8] {'x'}, dimensions={0} | all-to-all | bytes 2097152 | tf_op jit(solution)/shard_map/all_to_all | solution.py:26
  119.6 0.0 copy-start.2
  119.6 0.0 copy-start.3
  119.6 0.1 to_depth.1
  119.7 17.2 %all_to_all.58.got_ref.depth_ref = bf16[8,8,3200]{2,1,0:T(8,128)(2,1)S(1)} all-to-all(bf16[8,8,3200]{2,1,0:T(8,128)(2,1)S(1)} %to_depth.1), channel_id=1, replica_groups=mesh['x'=4,'z_hi'=2,'z_lo'=4,'core'=2,'dp'=8] {'z_hi','z_lo'}, dimensions={0} | all-to-all | bytes 819200 | tf_op jit(solution)/shard_map/all_to_all | solution.py:26
  136.9 14.6 %all_to_all.59.got_ref = bf16[16,8,1024]{2,1,0:T(8,128)(2,1)S(1)} all-to-all(bf16[16,8,1024]{2,1,0:T(8,128)(2,1)S(1)} %to_line.1), channel_id=1, replica_groups=mesh['x'=4,'z_hi'=2,'z_lo'=4,'core'=2,'dp'=8] {'core','dp'}, dimensions={0} | all-to-all | bytes 524288 | tf_op jit(solution)/shard_map/all_to_all | solution.py:26
  151.5 0.0 copy-done.2
  151.5 0.0 copy-done.3
  151.5 1.1 last_rows.1
  (1 shorter events, 0.0 us)
Async XLA Ops:
  0.6 44.1 %copy-start.4 = (f32[768]{0:T(1024)S(1)}, f32[768]{0:T(1024)}, u32[]{:S(2)}) copy-start(f32[768]{0:T(1024)} %gain_ref.7) | copy-start | bytes 9220
  0.6 44.0 %copy-start.5 = (f32[768]{0:T(1024)S(1)}, f32[768]{0:T(1024)}, u32[]{:S(2)}) copy-start(f32[768]{0:T(1024)} %bias_in_ref.1) | copy-start | bytes 9220
  0.7 44.0 %copy-start = (bf16[768,768]{1,0:T(8,128)(2,1)S(1)}, bf16[768,768]{1,0:T(8,128)(2,1)}, u32[]{:S(2)}) copy-start(bf16[768,768]{1,0:T(8,128)(2,1)} %weight_ref.3) | copy-start | bytes 3538948
  18.2 52.6 %copy-start.6 = (f32[256]{0:T(256)S(1)}, f32[256]{0:T(256)}, u32[]{:S(2)}) copy-start(f32[256]{0:T(256)} %gain_ref.6) | copy-start | bytes 3076
  18.2 52.6 %copy-start.7 = (f32[256]{0:T(256)S(1)}, f32[256]{0:T(256)}, u32[]{:S(2)}) copy-start(f32[256]{0:T(256)} %bias_ref.3) | copy-start | bytes 3076
  44.7 50.5 %copy-start.1 = (bf16[1,128,768]{2,1,0:T(8,128)(2,1)S(1)}, bf16[1,128,768]{2,1,0:T(8,128)(2,1)}, u32[]{:S(2)}) copy-start(bf16[1,128,768]{2,1,0:T(8,128)(2,1)} %param.9) | copy-start | bytes 589828
  119.6 31.9 %copy-start.2 = (bf16[256,768]{1,0:T(8,128)(2,1)S(1)}, bf16[256,768]{1,0:T(8,128)(2,1)}, u32[]{:S(2)}) copy-start(bf16[256,768]{1,0:T(8,128)(2,1)} %proj_ref.1) | copy-start | bytes 1179652
  119.6 31.9 %copy-start.3 = (bf16[1,128,768]{2,1,0:T(8,128)(2,1)S(1)}, bf16[1,128,768]{2,1,0:T(8,128)(2,1)}, u32[]{:S(2)}) copy-start(bf16[1,128,768]{2,1,0:T(8,128)(2,1)} %param.8) | copy-start | bytes 589828

commit v7 on v6

v7 whole, which is shorter than its diff:
```python
import math

import jax
import jax.numpy as jnp
from jax import lax
from jax.experimental import pallas as pl
from jax.experimental.pallas import tpu as pltpu
from jax.sharding import Mesh
from jax.sharding import PartitionSpec as P

SEQ = ("x", "z_hi", "z_lo", "core")
PLANE = ("x", "z_hi", "z_lo")
LINE = ("core", "dp")
BF16, F32 = jnp.bfloat16, jnp.float32
CH, MID = 768, 256
ROWS, SHIFT = 128, 16
PLANES, LINES, BATCH = 32, 16, 8
WIDE, HALF = CH // 2, MID + CH // 2
COUNTED = 8.0 * 8192.0
COEFF = math.sqrt(2.0 / math.pi)


def exchange(pieces, axes):
    return lax.all_to_all(pieces, axes, split_axis=0, concat_axis=0, tiled=True)


def kernel(body, *outs, name):
    shapes = tuple(jax.ShapeDtypeStruct(shape, dtype) for shape, dtype in outs)
    whole = pl.BlockSpec(memory_space=pltpu.VMEM)

    def call(*args, near=()):
        near = tuple(pltpu.with_memory_space_constraint(a, pltpu.VMEM) for a in near)
        args = (*near, *args)
        return pl.pallas_call(
            body,
            out_shape=shapes,
            in_specs=[whole] * len(args),
            out_specs=(whole,) * len(shapes),
            name=name,
            compiler_params=pltpu.CompilerParams(vmem_limit_bytes=24 << 20),
        )(*args)

    return call


def matmul(a, b, dims):
    return lax.dot_general(a, b, (dims, ((), ())), preferred_element_type=F32)


def later(x):
    return jnp.concatenate([jnp.zeros_like(x[:SHIFT]), x[:-SHIFT]], axis=0)


def earlier(x):
    return jnp.concatenate([x[SHIFT:], jnp.zeros_like(x[:SHIFT])], axis=0)


def woven(value):
    width = value.shape[1] // 2
    tiles = value.astype(F32).reshape(ROWS // 8, 8, 2 * width)
    a, b = tiles[:, :, :width], tiles[:, :, width:]
    upper = lax.broadcasted_iota(jnp.int32, a.shape, 1) < 4
    even = jnp.where(upper, a, pltpu.roll(b, 4, axis=1))
    odd = jnp.where(upper, pltpu.roll(a, 4, axis=1), b)
    return jnp.stack([even, odd], axis=1).reshape(PLANES, 8, width).astype(BF16)


def unwoven(pieces):
    width = pieces.shape[2]
    pairs = pieces.astype(F32).reshape(ROWS // 8, 2, 8, width)
    even, odd = pairs[:, 0], pairs[:, 1]
    upper = lax.broadcasted_iota(jnp.int32, even.shape, 1) < 4
    a = jnp.where(upper, even, pltpu.roll(odd, 4, axis=1))
    b = jnp.where(upper, pltpu.roll(even, 4, axis=1), odd)
    return jnp.concatenate([a.reshape(ROWS, width), b.reshape(ROWS, width)], axis=1)


def rounded(value):
    return value.astype(BF16).astype(F32)


def tile_of(pieces, width):
    row = lax.broadcasted_iota(jnp.int32, (8, width), 0)
    tile = jnp.zeros((8, width), F32)
    for k, piece in enumerate(pieces):
        tile = jnp.where(row == k, piece, tile)
    return tile


def in_two(value, width):
    high = rounded(value)
    return [
        part[:, k : k + width] for part in (high, value - high) for k in range(0, value.shape[1], width)
    ]


def row_of(tile, rows):
    return jnp.concatenate([tile[k : k + 1] for k in rows], axis=1)


def sum_rows(value):
    return jnp.sum(value, axis=0, keepdims=True)


def flat(ref):
    return ref[...].reshape(1, ref.shape[0])


def copies(ref, index, row):
    ref[:, :, index] = jnp.broadcast_to(row, (ref.shape[0], 1, row.shape[1]))


def tanh_of(value):
    return jnp.tanh(COEFF * (value + 0.044715 * value * value * value))


def gelu_of(value, inner):
    return 0.5 * value * (1.0 + inner)


def slope_of(value, inner):
    return 0.5 * (1.0 + inner) + 0.5 * value * (1.0 - inner * inner) * COEFF * (
        1.0 + 3.0 * 0.044715 * value * value
    )


def opening(x_hbm, cot_hbm, sums_ref, data_ref, far_cot_ref, x_ref, cot_ref, sems):
    pairs = ((x_hbm, x_ref), (cot_hbm, cot_ref))
    loads = [pltpu.make_async_copy(*pair, sems.at[k]) for k, pair in enumerate(pairs)]
    for load in loads:
        load.start()
    loads[0].wait()
    x = x_ref[...].astype(F32)
    mean = sum_rows(x) * (1.0 / ROWS)
    apart = x - mean
    copies(sums_ref, slice(0, CH), mean)
    copies(sums_ref, slice(CH, 2 * CH), sum_rows(apart * apart))
    data_ref[...] = woven(x)
    loads[1].wait()
    far_cot_ref[...] = woven(cot_ref[...])


def spread_all(sums_ref, data_ref, out_ref):
    sums = sums_ref[...]
    means = sums[:, :, :CH]
    mean = jnp.sum(means, axis=0) * (1.0 / LINES)
    apart = means - mean[None]
    squares = jnp.sum(sums[:, :, CH:] + float(ROWS) * (apart * apart), axis=0)
    tile = tile_of(in_two(mean, WIDE) + in_two(squares, WIDE), WIDE).astype(BF16)
    out_ref[:, :, :WIDE] = data_ref[...]
    out_ref[:, :, WIDE :] = jnp.broadcast_to(tile[None], (PLANES, 8, WIDE))


def over_pieces(parts, count):
    parts = parts.astype(F32)
    parts = parts + pltpu.roll(parts, 6, axis=1)
    total = jnp.sum(parts, axis=0)
    mean = total * (1.0 / PLANES)
    apart = parts - mean[None]
    between = jnp.sum(apart * apart, axis=0) * float(count)
    return row_of(mean, (0, 1)), row_of(total, (4, 5)) + row_of(between, (0, 1))


def forward_conv(got_ref, weight_ref, gain_ref, bias_ref, cot_ref, act_ref, x_ref, conv_ref, out_ref, stat_ref):
    center, squares = over_pieces(got_ref[:, :, WIDE :], ROWS * LINES)
    spread = jnp.sqrt(squares * (1.0 / COUNTED) + 1e-05)
    stat_ref[0:1, :] = center
    stat_ref[1:2, :] = spread
    x = unwoven(got_ref[:, :, : WIDE])
    x_ref[...] = x.astype(BF16)
    pre = flat(gain_ref) * ((x - center) / spread) + flat(bias_ref)
    act = gelu_of(pre, tanh_of(pre)).astype(BF16)
    act_ref[...] = act
    terms = matmul(act, weight_ref[...], ((1,), (0,)))
    conv = later(terms[:, :MID]) + terms[:, MID : 2 * MID] + earlier(terms[:, 2 * MID :])
    conv_ref[...] = conv
    mean = sum_rows(conv) * (1.0 / ROWS)
    apart = conv - mean
    tile = tile_of(in_two(mean, 128) + in_two(sum_rows(apart * apart), 128), 128).astype(BF16)
    out_ref[:, :, :WIDE] = cot_ref[...]
    out_ref[:, :, WIDE:] = jnp.broadcast_to(tile[None], (PLANES, 8, 128))


def middle_line(got_ref, out_ref):
    mean, squares = over_pieces(got_ref[:, :, WIDE:], ROWS)
    copies(out_ref, slice(0, MID), mean)
    copies(out_ref, slice(MID, 2 * MID), squares)


def middle(
    got_ref,
    plane_ref,
    gain_ref,
    bias_ref,
    proj_ref,
    conv_ref,
    data_ref,
    normed_ref,
    dpre_ref,
    sums_ref,
    spread_ref,
):
    means = got_ref[:, :, :MID]
    center = jnp.sum(means, axis=0) * (1.0 / LINES)
    apart = means - center[None]
    squares = jnp.sum(got_ref[:, :, MID:] + float(ROWS * PLANES) * (apart * apart), axis=0)
    spread = jnp.sqrt(squares * (1.0 / COUNTED) + 1e-05)
    spread_ref[0:1, :] = spread
    normed = (conv_ref[...] - center) / spread
    pre = flat(gain_ref) * normed + flat(bias_ref)
    inner = tanh_of(pre)
    cot = unwoven(plane_ref[:, :, :WIDE]).astype(BF16)
    dpre = matmul(cot, proj_ref[...], ((1,), (1,))) * slope_of(pre, inner)
    copies(sums_ref, slice(0, MID), sum_rows(dpre))
    copies(sums_ref, slice(MID, 2 * MID), sum_rows(dpre * normed))
    normed_ref[...] = normed
    dpre_ref[...] = dpre
    act = gelu_of(pre, inner)
    data_ref[:, :, :128] = woven(act)
    part = matmul(cot, act.astype(BF16), ((0,), (0,))).astype(BF16).reshape(PLANES, 3, 8, MID)
    for k in range(3):
        data_ref[:, :, 128 + MID * k : 128 + MID * (k + 1)] = part[:, k]


def middle_plane(sums_ref, data_ref, out_ref):
    tile = tile_of(in_two(jnp.sum(sums_ref[...], axis=0), 128), 128).astype(BF16)
    out_ref[:, :, : 128 + CH] = data_ref[...]
    out_ref[:, :, 128 + CH :] = jnp.broadcast_to(tile[None], (PLANES, 8, 128))


def filter_parts(
    got_ref,
    gain_ref,
    weight_ref,
    gain_in_ref,
    bias_in_ref,
    dpre_ref,
    normed_ref,
    spread_ref,
    act_in_ref,
    x_ref,
    stat_ref,
    parts_ref,
    act_ref,
    proj_ref,
    back_ref,
):
    tile = jnp.sum(got_ref[:, :, 128 + CH :].astype(F32), axis=0) * (1.0 / COUNTED)
    tile = tile + pltpu.roll(tile, 4, axis=0)
    first, second = row_of(tile, (0, 1)), row_of(tile, (2, 3))
    dconv = dpre_ref[...] - first - normed_ref[...] * second
    dconv = flat(gain_ref) * dconv / spread_ref[0:1, :]
    stacked = jnp.concatenate([earlier(dconv), dconv, later(dconv)], axis=1).astype(BF16)
    part = matmul(act_in_ref[...], stacked, ((0,), (0,)))
    parts_ref[0, :CH, :] = part[:, :WIDE].astype(BF16)
    parts_ref[1, :CH, :] = part[:, WIDE:].astype(BF16)
    act_ref[...] = unwoven(got_ref[:, :, :128]).astype(BF16)
    proj_ref[...] = jnp.sum(got_ref[:, :, 128 : 128 + CH].astype(F32), axis=0)
    normed = (x_ref[...].astype(F32) - stat_ref[0:1, :]) / stat_ref[1:2, :]
    pre = flat(gain_in_ref) * normed + flat(bias_in_ref)
    dpre = matmul(stacked, weight_ref[...], ((1,), (1,))) * slope_of(pre, tanh_of(pre))
    parts_ref[0, CH:, :] = tile_of(in_two(sum_rows(dpre), WIDE), WIDE).astype(BF16)
    parts_ref[1, CH:, :] = tile_of(in_two(sum_rows(dpre * normed), WIDE), WIDE).astype(BF16)
    back_ref[...] = woven(dpre)


def rows_of_128(value):
    return tile_of([value[:, k : k + 128] for k in range(0, value.shape[1], 128)], 128)


def to_plane(parts_ref, back_ref, out_ref):
    both = parts_ref[0].astype(F32) + parts_ref[1].astype(F32)
    pieces = both[:CH].astype(BF16).reshape(PLANES, 3, 8, WIDE)
    for k in range(3):
        out_ref[:, :, WIDE * k : WIDE * (k + 1)] = pieces[:, k]
    out_ref[:, :, 3 * WIDE : 4 * WIDE] = back_ref[...]
    sums = both[CH:] + pltpu.roll(both[CH:], 6, axis=0)
    tile = rows_of_128(row_of(sums, (0, 1))).astype(BF16)
    out_ref[:, :, 4 * WIDE :] = jnp.broadcast_to(tile[None], (PLANES, 8, 128))


def to_line(got_ref, proj_ref, out_ref):
    conv = [
        jnp.sum(got_ref[:, :, WIDE * k : WIDE * (k + 1)].astype(F32), axis=0) for k in range(3)
    ]
    proj = [proj_ref[:, MID * k : MID * (k + 1)] for k in range(3)]
    sums = jnp.sum(got_ref[:, :, 4 * WIDE :].astype(F32), axis=0)

    def own(core, tiles):
        upper = lax.broadcasted_iota(jnp.int32, tiles[0].shape, 0) < 4
        if core == 0:
            return tiles[0], tiles[1]
        return (
            jnp.where(upper, pltpu.roll(tiles[1], 4, axis=0), pltpu.roll(tiles[2], 4, axis=0)),
            pltpu.roll(tiles[2], 4, axis=0),
        )

    blank = jnp.zeros((8, WIDE - MID), F32)
    upper = lax.broadcasted_iota(jnp.int32, (8, WIDE), 0) < 4
    for core in range(2):
        conv_rows, conv_rest = own(core, conv)
        proj_rows, proj_rest = own(core, proj)
        proj_rest = jnp.concatenate([pltpu.roll(proj_rest, 4, axis=0), blank], axis=1)
        rest = jnp.where(upper, conv_rest, proj_rest)
        piece = jnp.concatenate([conv_rows, proj_rows, rest, sums], axis=1).astype(BF16)
        out_ref[core * BATCH : (core + 1) * BATCH] = jnp.broadcast_to(
            piece[None], (BATCH, 8, HALF + WIDE + 128)
        )


def last_rows(
    got_ref, plane_ref, x_ref, cot_ref, proj_ref, gain_ref, act_ref, stat_ref, out_ref, grad_ref, conv_ref, proj_grad_ref
):
    x = x_ref[...].astype(F32)
    update = matmul(act_ref[...], proj_ref[...], ((1,), (0,)))
    out_ref[...] = (x + update).astype(BF16)
    left, right = (
        jnp.sum(got_ref[BATCH * k : BATCH * (k + 1)].astype(F32), axis=0) for k in range(2)
    )
    first, second = (
        row_of(half[:, HALF + WIDE :], range(6)) * (1.0 / COUNTED) for half in (left, right)
    )
    spread = stat_ref[1:2, :]
    normed = (x - stat_ref[0:1, :]) / spread
    dpre = unwoven(plane_ref[:, :, 3 * WIDE : 4 * WIDE])
    change = flat(gain_ref) * (dpre - first - normed * second) / spread
    grad_ref[...] = (cot_ref[...].astype(F32) + change).astype(BF16)
    for k, half in enumerate((left, right)):
        conv_ref[0:8, WIDE * k : WIDE * (k + 1)] = half[:, :WIDE]
        conv_ref[8:12, WIDE * k : WIDE * (k + 1)] = half[:4, HALF : HALF + WIDE]
    both = left + right
    proj_grad_ref[0:8, :] = both[:, WIDE:HALF]
    proj_grad_ref[8:12, :] = both[4:8, HALF : HALF + MID]


def per_device(inputs, cotangent, conv_weight, proj_weight, gain_in, bias_in, gain_mid, bias_mid):
    x = inputs.reshape(ROWS, CH)
    cot = cotangent.reshape(ROWS, CH)
    rows, rows_mid = (ROWS, CH), (ROWS, MID)

    far, near = pl.BlockSpec(memory_space=pltpu.HBM), pl.BlockSpec(memory_space=pltpu.VMEM)
    sums, data, far_cot = pl.pallas_call(
        opening,
        out_shape=(
            jax.ShapeDtypeStruct((LINES, 1, 2 * CH), F32),
            jax.ShapeDtypeStruct((PLANES, 8, WIDE), BF16),
            jax.ShapeDtypeStruct((PLANES, 8, WIDE), BF16),
        ),
        in_specs=[far] * 2,
        out_specs=(near,) * 3,
        scratch_shapes=[
            pltpu.VMEM(rows, BF16),
            pltpu.VMEM(rows, BF16),
            pltpu.SemaphoreType.DMA((2,)),
        ],
        name="opening",
        compiler_params=pltpu.CompilerParams(vmem_limit_bytes=24 << 20),
    )(*(pltpu.with_memory_space_constraint(v, pltpu.HBM) for v in (x, cot)))
    sums = exchange(sums, LINE)
    (both,) = kernel(spread_all, ((PLANES, 8, 2 * WIDE), BF16), name="spread_all")(
        data, near=(sums,)
    )
    both = exchange(both, PLANE)

    act_in, far_x, conv, both, stat_in = kernel(
        forward_conv,
        (rows, BF16),
        (rows, BF16),
        (rows_mid, F32),
        ((PLANES, 8, WIDE + 128), BF16),
        ((8, CH), F32),
        name="forward_conv",
    )(far_cot, near=(both, conv_weight, gain_in, bias_in))
    both = exchange(both, PLANE)
    (sums,) = kernel(middle_line, ((LINES, 1, 2 * MID), F32), name="middle_line")(near=(both,))
    sums = exchange(sums, LINE)

    data, normed_mid, dpre_mid, sums, spread_mid = kernel(
        middle,
        ((PLANES, 8, 128 + CH), BF16),
        (rows_mid, F32),
        (rows_mid, F32),
        ((LINES, 1, 2 * MID), F32),
        ((8, MID), F32),
        name="middle",
    )(conv, near=(sums, both, gain_mid, bias_mid, proj_weight))
    sums = exchange(sums, LINE)
    (both,) = kernel(middle_plane, ((PLANES, 8, CH + 256), BF16), name="middle_plane")(
        data, near=(sums,)
    )
    both = exchange(both, PLANE)

    parts, act_mid, proj_part, back = kernel(
        filter_parts,
        ((2, CH + 8, WIDE), BF16),
        (rows_mid, BF16),
        ((8, CH), F32),
        ((PLANES, 8, WIDE), BF16),
        name="filter_parts",
    )(
        dpre_mid,
        normed_mid,
        spread_mid,
        act_in,
        far_x,
        stat_in,
        near=(both, gain_mid, conv_weight, gain_in, bias_in),
    )
    parts = exchange(parts, "core")
    (plane,) = kernel(to_plane, ((PLANES, 8, 4 * WIDE + 128), BF16), name="to_plane")(
        back, near=(parts,)
    )
    plane = exchange(plane, PLANE)
    (line,) = kernel(to_line, ((LINES, 8, HALF + WIDE + 128), BF16), name="to_line")(
        proj_part, near=(plane,)
    )
    line = exchange(line, LINE)
    block_out, input_grad, conv_grad, proj_grad = kernel(
        last_rows, (rows, BF16), (rows, BF16), ((12, CH), F32), ((12, MID), F32), name="last_rows"
    )(act_mid, stat_in, near=(line, plane, x, cot, proj_weight, gain_in))
    return (
        block_out.reshape(inputs.shape),
        input_grad.reshape(inputs.shape),
        conv_grad,
        proj_grad,
    )


def solution(mesh):
    split = Mesh(mesh.devices.reshape(4, 2, 4, 2, 8), ("x", "z_hi", "z_lo", "core", "dp"))
    rows = P("dp", SEQ, None)
    return jax.shard_map(
        per_device,
        mesh=split,
        in_specs=(rows, rows, P(), P(), P(), P(), P(), P()),
        out_specs=(rows, rows, P(SEQ, None), P(SEQ, None)),
        check_vma=False,
    )
```

time: 153 us -> 157 us (1.026)
  the two profiles are of different devices: /device:TPU:8 before, /device:TPU:72 now
where the time goes in v7:
time: 157 us; the launch traced here: 156 us
  blocking collectives  150 us (96%)
  Pallas kernels  5.1 us (3%)
    all_to_all x9, blocking collectives, exchange(): return lax.all_to_all(pieces, axes, split_axis=0, concat_axis=0, tiled=True)  150 us
    pallas_call x9, Pallas kernels, call(): pl.pallas_call(body, out_shape=shapes, in_specs=[whole] * len(args), out_...  3.87 us

profile of v7, /device:TPU:72, one launch (start us, length us, event | category | flops | bytes accessed | tf_op | source)
XLA Modules:
  0.0 156.1 jit_solution(4783033061961395620)
XLA Ops:
  0.6 0.0 copy-start.4
  0.6 0.0 copy-start.5
  0.7 0.0 copy-start
  0.7 1.2 opening.1
  1.9 14.9 %all_to_all.45.sums_ref = f32[16,1,1536]{2,1,0:T(1,128)S(1)} all-to-all(f32[16,1,1536]{2,1,0:T(1,128)S(1)} %get-tuple-element.25), channel_id=1, replica_groups=mesh['x'=4,'z_hi'=2,'z_lo'=4,'core'=2,'dp'=8] {'core','dp'}, dimensions={0} | all-to-all | bytes 196608 | tf_op jit(solution)/shard_map/all_to_all | solution.py:24
  16.8 0.1 spread_all.1
  16.9 27.1 %all_to_all.46.got_ref = bf16[32,8,768]{2,1,0:T(8,128)(2,1)S(1)} all-to-all(bf16[32,8,768]{2,1,0:T(8,128)(2,1)S(1)} %spread_all.1), channel_id=1, replica_groups=mesh['x'=4,'z_hi'=2,'z_lo'=4,'core'=2,'dp'=8] {'x','z_hi','z_lo'}, dimensions={0} | all-to-all | bytes 786432 | tf_op jit(solution)/shard_map/all_to_all | solution.py:24
  44.1 0.0 copy-done.4
  44.1 0.0 copy-done.5
  44.1 0.0 copy-done
  44.1 0.0 copy-start.1
  44.1 0.0 copy-start.6
  44.1 0.0 copy-start.7
  44.1 0.7 forward_conv.1
  44.8 16.2 %all_to_all.47.got_ref.plane_ref = bf16[32,8,512]{2,1,0:T(8,128)(2,1)S(1)} all-to-all(bf16[32,8,512]{2,1,0:T(8,128)(2,1)S(1)} %get-tuple-element.28), channel_id=1, replica_groups=mesh['x'=4,'z_hi'=2,'z_lo'=4,'core'=2,'dp'=8] {'x','z_hi','z_lo'}, dimensions={0} | all-to-all | bytes 524288 | tf_op jit(solution)/shard_map/all_to_all | solution.py:24
  61.0 0.1 middle_line.1
  61.1 10.4 %all_to_all.48.got_ref = f32[16,1,512]{2,1,0:T(1,128)S(1)} all-to-all(f32[16,1,512]{2,1,0:T(1,128)S(1)} %middle_line.1), channel_id=1, replica_groups=mesh['x'=4,'z_hi'=2,'z_lo'=4,'core'=2,'dp'=8] {'core','dp'}, dimensions={0} | all-to-all | bytes 65536 | tf_op jit(solution)/shard_map/all_to_all | solution.py:24
  71.5 0.0 copy-done.1
  71.5 0.0 copy-done.6
  71.5 0.0 copy-done.7
  71.5 0.5 middle.1
  72.0 10.2 %all_to_all.49.sums_ref = f32[16,1,512]{2,1,0:T(1,128)S(1)} all-to-all(f32[16,1,512]{2,1,0:T(1,128)S(1)} %get-tuple-element.30), channel_id=1, replica_groups=mesh['x'=4,'z_hi'=2,'z_lo'=4,'core'=2,'dp'=8] {'core','dp'}, dimensions={0} | all-to-all | bytes 65536 | tf_op jit(solution)/shard_map/all_to_all | solution.py:24
  82.2 0.1 middle_plane.1
  82.3 22.1 %all_to_all.50.got_ref = bf16[32,8,1024]{2,1,0:T(8,128)(2,1)S(1)} all-to-all(bf16[32,8,1024]{2,1,0:T(8,128)(2,1)S(1)} %middle_plane.1), channel_id=1, replica_groups=mesh['x'=4,'z_hi'=2,'z_lo'=4,'core'=2,'dp'=8] {'x','z_hi','z_lo'}, dimensions={0} | all-to-all | bytes 1048576 | tf_op jit(solution)/shard_map/all_to_all | solution.py:24
  104.4 1.1 filter_parts.1
  105.5 4.7 %all_to_all.51.parts_ref = bf16[2,776,384]{2,1,0:T(8,128)(2,1)S(1)} all-to-all(bf16[2,776,384]{2,1,0:T(8,128)(2,1)S(1)} %get-tuple-element.38), channel_id=1, replica_groups=mesh['x'=4,'z_hi'=2,'z_lo'=4,'core'=2,'dp'=8] {'core'}, dimensions={0} | all-to-all | bytes 2383872 | tf_op jit(solution)/shard_map/all_to_all | solution.py:24
  110.1 0.2 to_plane.1
  110.3 29.3 %all_to_all.52.got_ref.plane_ref = bf16[32,8,1664]{2,1,0:T(8,128)(2,1)S(1)} all-to-all(bf16[32,8,1664]{2,1,0:T(8,128)(2,1)S(1)} %to_plane.1), channel_id=1, replica_groups=mesh['x'=4,'z_hi'=2,'z_lo'=4,'core'=2,'dp'=8] {'x','z_hi','z_lo'}, dimensions={0} | all-to-all | bytes 1703936 | tf_op jit(solution)/shard_map/all_to_all | solution.py:24
  139.6 0.0 copy-start.2
  139.6 0.0 copy-start.3
  139.6 0.1 to_line.1
  139.7 15.2 %all_to_all.53.got_ref = bf16[16,8,1152]{2,1,0:T(8,128)(2,1)S(1)} all-to-all(bf16[16,8,1152]{2,1,0:T(8,128)(2,1)S(1)} %to_line.1), channel_id=1, replica_groups=mesh['x'=4,'z_hi'=2,'z_lo'=4,'core'=2,'dp'=8] {'core','dp'}, dimensions={0} | all-to-all | bytes 589824 | tf_op jit(solution)/shard_map/all_to_all | solution.py:24
  155.0 0.0 copy-done.2
  155.0 0.0 copy-done.3
  155.0 1.1 last_rows.1
Async XLA Ops:
  0.6 43.4 %copy-start.4 = (f32[768]{0:T(1024)S(1)}, f32[768]{0:T(1024)}, u32[]{:S(2)}) copy-start(f32[768]{0:T(1024)} %gain_ref.7) | copy-start | bytes 9220
  0.6 43.4 %copy-start.5 = (f32[768]{0:T(1024)S(1)}, f32[768]{0:T(1024)}, u32[]{:S(2)}) copy-start(f32[768]{0:T(1024)} %bias_in_ref.1) | copy-start | bytes 9220
  0.7 43.4 %copy-start = (bf16[768,768]{1,0:T(8,128)(2,1)S(1)}, bf16[768,768]{1,0:T(8,128)(2,1)}, u32[]{:S(2)}) copy-start(bf16[768,768]{1,0:T(8,128)(2,1)} %weight_ref.3) | copy-start | bytes 3538948
  44.1 27.4 %copy-start.1 = (bf16[256,768]{1,0:T(8,128)(2,1)S(1)}, bf16[256,768]{1,0:T(8,128)(2,1)}, u32[]{:S(2)}) copy-start(bf16[256,768]{1,0:T(8,128)(2,1)} %proj_ref.3) | copy-start | bytes 1179652
  44.1 27.4 %copy-start.6 = (f32[256]{0:T(256)S(1)}, f32[256]{0:T(256)}, u32[]{:S(2)}) copy-start(f32[256]{0:T(256)} %gain_ref.6) | copy-start | bytes 3076
  44.1 27.4 %copy-start.7 = (f32[256]{0:T(256)S(1)}, f32[256]{0:T(256)}, u32[]{:S(2)}) copy-start(f32[256]{0:T(256)} %bias_ref.3) | copy-start | bytes 3076
  139.6 15.4 %copy-start.2 = (bf16[1,128,768]{2,1,0:T(8,128)(2,1)S(1)}, bf16[1,128,768]{2,1,0:T(8,128)(2,1)}, u32[]{:S(2)}) copy-start(bf16[1,128,768]{2,1,0:T(8,128)(2,1)} %param.8) | copy-start | bytes 589828
  139.6 15.4 %copy-start.3 = (bf16[1,128,768]{2,1,0:T(8,128)(2,1)S(1)}, bf16[1,128,768]{2,1,0:T(8,128)(2,1)}, u32[]{:S(2)}) copy-start(bf16[1,128,768]{2,1,0:T(8,128)(2,1)} %param.9) | copy-start | bytes 589828

commit v8 on v6

--- a/solution.py
+++ b/solution.py
@@ -10,13 +10,11 @@
 
 SEQ = ("x", "z_hi", "z_lo", "core")
 PLANE = ("x", "z_hi", "z_lo")
-DEPTH = ("z_hi", "z_lo")
 LINE = ("core", "dp")
 BF16, F32 = jnp.bfloat16, jnp.float32
 CH, MID = 768, 256
 ROWS, SHIFT = 128, 16
 PLANES, LINES, BATCH = 32, 16, 8
-ACROSS, DEEP = 4, 8
 HALF = 512
 COUNTED = 8.0 * 8192.0
 COEFF = math.sqrt(2.0 / math.pi)
@@ -261,7 +259,7 @@
     back_ref[...] = woven(dpre)
 
 
-def to_plane(parts_ref, back_ref, out_ref):
+def to_plane(parts_ref, back_ref, out_hbm, out_ref, sem):
     both = parts_ref[0].astype(F32) + parts_ref[1].astype(F32)
     pieces = both[:CH].astype(BF16).reshape(PLANES, 3, 8, HALF)
     for k in range(3):
@@ -271,24 +269,16 @@
     sums = from_four(both[CH:])
     tile = tile_of([sums[:, k : k + 128] for k in range(0, CH, 128)], 128).astype(BF16)
     out_ref[:, :, begin:] = jnp.broadcast_to(tile[None], (PLANES, 8, 128))
-
-
-def to_depth(got_ref, out_ref):
-    sums = jnp.sum(got_ref[:, :, :, : 3 * HALF].astype(F32), axis=0)
-    out_ref[:, :, : 3 * HALF] = sums.astype(BF16)
-    begin = 3 * HALF + CH // 2
-    for k in range(ACROSS):
-        lanes = slice(3 * HALF + k * CH // 2, 3 * HALF + (k + 1) * CH // 2)
-        out_ref[:, :, lanes] = got_ref[k, :, :, 3 * HALF : begin]
-    sums = jnp.sum(got_ref[:, :, :, begin:].astype(F32), axis=0)
-    out_ref[:, :, 3 * HALF + 2 * CH :] = sums.astype(BF16)
+    store = pltpu.make_async_copy(out_ref, out_hbm, sem)
+    store.start()
+    store.wait()
 
 
 def to_line(got_ref, out_ref):
     tiles = [
         jnp.sum(got_ref[:, :, HALF * k : HALF * (k + 1)].astype(F32), axis=0) for k in range(3)
     ]
-    sums = jnp.sum(got_ref[:, :, 3 * HALF + 2 * CH :].astype(F32), axis=0)
+    sums = jnp.sum(got_ref[:, :, 3 * HALF + CH // 2 :].astype(F32), axis=0)
     low = pltpu.roll(in_four(row_of(sums, range(6))), 4, axis=0)
     upper = lax.broadcasted_iota(jnp.int32, (8, HALF), 0) < 4
     turned = [pltpu.roll(tile, 4, axis=0) for tile in tiles]
@@ -304,7 +294,7 @@
 
 
 def last_rows(
-    got_ref, depth_ref, x_ref, cot_ref, proj_ref, gain_ref, act_ref, stat_ref, out_ref, grad_ref, conv_ref, proj_grad_ref
+    got_ref, plane_ref, x_ref, cot_ref, proj_ref, gain_ref, act_ref, stat_ref, out_ref, grad_ref, conv_ref, proj_grad_ref
 ):
     x = x_ref[...].astype(F32)
     update = matmul(act_ref[...], proj_ref[...], ((1,), (0,)))
@@ -315,8 +305,7 @@
     first, second = (from_four(half[4:8, HALF:]) * (1.0 / COUNTED) for half in (left, right))
     spread = stat_ref[1:2, :]
     normed = (x - stat_ref[0:1, :]) / spread
-    begins = range(3 * HALF, 3 * HALF + 2 * CH, CH // 2)
-    dpre = unwoven(jnp.concatenate([depth_ref[:, :, k : k + CH // 2] for k in begins], axis=0))
+    dpre = unwoven(plane_ref[:, :, 3 * HALF : 3 * HALF + CH // 2])
     change = flat(gain_ref) * (dpre - first - normed * second) / spread
     grad_ref[...] = (cot_ref[...].astype(F32) + change).astype(BF16)
     for rows, lanes, count in ((slice(0, 8), 0, 8), (slice(8, 12), HALF, 4)):
@@ -399,19 +388,22 @@
         near=(both, gain_mid, cot, conv_weight, gain_in, bias_in),
     )
     parts = exchange(parts, "core")
-    (plane,) = kernel(to_plane, ((PLANES, 8, 3 * HALF + CH // 2 + 128), BF16), name="to_plane")(
-        back, near=(parts,)
-    )
-    plane = exchange(plane.reshape(ACROSS, DEEP, *plane.shape[1:]), "x")
-    (depth,) = kernel(to_depth, ((DEEP, 8, 3 * HALF + 2 * CH + 128), BF16), name="to_depth")(
-        near=(plane,)
-    )
-    depth = exchange(depth, DEPTH)
-    (line,) = kernel(to_line, ((LINES, 8, 2 * HALF), BF16), name="to_line")(near=(depth,))
+    shape = (PLANES, 8, 3 * HALF + CH // 2 + 128)
+    plane = pl.pallas_call(
+        to_plane,
+        out_shape=pltpu.HBM(shape, BF16),
+        in_specs=[near] * 2,
+        out_specs=far,
+        scratch_shapes=[pltpu.VMEM(shape, BF16), pltpu.SemaphoreType.DMA],
+        name="to_plane",
+        compiler_params=pltpu.CompilerParams(vmem_limit_bytes=24 << 20),
+    )(pltpu.with_memory_space_constraint(parts, pltpu.VMEM), back)
+    plane = exchange(plane, PLANE)
+    (line,) = kernel(to_line, ((LINES, 8, 2 * HALF), BF16), name="to_line")(near=(plane,))
     line = exchange(line, LINE)
     block_out, input_grad, conv_grad, proj_grad = kernel(
         last_rows, (rows, BF16), (rows, BF16), ((12, CH), F32), ((12, MID), F32), name="last_rows"
-    )(act_mid, stat_in, near=(line, depth, x, cot, proj_weight, gain_in))
+    )(act_mid, stat_in, near=(line, plane, x, cot, proj_weight, gain_in))
     return (
         block_out.reshape(inputs.shape),
         input_grad.reshape(inputs.shape),

time: 153 us -> 152 us (level)
  blocking collectives: 146 us -> 144 us
    all_to_all x10 -> x9, blocking collectives: 146 us -> 144 us  [exchange(): return lax.all_to_all(pieces, axes, split_axis=0, concat_axis=0, tiled=True)]
    pallas_call x10 -> x8, Pallas kernels: 3.73 us -> 3.52 us  [call(): pl.pallas_call(body, out_shape=shapes, in_specs=[whole] * len(args), out_...]
where the time goes in v8:
time: 152 us
  blocking collectives  144 us (95%)
  Pallas kernels  6.31 us (4%)
    all_to_all x9, blocking collectives, exchange(): return lax.all_to_all(pieces, axes, split_axis=0, concat_axis=0, tiled=True)  144 us
    pallas_call x8, Pallas kernels, call(): pl.pallas_call(body, out_shape=shapes, in_specs=[whole] * len(args), out_...  3.52 us

profile of v8, /device:TPU:8, one launch (start us, length us, event | category | flops | bytes accessed | tf_op | source)
XLA Modules:
  0.0 151.5 jit_solution(2465437957985526432)
XLA Ops:
  0.6 0.0 copy-start.4
  0.6 0.0 copy-start.5
  0.7 0.0 copy-start
  0.7 1.6 %opening.1 = (f32[16,1,1536]{2,1,0:T(1,128)S(1)}, bf16[32,8,384]{2,1,0:T(8,128)(2,1)S(1)}, bf16[32,8,128]{2,1,0:T(8,128)(2,1)S(1)}) custom-call(bf16[128,768]{1,0:T(8,128)(2,1)} %bitcast.7, bf16[128,768]{1,0:T(8,128)(2,1)} %bitcast.4, bf16[256,768]{1,0:T(8,128)(2,1)} %proj_ref.1), custom_call_target="tpu_custom_call" | custom-call | tf_op jit(solution)/shard_map/opening/pallas_call | solution.py:323
  2.3 15.8 %all_to_all.45.sums_ref = f32[16,1,1536]{2,1,0:T(1,128)S(1)} all-to-all(f32[16,1,1536]{2,1,0:T(1,128)S(1)} %get-tuple-element.24), channel_id=1, replica_groups=mesh['x'=4,'z_hi'=2,'z_lo'=4,'core'=2,'dp'=8] {'core','dp'}, dimensions={0} | all-to-all | bytes 196608 | tf_op jit(solution)/shard_map/all_to_all | solution.py:24
  18.1 0.1 spread_all.1
  18.2 0.0 copy-start.6
  18.2 0.0 copy-start.7
  18.2 26.4 %all_to_all.46.got_ref = bf16[32,8,768]{2,1,0:T(8,128)(2,1)S(1)} all-to-all(bf16[32,8,768]{2,1,0:T(8,128)(2,1)S(1)} %spread_all.1), channel_id=1, replica_groups=mesh['x'=4,'z_hi'=2,'z_lo'=4,'core'=2,'dp'=8] {'x','z_hi','z_lo'}, dimensions={0} | all-to-all | bytes 786432 | tf_op jit(solution)/shard_map/all_to_all | solution.py:24
  44.7 0.0 copy-start.1
  44.7 0.0 copy-done.4
  44.7 0.0 copy-done.5
  44.7 0.0 copy-done
  44.7 0.7 forward_conv.1
  45.4 15.3 %all_to_all.47.got_ref.plane_ref = bf16[32,8,256]{2,1,0:T(8,128)(2,1)S(1)} all-to-all(bf16[32,8,256]{2,1,0:T(8,128)(2,1)S(1)} %get-tuple-element.27), channel_id=1, replica_groups=mesh['x'=4,'z_hi'=2,'z_lo'=4,'core'=2,'dp'=8] {'x','z_hi','z_lo'}, dimensions={0} | all-to-all | bytes 262144 | tf_op jit(solution)/shard_map/all_to_all | solution.py:24
  60.7 0.1 middle_line.1
  60.8 10.0 %all_to_all.48.got_ref = f32[16,1,512]{2,1,0:T(1,128)S(1)} all-to-all(f32[16,1,512]{2,1,0:T(1,128)S(1)} %middle_line.1), channel_id=1, replica_groups=mesh['x'=4,'z_hi'=2,'z_lo'=4,'core'=2,'dp'=8] {'core','dp'}, dimensions={0} | all-to-all | bytes 65536 | tf_op jit(solution)/shard_map/all_to_all | solution.py:24
  70.8 0.0 copy-done.6
  70.8 0.0 copy-done.7
  70.8 0.2 middle.1
  71.1 10.2 %all_to_all.49.sums_ref = f32[16,1,512]{2,1,0:T(1,128)S(1)} all-to-all(f32[16,1,512]{2,1,0:T(1,128)S(1)} %get-tuple-element.29), channel_id=1, replica_groups=mesh['x'=4,'z_hi'=2,'z_lo'=4,'core'=2,'dp'=8] {'core','dp'}, dimensions={0} | all-to-all | bytes 65536 | tf_op jit(solution)/shard_map/all_to_all | solution.py:24
  81.3 0.1 middle_plane.1
  81.3 13.8 %all_to_all.50.got_ref = bf16[32,8,256]{2,1,0:T(8,128)(2,1)S(1)} all-to-all(bf16[32,8,256]{2,1,0:T(8,128)(2,1)S(1)} %middle_plane.1), channel_id=1, replica_groups=mesh['x'=4,'z_hi'=2,'z_lo'=4,'core'=2,'dp'=8] {'x','z_hi','z_lo'}, dimensions={0} | all-to-all | bytes 262144 | tf_op jit(solution)/shard_map/all_to_all | solution.py:24
  95.2 0.0 copy-done.1
  95.2 1.1 filter_parts.1
  96.3 5.0 %all_to_all.51.parts_ref = bf16[2,776,512]{2,1,0:T(8,128)(2,1)S(1)} all-to-all(bf16[2,776,512]{2,1,0:T(8,128)(2,1)S(1)} %get-tuple-element.37), channel_id=1, replica_groups=mesh['x'=4,'z_hi'=2,'z_lo'=4,'core'=2,'dp'=8] {'core'}, dimensions={0} | all-to-all | bytes 3178496 | tf_op jit(solution)/shard_map/all_to_all | solution.py:24
  101.3 1.2 to_plane.1
  102.5 0.0 copy-start.2
  102.5 0.0 copy-start.3
  102.5 33.2 %all_to_all.52.got_ref.plane_ref = bf16[32,8,2048]{2,1,0:T(8,128)(2,1)S(1)} all-to-all(bf16[32,8,2048]{2,1,0:T(8,128)(2,1)} %to_plane.1), channel_id=1, replica_groups=mesh['x'=4,'z_hi'=2,'z_lo'=4,'core'=2,'dp'=8] {'x','z_hi','z_lo'}, dimensions={0} | all-to-all | bytes 2097152 | tf_op jit(solution)/shard_map/all_to_all | solution.py:24
  135.7 0.1 to_line.1
  135.9 14.6 %all_to_all.53.got_ref = bf16[16,8,1024]{2,1,0:T(8,128)(2,1)S(1)} all-to-all(bf16[16,8,1024]{2,1,0:T(8,128)(2,1)S(1)} %to_line.1), channel_id=1, replica_groups=mesh['x'=4,'z_hi'=2,'z_lo'=4,'core'=2,'dp'=8] {'core','dp'}, dimensions={0} | all-to-all | bytes 524288 | tf_op jit(solution)/shard_map/all_to_all | solution.py:24
  150.4 0.0 copy-done.2
  150.5 0.0 copy-done.3
  150.5 1.1 last_rows.1
Async XLA Ops:
  0.6 44.1 %copy-start.4 = (f32[768]{0:T(1024)S(1)}, f32[768]{0:T(1024)}, u32[]{:S(2)}) copy-start(f32[768]{0:T(1024)} %gain_ref.7) | copy-start | bytes 9220
  0.6 44.0 %copy-start.5 = (f32[768]{0:T(1024)S(1)}, f32[768]{0:T(1024)}, u32[]{:S(2)}) copy-start(f32[768]{0:T(1024)} %bias_in_ref.1) | copy-start | bytes 9220
  0.7 44.0 %copy-start = (bf16[768,768]{1,0:T(8,128)(2,1)S(1)}, bf16[768,768]{1,0:T(8,128)(2,1)}, u32[]{:S(2)}) copy-start(bf16[768,768]{1,0:T(8,128)(2,1)} %weight_ref.3) | copy-start | bytes 3538948
  18.2 52.6 %copy-start.6 = (f32[256]{0:T(256)S(1)}, f32[256]{0:T(256)}, u32[]{:S(2)}) copy-start(f32[256]{0:T(256)} %gain_ref.6) | copy-start | bytes 3076
  18.2 52.6 %copy-start.7 = (f32[256]{0:T(256)S(1)}, f32[256]{0:T(256)}, u32[]{:S(2)}) copy-start(f32[256]{0:T(256)} %bias_ref.3) | copy-start | bytes 3076
  44.7 50.5 %copy-start.1 = (bf16[1,128,768]{2,1,0:T(8,128)(2,1)S(1)}, bf16[1,128,768]{2,1,0:T(8,128)(2,1)}, u32[]{:S(2)}) copy-start(bf16[1,128,768]{2,1,0:T(8,128)(2,1)} %param.9) | copy-start | bytes 589828
  102.5 48.0 %copy-start.2 = (bf16[256,768]{1,0:T(8,128)(2,1)S(1)}, bf16[256,768]{1,0:T(8,128)(2,1)}, u32[]{:S(2)}) copy-start(bf16[256,768]{1,0:T(8,128)(2,1)} %proj_ref.1) | copy-start | bytes 1179652
  102.5 48.0 %copy-start.3 = (bf16[1,128,768]{2,1,0:T(8,128)(2,1)S(1)}, bf16[1,128,768]{2,1,0:T(8,128)(2,1)}, u32[]{:S(2)}) copy-start(bf16[1,128,768]{2,1,0:T(8,128)(2,1)} %param.8) | copy-start | bytes 589828

commit v9 on v8

--- a/solution.py
+++ b/solution.py
@@ -259,7 +259,7 @@
     back_ref[...] = woven(dpre)
 
 
-def to_plane(parts_ref, back_ref, out_hbm, out_ref, sem):
+def to_plane(parts_ref, back_ref, out_ref):
     both = parts_ref[0].astype(F32) + parts_ref[1].astype(F32)
     pieces = both[:CH].astype(BF16).reshape(PLANES, 3, 8, HALF)
     for k in range(3):
@@ -269,9 +269,6 @@
     sums = from_four(both[CH:])
     tile = tile_of([sums[:, k : k + 128] for k in range(0, CH, 128)], 128).astype(BF16)
     out_ref[:, :, begin:] = jnp.broadcast_to(tile[None], (PLANES, 8, 128))
-    store = pltpu.make_async_copy(out_ref, out_hbm, sem)
-    store.start()
-    store.wait()
 
 
 def to_line(got_ref, out_ref):
@@ -294,24 +291,47 @@
 
 
 def last_rows(
-    got_ref, plane_ref, x_ref, cot_ref, proj_ref, gain_ref, act_ref, stat_ref, out_ref, grad_ref, conv_ref, proj_grad_ref
+    got_ref,
+    plane_ref,
+    x_ref,
+    cot_ref,
+    proj_ref,
+    gain_ref,
+    act_ref,
+    stat_ref,
+    out_hbm,
+    grad_hbm,
+    conv_hbm,
+    proj_hbm,
+    out_ref,
+    grad_ref,
+    conv_ref,
+    proj_grad_ref,
+    sems,
 ):
-    x = x_ref[...].astype(F32)
+    pairs = ((out_ref, out_hbm), (conv_ref, conv_hbm), (proj_grad_ref, proj_hbm), (grad_ref, grad_hbm))
+    stores = [pltpu.make_async_copy(*pair, sems.at[k]) for k, pair in enumerate(pairs)]
     update = matmul(act_ref[...], proj_ref[...], ((1,), (0,)))
-    out_ref[...] = (x + update).astype(BF16)
+    out_ref[...] = (x_ref[...].astype(F32) + update).astype(BF16)
+    stores[0].start()
     left, right = (
         jnp.sum(got_ref[BATCH * k : BATCH * (k + 1)].astype(F32), axis=0) for k in range(2)
     )
-    first, second = (from_four(half[4:8, HALF:]) * (1.0 / COUNTED) for half in (left, right))
-    spread = stat_ref[1:2, :]
-    normed = (x - stat_ref[0:1, :]) / spread
-    dpre = unwoven(plane_ref[:, :, 3 * HALF : 3 * HALF + CH // 2])
-    change = flat(gain_ref) * (dpre - first - normed * second) / spread
-    grad_ref[...] = (cot_ref[...].astype(F32) + change).astype(BF16)
     for rows, lanes, count in ((slice(0, 8), 0, 8), (slice(8, 12), HALF, 4)):
         conv_ref[rows, :HALF] = left[:count, lanes : lanes + HALF]
         conv_ref[rows, HALF:] = right[:count, lanes : lanes + CH - HALF]
         proj_grad_ref[rows, :] = right[:count, lanes + CH - HALF : lanes + HALF]
+    stores[1].start()
+    stores[2].start()
+    first, second = (from_four(half[4:8, HALF:]) * (1.0 / COUNTED) for half in (left, right))
+    spread = stat_ref[1:2, :]
+    normed = (x_ref[...].astype(F32) - stat_ref[0:1, :]) / spread
+    dpre = unwoven(plane_ref[:, :, 3 * HALF : 3 * HALF + CH // 2])
+    change = flat(gain_ref) * (dpre - first - normed * second) / spread
+    grad_ref[...] = (cot_ref[...].astype(F32) + change).astype(BF16)
+    stores[3].start()
+    for store in stores:
+        store.wait()
 
 
 def per_device(inputs, cotangent, conv_weight, proj_weight, gain_in, bias_in, gain_mid, bias_mid):
@@ -388,22 +408,23 @@
         near=(both, gain_mid, cot, conv_weight, gain_in, bias_in),
     )
     parts = exchange(parts, "core")
-    shape = (PLANES, 8, 3 * HALF + CH // 2 + 128)
-    plane = pl.pallas_call(
-        to_plane,
-        out_shape=pltpu.HBM(shape, BF16),
-        in_specs=[near] * 2,
-        out_specs=far,
-        scratch_shapes=[pltpu.VMEM(shape, BF16), pltpu.SemaphoreType.DMA],
-        name="to_plane",
-        compiler_params=pltpu.CompilerParams(vmem_limit_bytes=24 << 20),
-    )(pltpu.with_memory_space_constraint(parts, pltpu.VMEM), back)
+    (plane,) = kernel(to_plane, ((PLANES, 8, 3 * HALF + CH // 2 + 128), BF16), name="to_plane")(
+        back, near=(parts,)
+    )
     plane = exchange(plane, PLANE)
     (line,) = kernel(to_line, ((LINES, 8, 2 * HALF), BF16), name="to_line")(near=(plane,))
     line = exchange(line, LINE)
-    block_out, input_grad, conv_grad, proj_grad = kernel(
-        last_rows, (rows, BF16), (rows, BF16), ((12, CH), F32), ((12, MID), F32), name="last_rows"
-    )(act_mid, stat_in, near=(line, plane, x, cot, proj_weight, gain_in))
+    ends = ((rows, BF16), (rows, BF16), ((12, CH), F32), ((12, MID), F32))
+    held = (line, plane, x, cot, proj_weight, gain_in)
+    block_out, input_grad, conv_grad, proj_grad = pl.pallas_call(
+        last_rows,
+        out_shape=tuple(pltpu.HBM(*end) for end in ends),
+        in_specs=[near] * 8,
+        out_specs=(far,) * 4,
+        scratch_shapes=[*(pltpu.VMEM(*end) for end in ends), pltpu.SemaphoreType.DMA((4,))],
+        name="last_rows",
+        compiler_params=pltpu.CompilerParams(vmem_limit_bytes=24 << 20),
+    )(*(pltpu.with_memory_space_constraint(v, pltpu.VMEM) for v in held), act_mid, stat_in)
     return (
         block_out.reshape(inputs.shape),
         input_grad.reshape(inputs.shape),

time: 152 us -> 150 us (0.987)
  no operation moved by 1% of the time
where the time goes in v9:
time: 150 us
  blocking collectives  144 us (96%)
  Pallas kernels  5.43 us (4%)
    all_to_all x9, blocking collectives, exchange(): return lax.all_to_all(pieces, axes, split_axis=0, concat_axis=0, tiled=True)  144 us

profile of v9, /device:TPU:8, one launch (start us, length us, event | category | flops | bytes accessed | tf_op | source)
XLA Modules:
  0.0 150.0 jit_solution(18308230198863579962)
XLA Ops:
  0.6 0.0 copy-start.4
  0.6 0.0 copy-start.5
  0.7 0.0 copy-start
  0.7 1.6 %opening.1 = (f32[16,1,1536]{2,1,0:T(1,128)S(1)}, bf16[32,8,384]{2,1,0:T(8,128)(2,1)S(1)}, bf16[32,8,128]{2,1,0:T(8,128)(2,1)S(1)}) custom-call(bf16[128,768]{1,0:T(8,128)(2,1)} %bitcast.7, bf16[128,768]{1,0:T(8,128)(2,1)} %bitcast.4, bf16[256,768]{1,0:T(8,128)(2,1)} %proj_ref.1), custom_call_target="tpu_custom_call" | custom-call | tf_op jit(solution)/shard_map/opening/pallas_call | solution.py:343
  2.3 15.8 %all_to_all.45.sums_ref = f32[16,1,1536]{2,1,0:T(1,128)S(1)} all-to-all(f32[16,1,1536]{2,1,0:T(1,128)S(1)} %get-tuple-element.24), channel_id=1, replica_groups=mesh['x'=4,'z_hi'=2,'z_lo'=4,'core'=2,'dp'=8] {'core','dp'}, dimensions={0} | all-to-all | bytes 196608 | tf_op jit(solution)/shard_map/all_to_all | solution.py:24
  18.1 0.1 spread_all.1
  18.2 0.0 copy-start.6
  18.2 0.0 copy-start.7
  18.2 26.4 %all_to_all.46.got_ref = bf16[32,8,768]{2,1,0:T(8,128)(2,1)S(1)} all-to-all(bf16[32,8,768]{2,1,0:T(8,128)(2,1)S(1)} %spread_all.1), channel_id=1, replica_groups=mesh['x'=4,'z_hi'=2,'z_lo'=4,'core'=2,'dp'=8] {'x','z_hi','z_lo'}, dimensions={0} | all-to-all | bytes 786432 | tf_op jit(solution)/shard_map/all_to_all | solution.py:24
  44.7 0.0 copy-start.1
  44.7 0.0 copy-done.4
  44.7 0.0 copy-done.5
  44.7 0.0 copy-done
  44.7 0.7 forward_conv.1
  45.4 15.3 %all_to_all.47.got_ref.plane_ref = bf16[32,8,256]{2,1,0:T(8,128)(2,1)S(1)} all-to-all(bf16[32,8,256]{2,1,0:T(8,128)(2,1)S(1)} %get-tuple-element.27), channel_id=1, replica_groups=mesh['x'=4,'z_hi'=2,'z_lo'=4,'core'=2,'dp'=8] {'x','z_hi','z_lo'}, dimensions={0} | all-to-all | bytes 262144 | tf_op jit(solution)/shard_map/all_to_all | solution.py:24
  60.7 0.1 middle_line.1
  60.8 10.0 %all_to_all.48.got_ref = f32[16,1,512]{2,1,0:T(1,128)S(1)} all-to-all(f32[16,1,512]{2,1,0:T(1,128)S(1)} %middle_line.1), channel_id=1, replica_groups=mesh['x'=4,'z_hi'=2,'z_lo'=4,'core'=2,'dp'=8] {'core','dp'}, dimensions={0} | all-to-all | bytes 65536 | tf_op jit(solution)/shard_map/all_to_all | solution.py:24
  70.8 0.0 copy-done.6
  70.8 0.0 copy-done.7
  70.8 0.2 middle.1
  71.1 10.2 %all_to_all.49.sums_ref = f32[16,1,512]{2,1,0:T(1,128)S(1)} all-to-all(f32[16,1,512]{2,1,0:T(1,128)S(1)} %get-tuple-element.29), channel_id=1, replica_groups=mesh['x'=4,'z_hi'=2,'z_lo'=4,'core'=2,'dp'=8] {'core','dp'}, dimensions={0} | all-to-all | bytes 65536 | tf_op jit(solution)/shard_map/all_to_all | solution.py:24
  81.3 0.1 middle_plane.1
  81.3 13.8 %all_to_all.50.got_ref = bf16[32,8,256]{2,1,0:T(8,128)(2,1)S(1)} all-to-all(bf16[32,8,256]{2,1,0:T(8,128)(2,1)S(1)} %middle_plane.1), channel_id=1, replica_groups=mesh['x'=4,'z_hi'=2,'z_lo'=4,'core'=2,'dp'=8] {'x','z_hi','z_lo'}, dimensions={0} | all-to-all | bytes 262144 | tf_op jit(solution)/shard_map/all_to_all | solution.py:24
  95.2 0.0 copy-done.1
  95.2 1.1 filter_parts.1
  96.3 5.0 %all_to_all.51.parts_ref = bf16[2,776,512]{2,1,0:T(8,128)(2,1)S(1)} all-to-all(bf16[2,776,512]{2,1,0:T(8,128)(2,1)S(1)} %get-tuple-element.37), channel_id=1, replica_groups=mesh['x'=4,'z_hi'=2,'z_lo'=4,'core'=2,'dp'=8] {'core'}, dimensions={0} | all-to-all | bytes 3178496 | tf_op jit(solution)/shard_map/all_to_all | solution.py:24
  101.3 0.2 to_plane.1
  101.5 0.0 copy-start.2
  101.5 0.0 copy-start.3
  101.5 32.7 %all_to_all.52.got_ref.plane_ref = bf16[32,8,2048]{2,1,0:T(8,128)(2,1)S(1)} all-to-all(bf16[32,8,2048]{2,1,0:T(8,128)(2,1)S(1)} %to_plane.1), channel_id=1, replica_groups=mesh['x'=4,'z_hi'=2,'z_lo'=4,'core'=2,'dp'=8] {'x','z_hi','z_lo'}, dimensions={0} | all-to-all | bytes 2097152 | tf_op jit(solution)/shard_map/all_to_all | solution.py:24
  134.2 0.1 to_line.1
  134.3 14.5 %all_to_all.53.got_ref = bf16[16,8,1024]{2,1,0:T(8,128)(2,1)S(1)} all-to-all(bf16[16,8,1024]{2,1,0:T(8,128)(2,1)S(1)} %to_line.1), channel_id=1, replica_groups=mesh['x'=4,'z_hi'=2,'z_lo'=4,'core'=2,'dp'=8] {'core','dp'}, dimensions={0} | all-to-all | bytes 524288 | tf_op jit(solution)/shard_map/all_to_all | solution.py:24
  148.8 0.0 copy-done.2
  148.8 0.0 copy-done.3
  148.8 1.2 last_rows.1
Async XLA Ops:
  0.6 44.1 %copy-start.4 = (f32[768]{0:T(1024)S(1)}, f32[768]{0:T(1024)}, u32[]{:S(2)}) copy-start(f32[768]{0:T(1024)} %gain_ref.7) | copy-start | bytes 9220
  0.6 44.0 %copy-start.5 = (f32[768]{0:T(1024)S(1)}, f32[768]{0:T(1024)}, u32[]{:S(2)}) copy-start(f32[768]{0:T(1024)} %bias_in_ref.1) | copy-start | bytes 9220
  0.7 44.0 %copy-start = (bf16[768,768]{1,0:T(8,128)(2,1)S(1)}, bf16[768,768]{1,0:T(8,128)(2,1)}, u32[]{:S(2)}) copy-start(bf16[768,768]{1,0:T(8,128)(2,1)} %weight_ref.3) | copy-start | bytes 3538948
  18.2 52.6 %copy-start.6 = (f32[256]{0:T(256)S(1)}, f32[256]{0:T(256)}, u32[]{:S(2)}) copy-start(f32[256]{0:T(256)} %gain_ref.6) | copy-start | bytes 3076
  18.2 52.6 %copy-start.7 = (f32[256]{0:T(256)S(1)}, f32[256]{0:T(256)}, u32[]{:S(2)}) copy-start(f32[256]{0:T(256)} %bias_ref.3) | copy-start | bytes 3076
  44.7 50.5 %copy-start.1 = (bf16[1,128,768]{2,1,0:T(8,128)(2,1)S(1)}, bf16[1,128,768]{2,1,0:T(8,128)(2,1)}, u32[]{:S(2)}) copy-start(bf16[1,128,768]{2,1,0:T(8,128)(2,1)} %param.9) | copy-start | bytes 589828
  101.5 47.3 %copy-start.2 = (bf16[256,768]{1,0:T(8,128)(2,1)S(1)}, bf16[256,768]{1,0:T(8,128)(2,1)}, u32[]{:S(2)}) copy-start(bf16[256,768]{1,0:T(8,128)(2,1)} %proj_ref.1) | copy-start | bytes 1179652
  101.5 47.3 %copy-start.3 = (bf16[1,128,768]{2,1,0:T(8,128)(2,1)S(1)}, bf16[1,128,768]{2,1,0:T(8,128)(2,1)}, u32[]{:S(2)}) copy-start(bf16[1,128,768]{2,1,0:T(8,128)(2,1)} %param.8) | copy-start | bytes 589828

commit v10 on v8

--- a/solution.py
+++ b/solution.py
@@ -234,7 +234,8 @@
     act_in_ref,
     x_ref,
     stat_ref,
-    parts_ref,
+    kept_ref,
+    sent_ref,
     act_ref,
     back_ref,
 ):
@@ -245,22 +246,29 @@
     dconv = flat(gain_ref) * dconv / spread_ref[0:1, :]
     stacked = jnp.concatenate([earlier(dconv), dconv, later(dconv)], axis=1).astype(BF16)
     conv_part = matmul(act_in_ref[...], stacked, ((0,), (0,)))
-    parts_ref[0, :CH, :] = conv_part[:, :HALF].astype(BF16)
-    parts_ref[1, :CH, : HALF - MID] = conv_part[:, HALF:].astype(BF16)
     act = unwoven(got_ref[:, :, :128]).astype(BF16)
     act_ref[...] = act
     proj_part = matmul(cot_ref[...], act, ((0,), (0,)))
-    parts_ref[1, :CH, HALF - MID :] = proj_part.astype(BF16)
     normed = (x_ref[...].astype(F32) - stat_ref[0:1, :]) / stat_ref[1:2, :]
     pre = flat(gain_in_ref) * normed + flat(bias_in_ref)
     dpre = matmul(stacked, weight_ref[...], ((1,), (1,))) * slope_of(pre, tanh_of(pre))
-    parts_ref[0, CH:, :] = in_four(sum_rows(dpre)).astype(BF16)
-    parts_ref[1, CH:, :] = in_four(sum_rows(dpre * normed)).astype(BF16)
+    sums = in_four(sum_rows(dpre)).astype(BF16), in_four(sum_rows(dpre * normed)).astype(BF16)
+
+    def place(left_ref, right_ref):
+        left_ref[:CH, :] = conv_part[:, :HALF].astype(BF16)
+        right_ref[:CH, : HALF - MID] = conv_part[:, HALF:].astype(BF16)
+        right_ref[:CH, HALF - MID :] = proj_part.astype(BF16)
+        left_ref[CH:, :] = sums[0]
+        right_ref[CH:, :] = sums[1]
+
+    core = lax.axis_index("core")
+    pl.when(core == 0)(lambda: place(kept_ref, sent_ref))
+    pl.when(core == 1)(lambda: place(sent_ref, kept_ref))
     back_ref[...] = woven(dpre)
 
 
-def to_plane(parts_ref, back_ref, out_hbm, out_ref, sem):
-    both = parts_ref[0].astype(F32) + parts_ref[1].astype(F32)
+def to_plane(got_ref, kept_ref, back_ref, out_ref):
+    both = kept_ref[...].astype(F32) + got_ref[...].astype(F32)
     pieces = both[:CH].astype(BF16).reshape(PLANES, 3, 8, HALF)
     for k in range(3):
         out_ref[:, :, HALF * k : HALF * (k + 1)] = pieces[:, k]
@@ -269,9 +277,6 @@
     sums = from_four(both[CH:])
     tile = tile_of([sums[:, k : k + 128] for k in range(0, CH, 128)], 128).astype(BF16)
     out_ref[:, :, begin:] = jnp.broadcast_to(tile[None], (PLANES, 8, 128))
-    store = pltpu.make_async_copy(out_ref, out_hbm, sem)
-    store.start()
-    store.wait()
 
 
 def to_line(got_ref, out_ref):
@@ -372,9 +377,10 @@
     )
     both = exchange(both, PLANE)
 
-    parts, act_mid, back = kernel(
+    kept, sent, act_mid, back = kernel(
         filter_parts,
-        ((2, CH + 8, HALF), BF16),
+        ((CH + 8, HALF), BF16),
+        ((CH + 8, HALF), BF16),
         (rows_mid, BF16),
         ((PLANES, 8, CH // 2), BF16),
         name="filter_parts",
@@ -387,17 +393,10 @@
         stat_in,
         near=(both, gain_mid, cot, conv_weight, gain_in, bias_in),
     )
-    parts = exchange(parts, "core")
-    shape = (PLANES, 8, 3 * HALF + CH // 2 + 128)
-    plane = pl.pallas_call(
-        to_plane,
-        out_shape=pltpu.HBM(shape, BF16),
-        in_specs=[near] * 2,
-        out_specs=far,
-        scratch_shapes=[pltpu.VMEM(shape, BF16), pltpu.SemaphoreType.DMA],
-        name="to_plane",
-        compiler_params=pltpu.CompilerParams(vmem_limit_bytes=24 << 20),
-    )(pltpu.with_memory_space_constraint(parts, pltpu.VMEM), back)
+    got = lax.ppermute(sent, "core", [(0, 1), (1, 0)])
+    (plane,) = kernel(to_plane, ((PLANES, 8, 3 * HALF + CH // 2 + 128), BF16), name="to_plane")(
+        kept, back, near=(got,)
+    )
     plane = exchange(plane, PLANE)
     (line,) = kernel(to_line, ((LINES, 8, 2 * HALF), BF16), name="to_line")(near=(plane,))
     line = exchange(line, LINE)

time: 152 us -> 150 us (0.987)
  blocking collectives: 144 us -> 139 us
  waiting for transfers between devices: 0 us -> 2.26 us
  starting transfers between devices: 0 us -> 1.92 us
    all_to_all x9 -> x8, blocking collectives: 144 us -> 139 us  [exchange(): return lax.all_to_all(pieces, axes, split_axis=0, concat_axis=0, tiled=True)]
    ppermute x0 -> x1, waiting for transfers between devices: none -> 2.26 us  [per_device(): got = lax.ppermute(sent, 'core', [(0, 1), (1, 0)])]
    ppermute x0 -> x1, starting transfers between devices: none -> 1.92 us  [per_device(): got = lax.ppermute(sent, 'core', [(0, 1), (1, 0)])]
    pallas_call x8 -> x9, Pallas kernels: 3.52 us -> 3.87 us  [call(): pl.pallas_call(body, out_shape=shapes, in_specs=[whole] * len(args), out_...]
  transfers between devices with their start and end apart: 0 -> 1, of which waited for: 0 -> 1; matrix products, arithmetic and copies ran while one was open for 0% -> 0% of each run, Pallas kernels for 0% -> 0%
where the time goes in v10:
time: 150 us; the launch traced here: 149 us
  blocking collectives  139 us (93%)
  Pallas kernels  5.47 us (4%)
  waiting for transfers between devices  2.26 us (2%)
  starting transfers between devices  1.92 us (1%)
    all_to_all x8, blocking collectives, exchange(): return lax.all_to_all(pieces, axes, split_axis=0, concat_axis=0, tiled=True)  139 us
    pallas_call x9, Pallas kernels, call(): pl.pallas_call(body, out_shape=shapes, in_specs=[whole] * len(args), out_...  3.87 us
  transfers between devices with their start and end apart: 1, of which 1 were waited for; matrix products, arithmetic and copies ran while one was open for 0% of the time, Pallas kernels for 0%

profile of v10, /device:TPU:8, one launch (start us, length us, event | category | flops | bytes accessed | tf_op | source)
XLA Modules:
  0.0 149.2 jit_solution(10308421476174511990)
XLA Ops:
  0.6 0.0 copy-start
  0.6 0.0 copy-start.4
  0.7 0.0 copy-start.5
  0.7 1.6 %opening.1 = (f32[16,1,1536]{2,1,0:T(1,128)S(1)}, bf16[32,8,384]{2,1,0:T(8,128)(2,1)S(1)}, bf16[32,8,128]{2,1,0:T(8,128)(2,1)S(1)}) custom-call(bf16[128,768]{1,0:T(8,128)(2,1)} %bitcast.7, bf16[128,768]{1,0:T(8,128)(2,1)} %bitcast.4, bf16[256,768]{1,0:T(8,128)(2,1)} %proj_ref.1), custom_call_target="tpu_custom_call" | custom-call | tf_op jit(solution)/shard_map/opening/pallas_call | solution.py:328
  2.3 15.8 %all_to_all.40.sums_ref = f32[16,1,1536]{2,1,0:T(1,128)S(1)} all-to-all(f32[16,1,1536]{2,1,0:T(1,128)S(1)} %get-tuple-element.25), channel_id=1, replica_groups=mesh['x'=4,'z_hi'=2,'z_lo'=4,'core'=2,'dp'=8] {'core','dp'}, dimensions={0} | all-to-all | bytes 196608 | tf_op jit(solution)/shard_map/all_to_all | solution.py:24
  18.1 0.1 spread_all.1
  18.2 26.4 %all_to_all.41.got_ref = bf16[32,8,768]{2,1,0:T(8,128)(2,1)S(1)} all-to-all(bf16[32,8,768]{2,1,0:T(8,128)(2,1)S(1)} %spread_all.1), channel_id=1, replica_groups=mesh['x'=4,'z_hi'=2,'z_lo'=4,'core'=2,'dp'=8] {'x','z_hi','z_lo'}, dimensions={0} | all-to-all | bytes 786432 | tf_op jit(solution)/shard_map/all_to_all | solution.py:24
  44.6 0.0 copy-start.6
  44.6 0.0 copy-start.7
  44.6 0.0 copy-done
  44.6 0.0 copy-done.4
  44.7 0.0 copy-done.5
  44.7 0.0 copy-start.1
  44.7 0.7 forward_conv.1
  45.4 15.3 %all_to_all.42.got_ref.plane_ref = bf16[32,8,256]{2,1,0:T(8,128)(2,1)S(1)} all-to-all(bf16[32,8,256]{2,1,0:T(8,128)(2,1)S(1)} %get-tuple-element.28), channel_id=1, replica_groups=mesh['x'=4,'z_hi'=2,'z_lo'=4,'core'=2,'dp'=8] {'x','z_hi','z_lo'}, dimensions={0} | all-to-all | bytes 262144 | tf_op jit(solution)/shard_map/all_to_all | solution.py:24
  60.7 0.1 middle_line.1
  60.8 10.0 %all_to_all.43.got_ref = f32[16,1,512]{2,1,0:T(1,128)S(1)} all-to-all(f32[16,1,512]{2,1,0:T(1,128)S(1)} %middle_line.1), channel_id=1, replica_groups=mesh['x'=4,'z_hi'=2,'z_lo'=4,'core'=2,'dp'=8] {'core','dp'}, dimensions={0} | all-to-all | bytes 65536 | tf_op jit(solution)/shard_map/all_to_all | solution.py:24
  70.8 0.0 copy-done.6
  70.8 0.0 copy-done.7
  70.8 0.2 middle.1
  71.0 10.2 %all_to_all.44.sums_ref = f32[16,1,512]{2,1,0:T(1,128)S(1)} all-to-all(f32[16,1,512]{2,1,0:T(1,128)S(1)} %get-tuple-element.30), channel_id=1, replica_groups=mesh['x'=4,'z_hi'=2,'z_lo'=4,'core'=2,'dp'=8] {'core','dp'}, dimensions={0} | all-to-all | bytes 65536 | tf_op jit(solution)/shard_map/all_to_all | solution.py:24
  81.2 0.1 middle_plane.1
  81.3 13.8 %all_to_all.45.got_ref = bf16[32,8,256]{2,1,0:T(8,128)(2,1)S(1)} all-to-all(bf16[32,8,256]{2,1,0:T(8,128)(2,1)S(1)} %middle_plane.1), channel_id=1, replica_groups=mesh['x'=4,'z_hi'=2,'z_lo'=4,'core'=2,'dp'=8] {'x','z_hi','z_lo'}, dimensions={0} | all-to-all | bytes 262144 | tf_op jit(solution)/shard_map/all_to_all | solution.py:24
  95.1 0.0 copy-done.1
  95.1 1.3 filter_parts.1
  96.4 1.9 %collective-permute-start = (bf16[776,512]{1,0:T(8,128)(2,1)S(1)}, bf16[776,512]{1,0:T(8,128)(2,1)S(1)}, u32[]{:S(2)}, u32[]{:S(2)}) collective-permute-start(bf16[776,512]{1,0:T(8,128)(2,1)S(1)} %get-tuple-element.38), channel_id=1, source_target_pairs={{0,8},{8,0},{1,9},{9,1},{2,10},{10,2},{3,11},{11,3},{4,12},{12,4},... | collective-permute-start | bytes 2383880 | tf_op jit(solution)/shard_map/ppermute | solution.py:396
  98.3 2.3 %collective-permute-done.got_ref = bf16[776,512]{1,0:T(8,128)(2,1)S(1)} collective-permute-done((bf16[776,512]{1,0:T(8,128)(2,1)S(1)}, bf16[776,512]{1,0:T(8,128)(2,1)S(1)}, u32[]{:S(2)}, u32[]{:S(2)}) %collective-permute-start) | collective-permute-done | bytes 794656 | tf_op jit(solution)/shard_map/ppermute | solution.py:396
  100.6 0.2 to_plane.1
  100.8 32.5 %all_to_all.46.got_ref.plane_ref = bf16[32,8,2048]{2,1,0:T(8,128)(2,1)S(1)} all-to-all(bf16[32,8,2048]{2,1,0:T(8,128)(2,1)S(1)} %to_plane.1), channel_id=1, replica_groups=mesh['x'=4,'z_hi'=2,'z_lo'=4,'core'=2,'dp'=8] {'x','z_hi','z_lo'}, dimensions={0} | all-to-all | bytes 2097152 | tf_op jit(solution)/shard_map/all_to_all | solution.py:24
  133.4 0.0 copy-start.2
  133.4 0.0 copy-start.3
  133.4 0.1 to_line.1
  133.5 14.6 %all_to_all.47.got_ref = bf16[16,8,1024]{2,1,0:T(8,128)(2,1)S(1)} all-to-all(bf16[16,8,1024]{2,1,0:T(8,128)(2,1)S(1)} %to_line.1), channel_id=1, replica_groups=mesh['x'=4,'z_hi'=2,'z_lo'=4,'core'=2,'dp'=8] {'core','dp'}, dimensions={0} | all-to-all | bytes 524288 | tf_op jit(solution)/shard_map/all_to_all | solution.py:24
  148.2 0.0 copy-done.2
  148.2 0.0 copy-done.3
  148.2 1.1 last_rows.1
Async XLA Ops:
  0.6 44.0 %copy-start = (bf16[768,768]{1,0:T(8,128)(2,1)S(1)}, bf16[768,768]{1,0:T(8,128)(2,1)}, u32[]{:S(2)}) copy-start(bf16[768,768]{1,0:T(8,128)(2,1)} %weight_ref.3) | copy-start | bytes 3538948
  0.6 44.0 %copy-start.4 = (f32[768]{0:T(1024)S(1)}, f32[768]{0:T(1024)}, u32[]{:S(2)}) copy-start(f32[768]{0:T(1024)} %gain_ref.7) | copy-start | bytes 9220
  0.7 44.0 %copy-start.5 = (f32[768]{0:T(1024)S(1)}, f32[768]{0:T(1024)}, u32[]{:S(2)}) copy-start(f32[768]{0:T(1024)} %bias_in_ref.1) | copy-start | bytes 9220
  44.6 26.2 %copy-start.6 = (f32[256]{0:T(256)S(1)}, f32[256]{0:T(256)}, u32[]{:S(2)}) copy-start(f32[256]{0:T(256)} %gain_ref.6) | copy-start | bytes 3076
  44.6 26.2 %copy-start.7 = (f32[256]{0:T(256)S(1)}, f32[256]{0:T(256)}, u32[]{:S(2)}) copy-start(f32[256]{0:T(256)} %bias_ref.3) | copy-start | bytes 3076
  44.7 50.5 %copy-start.1 = (bf16[1,128,768]{2,1,0:T(8,128)(2,1)S(1)}, bf16[1,128,768]{2,1,0:T(8,128)(2,1)}, u32[]{:S(2)}) copy-start(bf16[1,128,768]{2,1,0:T(8,128)(2,1)} %param.9) | copy-start | bytes 589828
  96.4 4.2 %collective-permute-start = (bf16[776,512]{1,0:T(8,128)(2,1)S(1)}, bf16[776,512]{1,0:T(8,128)(2,1)S(1)}, u32[]{:S(2)}, u32[]{:S(2)}) collective-permute-start(bf16[776,512]{1,0:T(8,128)(2,1)S(1)} %get-tuple-element.38), channel_id=1, source_target_pairs={{0,8},{8,0},{1,9},{9,1},{2,10},{10,2},{3,11},{11,3},{4,12},{12,4},... | collective-permute-start | bytes 2383880 | tf_op jit(solution)/shard_map/ppermute | solution.py:396
  133.4 14.8 %copy-start.2 = (bf16[256,768]{1,0:T(8,128)(2,1)S(1)}, bf16[256,768]{1,0:T(8,128)(2,1)}, u32[]{:S(2)}) copy-start(bf16[256,768]{1,0:T(8,128)(2,1)} %proj_ref.1) | copy-start | bytes 1179652
  133.4 14.8 %copy-start.3 = (bf16[1,128,768]{2,1,0:T(8,128)(2,1)S(1)}, bf16[1,128,768]{2,1,0:T(8,128)(2,1)}, u32[]{:S(2)}) copy-start(bf16[1,128,768]{2,1,0:T(8,128)(2,1)} %param.8) | copy-start | bytes 589828

commit v11 on v10

--- a/solution.py
+++ b/solution.py
@@ -124,21 +124,16 @@
     )
 
 
-def opening(x_hbm, cot_hbm, proj_hbm, sums_ref, data_ref, dact_ref, x_ref, cot_ref, proj_ref, sems):
-    pairs = ((x_hbm, x_ref), (cot_hbm, cot_ref), (proj_hbm, proj_ref))
-    loads = [pltpu.make_async_copy(*pair, sems.at[k]) for k, pair in enumerate(pairs)]
-    for load in loads:
-        load.start()
-    loads[0].wait()
+def opening(x_hbm, sums_ref, data_ref, x_ref, sem):
+    load = pltpu.make_async_copy(x_hbm, x_ref, sem)
+    load.start()
+    load.wait()
     x = x_ref[...].astype(F32)
     mean = sum_rows(x) * (1.0 / ROWS)
     apart = x - mean
     copies(sums_ref, slice(0, CH), mean)
     copies(sums_ref, slice(CH, 2 * CH), sum_rows(apart * apart))
     data_ref[...] = woven(x)
-    loads[1].wait()
-    loads[2].wait()
-    dact_ref[...] = woven(matmul(cot_ref[...], proj_ref[...], ((1,), (1,))))
 
 
 def spread_all(sums_ref, data_ref, out_ref):
@@ -162,7 +157,7 @@
     return row_of(mean, (0, 1)), row_of(total, (4, 5)) + row_of(between, (0, 1))
 
 
-def forward_conv(got_ref, weight_ref, gain_ref, bias_ref, dact_ref, act_ref, x_ref, conv_ref, out_ref, stat_ref):
+def forward_conv(got_ref, weight_ref, gain_ref, bias_ref, cot_ref, proj_ref, act_ref, x_ref, conv_ref, out_ref, stat_ref):
     center, squares = over_pieces(got_ref[:, :, CH // 2 :], ROWS * LINES)
     spread = jnp.sqrt(squares * (1.0 / COUNTED) + 1e-05)
     stat_ref[0:1, :] = center
@@ -178,7 +173,7 @@
     mean = sum_rows(conv) * (1.0 / ROWS)
     apart = conv - mean
     tile = tile_of(in_two(mean, 128) + in_two(sum_rows(apart * apart), 128), 128).astype(BF16)
-    out_ref[:, :, :128] = dact_ref[...]
+    out_ref[:, :, :128] = woven(matmul(cot_ref[...], proj_ref[...], ((1,), (1,))))
     out_ref[:, :, 128:] = jnp.broadcast_to(tile[None], (PLANES, 8, 128))
 
 
@@ -221,7 +216,7 @@
     return jnp.concatenate([tile[k : k + 1, : CH // 2] + tile[k + 2 : k + 3, : CH // 2] for k in range(2)], axis=1)
 
 
-def filter_parts(
+def filter_sent(
     got_ref,
     gain_ref,
     cot_ref,
@@ -234,10 +229,11 @@
     act_in_ref,
     x_ref,
     stat_ref,
-    kept_ref,
     sent_ref,
+    stacked_ref,
     act_ref,
-    back_ref,
+    dpre_out_ref,
+    sums_ref,
 ):
     tile = jnp.sum(got_ref[:, :, 128:].astype(F32), axis=0) * (1.0 / COUNTED)
     tile = tile + pltpu.roll(tile, 4, axis=0)
@@ -245,26 +241,52 @@
     dconv = dpre_ref[...] - first - normed_ref[...] * second
     dconv = flat(gain_ref) * dconv / spread_ref[0:1, :]
     stacked = jnp.concatenate([earlier(dconv), dconv, later(dconv)], axis=1).astype(BF16)
-    conv_part = matmul(act_in_ref[...], stacked, ((0,), (0,)))
-    act = unwoven(got_ref[:, :, :128]).astype(BF16)
-    act_ref[...] = act
-    proj_part = matmul(cot_ref[...], act, ((0,), (0,)))
+    stacked_ref[...] = stacked
+    act_ref[...] = unwoven(got_ref[:, :, :128]).astype(BF16)
     normed = (x_ref[...].astype(F32) - stat_ref[0:1, :]) / stat_ref[1:2, :]
     pre = flat(gain_in_ref) * normed + flat(bias_in_ref)
     dpre = matmul(stacked, weight_ref[...], ((1,), (1,))) * slope_of(pre, tanh_of(pre))
-    sums = in_four(sum_rows(dpre)).astype(BF16), in_four(sum_rows(dpre * normed)).astype(BF16)
-
-    def place(left_ref, right_ref):
-        left_ref[:CH, :] = conv_part[:, :HALF].astype(BF16)
-        right_ref[:CH, : HALF - MID] = conv_part[:, HALF:].astype(BF16)
-        right_ref[:CH, HALF - MID :] = proj_part.astype(BF16)
-        left_ref[CH:, :] = sums[0]
-        right_ref[CH:, :] = sums[1]
-
+    dpre_out_ref[...] = dpre
+    both = in_four(sum_rows(dpre)).astype(BF16), in_four(sum_rows(dpre * normed)).astype(BF16)
     core = lax.axis_index("core")
-    pl.when(core == 0)(lambda: place(kept_ref, sent_ref))
-    pl.when(core == 1)(lambda: place(sent_ref, kept_ref))
-    back_ref[...] = woven(dpre)
+
+    @pl.when(core == 0)
+    def _():
+        right_half(sent_ref, act_in_ref, stacked_ref, cot_ref, act_ref)
+        sent_ref[CH:, :] = both[1]
+        sums_ref[...] = both[0]
+
+    @pl.when(core == 1)
+    def _():
+        left_half(sent_ref, act_in_ref, stacked_ref)
+        sent_ref[CH:, :] = both[0]
+        sums_ref[...] = both[1]
+
+
+def left_half(out_ref, act_in_ref, stacked_ref):
+    part = matmul(act_in_ref[...], stacked_ref[:, :HALF], ((0,), (0,)))
+    out_ref[:CH, :] = part.astype(BF16)
+
+
+def right_half(out_ref, act_in_ref, stacked_ref, cot_ref, act_ref):
+    part = matmul(act_in_ref[...], stacked_ref[:, HALF:], ((0,), (0,)))
+    out_ref[:CH, : HALF - MID] = part.astype(BF16)
+    part = matmul(cot_ref[...], act_ref[...], ((0,), (0,)))
+    out_ref[:CH, HALF - MID :] = part.astype(BF16)
+
+
+def filter_kept(cot_ref, act_in_ref, stacked_ref, act_ref, dpre_ref, sums_ref, kept_ref, back_ref):
+    core = lax.axis_index("core")
+    kept_ref[CH:, :] = sums_ref[...]
+    back_ref[...] = woven(dpre_ref[...])
+
+    @pl.when(core == 0)
+    def _():
+        left_half(kept_ref, act_in_ref, stacked_ref)
+
+    @pl.when(core == 1)
+    def _():
+        right_half(kept_ref, act_in_ref, stacked_ref, cot_ref, act_ref)
 
 
 def to_plane(got_ref, kept_ref, back_ref, out_ref):
@@ -325,24 +347,18 @@
     rows, rows_mid = (ROWS, CH), (ROWS, MID)
 
     far, near = pl.BlockSpec(memory_space=pltpu.HBM), pl.BlockSpec(memory_space=pltpu.VMEM)
-    sums, data, dact = pl.pallas_call(
+    sums, data = pl.pallas_call(
         opening,
         out_shape=(
             jax.ShapeDtypeStruct((LINES, 1, 2 * CH), F32),
             jax.ShapeDtypeStruct((PLANES, 8, CH // 2), BF16),
-            jax.ShapeDtypeStruct((PLANES, 8, 128), BF16),
         ),
-        in_specs=[far] * 3,
-        out_specs=(near,) * 3,
-        scratch_shapes=[
-            pltpu.VMEM(rows, BF16),
-            pltpu.VMEM(rows, BF16),
-            pltpu.VMEM((MID, CH), BF16),
-            pltpu.SemaphoreType.DMA((3,)),
-        ],
+        in_specs=[far],
+        out_specs=(near, near),
+        scratch_shapes=[pltpu.VMEM(rows, BF16), pltpu.SemaphoreType.DMA],
         name="opening",
         compiler_params=pltpu.CompilerParams(vmem_limit_bytes=24 << 20),
-    )(*(pltpu.with_memory_space_constraint(v, pltpu.HBM) for v in (x, cot, proj_weight)))
+    )(pltpu.with_memory_space_constraint(x, pltpu.HBM))
     sums = exchange(sums, LINE)
     (both,) = kernel(spread_all, ((PLANES, 8, CH), BF16), name="spread_all")(
         data, near=(sums,)
@@ -357,7 +373,7 @@
         ((PLANES, 8, 256), BF16),
         ((8, CH), F32),
         name="forward_conv",
-    )(dact, near=(both, conv_weight, gain_in, bias_in))
+    )(near=(both, conv_weight, gain_in, bias_in, cot, proj_weight))
     both = exchange(both, PLANE)
     (sums,) = kernel(middle_line, ((LINES, 1, 2 * MID), F32), name="middle_line")(near=(both,))
     sums = exchange(sums, LINE)
@@ -377,13 +393,14 @@
     )
     both = exchange(both, PLANE)
 
-    kept, sent, act_mid, back = kernel(
-        filter_parts,
+    sent, stacked, act_mid, dpre_in, sums = kernel(
+        filter_sent,
         ((CH + 8, HALF), BF16),
-        ((CH + 8, HALF), BF16),
+        (rows, BF16),
         (rows_mid, BF16),
-        ((PLANES, 8, CH // 2), BF16),
-        name="filter_parts",
+        (rows, F32),
+        ((8, HALF), BF16),
+        name="filter_sent",
     )(
         dpre_mid,
         normed_mid,
@@ -394,6 +411,9 @@
         near=(both, gain_mid, cot, conv_weight, gain_in, bias_in),
     )
     got = lax.ppermute(sent, "core", [(0, 1), (1, 0)])
+    kept, back = kernel(
+        filter_kept, ((CH + 8, HALF), BF16), ((PLANES, 8, CH // 2), BF16), name="filter_kept"
+    )(act_in, stacked, act_mid, dpre_in, sums, near=(cot,))
     (plane,) = kernel(to_plane, ((PLANES, 8, 3 * HALF + CH // 2 + 128), BF16), name="to_plane")(
         kept, back, near=(got,)
     )

time: 150 us -> 149 us (level)
    pallas_call x9 -> x10, Pallas kernels: 3.87 us -> 4.2 us  [call(): pl.pallas_call(body, out_shape=shapes, in_specs=[whole] * len(args), out_...]
where the time goes in v11:
time: 149 us
  blocking collectives  139 us (93%)
  Pallas kernels  5.4 us (4%)
  starting transfers between devices  1.92 us (1%)
  waiting for transfers between devices  1.84 us (1%)
    all_to_all x8, blocking collectives, exchange(): return lax.all_to_all(pieces, axes, split_axis=0, concat_axis=0, tiled=True)  139 us
    pallas_call x10, Pallas kernels, call(): pl.pallas_call(body, out_shape=shapes, in_specs=[whole] * len(args), out_...  4.2 us
  transfers between devices with their start and end apart: 1, of which 1 were waited for; matrix products, arithmetic and copies ran while one was open for 0% of the time, Pallas kernels for 0%

profile of v11, /device:TPU:8, one launch (start us, length us, event | category | flops | bytes accessed | tf_op | source)
XLA Modules:
  0.0 148.7 jit_solution(3358547966055705706)
XLA Ops:
  0.6 0.0 copy-start.4
  0.6 0.0 copy-start.5
  0.7 0.0 copy-start.2
  0.7 0.0 copy-start
  0.7 0.0 copy-start.1
  0.7 1.2 opening.1
  1.9 15.8 %all_to_all.40.sums_ref = f32[16,1,1536]{2,1,0:T(1,128)S(1)} all-to-all(f32[16,1,1536]{2,1,0:T(1,128)S(1)} %get-tuple-element.27), channel_id=1, replica_groups=mesh['x'=4,'z_hi'=2,'z_lo'=4,'core'=2,'dp'=8] {'core','dp'}, dimensions={0} | all-to-all | bytes 196608 | tf_op jit(solution)/shard_map/all_to_all | solution.py:24
  17.7 0.1 spread_all.1
  17.8 26.4 %all_to_all.41.got_ref = bf16[32,8,768]{2,1,0:T(8,128)(2,1)S(1)} all-to-all(bf16[32,8,768]{2,1,0:T(8,128)(2,1)S(1)} %spread_all.1), channel_id=1, replica_groups=mesh['x'=4,'z_hi'=2,'z_lo'=4,'core'=2,'dp'=8] {'x','z_hi','z_lo'}, dimensions={0} | all-to-all | bytes 786432 | tf_op jit(solution)/shard_map/all_to_all | solution.py:24
  44.3 0.0 copy-done.4
  44.3 0.0 copy-done.5
  44.3 0.0 copy-done.2
  44.3 0.0 copy-done
  44.3 0.0 copy-done.1
  44.3 0.0 copy-start.6
  44.3 0.0 copy-start.7
  44.3 0.8 forward_conv.1
  45.1 15.3 %all_to_all.42.got_ref.plane_ref = bf16[32,8,256]{2,1,0:T(8,128)(2,1)S(1)} all-to-all(bf16[32,8,256]{2,1,0:T(8,128)(2,1)S(1)} %get-tuple-element.29), channel_id=1, replica_groups=mesh['x'=4,'z_hi'=2,'z_lo'=4,'core'=2,'dp'=8] {'x','z_hi','z_lo'}, dimensions={0} | all-to-all | bytes 262144 | tf_op jit(solution)/shard_map/all_to_all | solution.py:24
  60.5 0.1 middle_line.1
  60.6 10.0 %all_to_all.43.got_ref = f32[16,1,512]{2,1,0:T(1,128)S(1)} all-to-all(f32[16,1,512]{2,1,0:T(1,128)S(1)} %middle_line.1), channel_id=1, replica_groups=mesh['x'=4,'z_hi'=2,'z_lo'=4,'core'=2,'dp'=8] {'core','dp'}, dimensions={0} | all-to-all | bytes 65536 | tf_op jit(solution)/shard_map/all_to_all | solution.py:24
  70.6 0.0 copy-done.6
  70.6 0.0 copy-done.7
  70.6 0.2 middle.1
  70.8 10.2 %all_to_all.44.sums_ref = f32[16,1,512]{2,1,0:T(1,128)S(1)} all-to-all(f32[16,1,512]{2,1,0:T(1,128)S(1)} %get-tuple-element.31), channel_id=1, replica_groups=mesh['x'=4,'z_hi'=2,'z_lo'=4,'core'=2,'dp'=8] {'core','dp'}, dimensions={0} | all-to-all | bytes 65536 | tf_op jit(solution)/shard_map/all_to_all | solution.py:24
  81.0 0.1 middle_plane.1
  81.1 13.8 %all_to_all.45.got_ref = bf16[32,8,256]{2,1,0:T(8,128)(2,1)S(1)} all-to-all(bf16[32,8,256]{2,1,0:T(8,128)(2,1)S(1)} %middle_plane.1), channel_id=1, replica_groups=mesh['x'=4,'z_hi'=2,'z_lo'=4,'core'=2,'dp'=8] {'x','z_hi','z_lo'}, dimensions={0} | all-to-all | bytes 262144 | tf_op jit(solution)/shard_map/all_to_all | solution.py:24
  94.9 1.1 filter_sent.1
  96.0 1.9 %collective-permute-start = (bf16[776,512]{1,0:T(8,128)(2,1)S(1)}, bf16[776,512]{1,0:T(8,128)(2,1)S(1)}, u32[]{:S(2)}, u32[]{:S(2)}) collective-permute-start(bf16[776,512]{1,0:T(8,128)(2,1)S(1)} %get-tuple-element.39), channel_id=1, source_target_pairs={{0,8},{8,0},{1,9},{9,1},{2,10},{10,2},{3,11},{11,3},{4,12},{12,4},... | collective-permute-start | bytes 2383880 | tf_op jit(solution)/shard_map/ppermute | solution.py:413
  97.9 0.4 filter_kept.1
  98.3 1.8 %collective-permute-done.got_ref = bf16[776,512]{1,0:T(8,128)(2,1)S(1)} collective-permute-done((bf16[776,512]{1,0:T(8,128)(2,1)S(1)}, bf16[776,512]{1,0:T(8,128)(2,1)S(1)}, u32[]{:S(2)}, u32[]{:S(2)}) %collective-permute-start) | collective-permute-done | bytes 794656 | tf_op jit(solution)/shard_map/ppermute | solution.py:413
  100.2 0.2 to_plane.1
  100.4 32.5 %all_to_all.46.got_ref.plane_ref = bf16[32,8,2048]{2,1,0:T(8,128)(2,1)S(1)} all-to-all(bf16[32,8,2048]{2,1,0:T(8,128)(2,1)S(1)} %to_plane.1), channel_id=1, replica_groups=mesh['x'=4,'z_hi'=2,'z_lo'=4,'core'=2,'dp'=8] {'x','z_hi','z_lo'}, dimensions={0} | all-to-all | bytes 2097152 | tf_op jit(solution)/shard_map/all_to_all | solution.py:24
  132.9 0.0 copy-start.3
  132.9 0.1 to_line.1
  133.1 14.5 %all_to_all.47.got_ref = bf16[16,8,1024]{2,1,0:T(8,128)(2,1)S(1)} all-to-all(bf16[16,8,1024]{2,1,0:T(8,128)(2,1)S(1)} %to_line.1), channel_id=1, replica_groups=mesh['x'=4,'z_hi'=2,'z_lo'=4,'core'=2,'dp'=8] {'core','dp'}, dimensions={0} | all-to-all | bytes 524288 | tf_op jit(solution)/shard_map/all_to_all | solution.py:24
  147.6 0.0 copy-done.3
  147.6 1.1 last_rows.1
Async XLA Ops:
  0.6 43.6 %copy-start.4 = (f32[768]{0:T(1024)S(1)}, f32[768]{0:T(1024)}, u32[]{:S(2)}) copy-start(f32[768]{0:T(1024)} %gain_ref.7) | copy-start | bytes 9220
  0.6 43.6 %copy-start.5 = (f32[768]{0:T(1024)S(1)}, f32[768]{0:T(1024)}, u32[]{:S(2)}) copy-start(f32[768]{0:T(1024)} %bias_in_ref.1) | copy-start | bytes 9220
  0.7 43.6 %copy-start.2 = (bf16[256,768]{1,0:T(8,128)(2,1)S(1)}, bf16[256,768]{1,0:T(8,128)(2,1)}, u32[]{:S(2)}) copy-start(bf16[256,768]{1,0:T(8,128)(2,1)} %proj_ref.3) | copy-start | bytes 1179652
  0.7 43.6 %copy-start = (bf16[768,768]{1,0:T(8,128)(2,1)S(1)}, bf16[768,768]{1,0:T(8,128)(2,1)}, u32[]{:S(2)}) copy-start(bf16[768,768]{1,0:T(8,128)(2,1)} %weight_ref.3) | copy-start | bytes 3538948
  0.7 43.6 %copy-start.1 = (bf16[1,128,768]{2,1,0:T(8,128)(2,1)S(1)}, bf16[1,128,768]{2,1,0:T(8,128)(2,1)}, u32[]{:S(2)}) copy-start(bf16[1,128,768]{2,1,0:T(8,128)(2,1)} %param.9) | copy-start | bytes 589828
  44.3 26.3 %copy-start.6 = (f32[256]{0:T(256)S(1)}, f32[256]{0:T(256)}, u32[]{:S(2)}) copy-start(f32[256]{0:T(256)} %gain_ref.6) | copy-start | bytes 3076
  44.3 26.3 %copy-start.7 = (f32[256]{0:T(256)S(1)}, f32[256]{0:T(256)}, u32[]{:S(2)}) copy-start(f32[256]{0:T(256)} %bias_ref.3) | copy-start | bytes 3076
  96.0 4.2 %collective-permute-start = (bf16[776,512]{1,0:T(8,128)(2,1)S(1)}, bf16[776,512]{1,0:T(8,128)(2,1)S(1)}, u32[]{:S(2)}, u32[]{:S(2)}) collective-permute-start(bf16[776,512]{1,0:T(8,128)(2,1)S(1)} %get-tuple-element.39), channel_id=1, source_target_pairs={{0,8},{8,0},{1,9},{9,1},{2,10},{10,2},{3,11},{11,3},{4,12},{12,4},... | collective-permute-start | bytes 2383880 | tf_op jit(solution)/shard_map/ppermute | solution.py:413
  132.9 14.7 %copy-start.3 = (bf16[1,128,768]{2,1,0:T(8,128)(2,1)S(1)}, bf16[1,128,768]{2,1,0:T(8,128)(2,1)}, u32[]{:S(2)}) copy-start(bf16[1,128,768]{2,1,0:T(8,128)(2,1)} %param.8) | copy-start | bytes 589828

commit v12 on v11

--- a/solution.py
+++ b/solution.py
@@ -275,8 +275,12 @@
     out_ref[:CH, HALF - MID :] = part.astype(BF16)
 
 
-def filter_kept(cot_ref, act_in_ref, stacked_ref, act_ref, dpre_ref, sums_ref, kept_ref, back_ref):
+def filter_kept(
+    cot_ref, x_ref, proj_ref, act_in_ref, stacked_ref, act_ref, dpre_ref, sums_ref, kept_ref, back_ref, out_ref
+):
     core = lax.axis_index("core")
+    update = matmul(act_ref[...], proj_ref[...], ((1,), (0,)))
+    out_ref[...] = (x_ref[...].astype(F32) + update).astype(BF16)
     kept_ref[CH:, :] = sums_ref[...]
     back_ref[...] = woven(dpre_ref[...])
 
@@ -321,11 +325,9 @@
 
 
 def last_rows(
-    got_ref, plane_ref, x_ref, cot_ref, proj_ref, gain_ref, act_ref, stat_ref, out_ref, grad_ref, conv_ref, proj_grad_ref
+    got_ref, plane_ref, x_ref, cot_ref, gain_ref, stat_ref, grad_ref, conv_ref, proj_grad_ref
 ):
     x = x_ref[...].astype(F32)
-    update = matmul(act_ref[...], proj_ref[...], ((1,), (0,)))
-    out_ref[...] = (x + update).astype(BF16)
     left, right = (
         jnp.sum(got_ref[BATCH * k : BATCH * (k + 1)].astype(F32), axis=0) for k in range(2)
     )
@@ -411,18 +413,22 @@
         near=(both, gain_mid, cot, conv_weight, gain_in, bias_in),
     )
     got = lax.ppermute(sent, "core", [(0, 1), (1, 0)])
-    kept, back = kernel(
-        filter_kept, ((CH + 8, HALF), BF16), ((PLANES, 8, CH // 2), BF16), name="filter_kept"
-    )(act_in, stacked, act_mid, dpre_in, sums, near=(cot,))
+    kept, back, block_out = kernel(
+        filter_kept,
+        ((CH + 8, HALF), BF16),
+        ((PLANES, 8, CH // 2), BF16),
+        (rows, BF16),
+        name="filter_kept",
+    )(act_in, stacked, act_mid, dpre_in, sums, near=(cot, x, proj_weight))
     (plane,) = kernel(to_plane, ((PLANES, 8, 3 * HALF + CH // 2 + 128), BF16), name="to_plane")(
         kept, back, near=(got,)
     )
     plane = exchange(plane, PLANE)
     (line,) = kernel(to_line, ((LINES, 8, 2 * HALF), BF16), name="to_line")(near=(plane,))
     line = exchange(line, LINE)
-    block_out, input_grad, conv_grad, proj_grad = kernel(
-        last_rows, (rows, BF16), (rows, BF16), ((12, CH), F32), ((12, MID), F32), name="last_rows"
-    )(act_mid, stat_in, near=(line, plane, x, cot, proj_weight, gain_in))
+    input_grad, conv_grad, proj_grad = kernel(
+        last_rows, (rows, BF16), ((12, CH), F32), ((12, MID), F32), name="last_rows"
+    )(stat_in, near=(line, plane, x, cot, gain_in))
     return (
         block_out.reshape(inputs.shape),
         input_grad.reshape(inputs.shape),

time: 149 us -> 149 us (level)
  transfers between devices with their start and end apart: 1 -> 1, of which waited for: 1 -> 1; matrix products, arithmetic and copies ran while one was open for 0% -> 0% of each run, Pallas kernels for 0% -> 1%
where the time goes in v12:
time: 149 us
  blocking collectives  139 us (93%)
  Pallas kernels  6.11 us (4%)
  starting transfers between devices  1.92 us (1%)
    all_to_all x8, blocking collectives, exchange(): return lax.all_to_all(pieces, axes, split_axis=0, concat_axis=0, tiled=True)  139 us
    pallas_call x10, Pallas kernels, call(): pl.pallas_call(body, out_shape=shapes, in_specs=[whole] * len(args), out_...  4.91 us
  transfers between devices with their start and end apart: 1, of which 1 were waited for; matrix products, arithmetic and copies ran while one was open for 0% of the time, Pallas kernels for 1%

profile of v12, /device:TPU:8, one launch (start us, length us, event | category | flops | bytes accessed | tf_op | source)
XLA Modules:
  0.0 148.6 jit_solution(10408773735213831307)
XLA Ops:
  0.6 0.0 copy-start.4
  0.6 0.0 copy-start.5
  0.7 0.0 copy-start.3
  0.7 0.0 copy-start
  0.7 0.0 copy-start.1
  0.7 1.2 opening.1
  1.9 15.8 %all_to_all.40.sums_ref = f32[16,1,1536]{2,1,0:T(1,128)S(1)} all-to-all(f32[16,1,1536]{2,1,0:T(1,128)S(1)} %get-tuple-element.27), channel_id=1, replica_groups=mesh['x'=4,'z_hi'=2,'z_lo'=4,'core'=2,'dp'=8] {'core','dp'}, dimensions={0} | all-to-all | bytes 196608 | tf_op jit(solution)/shard_map/all_to_all | solution.py:24
  17.7 0.1 spread_all.1
  17.8 26.4 %all_to_all.41.got_ref = bf16[32,8,768]{2,1,0:T(8,128)(2,1)S(1)} all-to-all(bf16[32,8,768]{2,1,0:T(8,128)(2,1)S(1)} %spread_all.1), channel_id=1, replica_groups=mesh['x'=4,'z_hi'=2,'z_lo'=4,'core'=2,'dp'=8] {'x','z_hi','z_lo'}, dimensions={0} | all-to-all | bytes 786432 | tf_op jit(solution)/shard_map/all_to_all | solution.py:24
  44.3 0.0 copy-done.4
  44.3 0.0 copy-done.5
  44.3 0.0 copy-done.3
  44.3 0.0 copy-done
  44.3 0.0 copy-done.1
  44.3 0.0 copy-start.6
  44.3 0.0 copy-start.7
  44.3 0.8 forward_conv.1
  45.1 15.3 %all_to_all.42.got_ref.plane_ref = bf16[32,8,256]{2,1,0:T(8,128)(2,1)S(1)} all-to-all(bf16[32,8,256]{2,1,0:T(8,128)(2,1)S(1)} %get-tuple-element.30), channel_id=1, replica_groups=mesh['x'=4,'z_hi'=2,'z_lo'=4,'core'=2,'dp'=8] {'x','z_hi','z_lo'}, dimensions={0} | all-to-all | bytes 262144 | tf_op jit(solution)/shard_map/all_to_all | solution.py:24
  60.5 0.1 middle_line.1
  60.6 10.0 %all_to_all.43.got_ref = f32[16,1,512]{2,1,0:T(1,128)S(1)} all-to-all(f32[16,1,512]{2,1,0:T(1,128)S(1)} %middle_line.1), channel_id=1, replica_groups=mesh['x'=4,'z_hi'=2,'z_lo'=4,'core'=2,'dp'=8] {'core','dp'}, dimensions={0} | all-to-all | bytes 65536 | tf_op jit(solution)/shard_map/all_to_all | solution.py:24
  70.6 0.0 copy-done.6
  70.6 0.0 copy-done.7
  70.6 0.2 middle.1
  70.8 10.2 %all_to_all.44.sums_ref = f32[16,1,512]{2,1,0:T(1,128)S(1)} all-to-all(f32[16,1,512]{2,1,0:T(1,128)S(1)} %get-tuple-element.32), channel_id=1, replica_groups=mesh['x'=4,'z_hi'=2,'z_lo'=4,'core'=2,'dp'=8] {'core','dp'}, dimensions={0} | all-to-all | bytes 65536 | tf_op jit(solution)/shard_map/all_to_all | solution.py:24
  81.0 0.1 middle_plane.1
  81.1 0.0 copy-start.2
  81.1 14.0 %all_to_all.45.got_ref = bf16[32,8,256]{2,1,0:T(8,128)(2,1)S(1)} all-to-all(bf16[32,8,256]{2,1,0:T(8,128)(2,1)S(1)} %middle_plane.1), channel_id=1, replica_groups=mesh['x'=4,'z_hi'=2,'z_lo'=4,'core'=2,'dp'=8] {'x','z_hi','z_lo'}, dimensions={0} | all-to-all | bytes 262144 | tf_op jit(solution)/shard_map/all_to_all | solution.py:24
  95.1 1.1 filter_sent.1
  96.1 1.9 %collective-permute-start = (bf16[776,512]{1,0:T(8,128)(2,1)S(1)}, bf16[776,512]{1,0:T(8,128)(2,1)S(1)}, u32[]{:S(2)}, u32[]{:S(2)}) collective-permute-start(bf16[776,512]{1,0:T(8,128)(2,1)S(1)} %get-tuple-element.44), channel_id=1, source_target_pairs={{0,8},{8,0},{1,9},{9,1},{2,10},{10,2},{3,11},{11,3},{4,12},{12,4},... | collective-permute-start | bytes 2383880 | tf_op jit(solution)/shard_map/ppermute | solution.py:415
  98.1 0.0 copy-done.2
  98.1 1.3 filter_kept.1
  99.4 1.0 collective-permute-done.got_ref
  100.3 0.2 to_plane.1
  100.6 32.5 %all_to_all.46.got_ref.plane_ref = bf16[32,8,2048]{2,1,0:T(8,128)(2,1)S(1)} all-to-all(bf16[32,8,2048]{2,1,0:T(8,128)(2,1)S(1)} %to_plane.1), channel_id=1, replica_groups=mesh['x'=4,'z_hi'=2,'z_lo'=4,'core'=2,'dp'=8] {'x','z_hi','z_lo'}, dimensions={0} | all-to-all | bytes 2097152 | tf_op jit(solution)/shard_map/all_to_all | solution.py:24
  133.1 0.1 to_line.1
  133.2 14.5 %all_to_all.47.got_ref = bf16[16,8,1024]{2,1,0:T(8,128)(2,1)S(1)} all-to-all(bf16[16,8,1024]{2,1,0:T(8,128)(2,1)S(1)} %to_line.1), channel_id=1, replica_groups=mesh['x'=4,'z_hi'=2,'z_lo'=4,'core'=2,'dp'=8] {'core','dp'}, dimensions={0} | all-to-all | bytes 524288 | tf_op jit(solution)/shard_map/all_to_all | solution.py:24
  147.7 0.9 last_rows.1
Async XLA Ops:
  0.6 43.6 %copy-start.4 = (f32[768]{0:T(1024)S(1)}, f32[768]{0:T(1024)}, u32[]{:S(2)}) copy-start(f32[768]{0:T(1024)} %gain_ref.7) | copy-start | bytes 9220
  0.6 43.6 %copy-start.5 = (f32[768]{0:T(1024)S(1)}, f32[768]{0:T(1024)}, u32[]{:S(2)}) copy-start(f32[768]{0:T(1024)} %bias_in_ref.1) | copy-start | bytes 9220
  0.7 43.6 %copy-start.3 = (bf16[256,768]{1,0:T(8,128)(2,1)S(1)}, bf16[256,768]{1,0:T(8,128)(2,1)}, u32[]{:S(2)}) copy-start(bf16[256,768]{1,0:T(8,128)(2,1)} %proj_ref.3) | copy-start | bytes 1179652
  0.7 43.6 %copy-start = (bf16[768,768]{1,0:T(8,128)(2,1)S(1)}, bf16[768,768]{1,0:T(8,128)(2,1)}, u32[]{:S(2)}) copy-start(bf16[768,768]{1,0:T(8,128)(2,1)} %weight_ref.3) | copy-start | bytes 3538948
  0.7 43.6 %copy-start.1 = (bf16[1,128,768]{2,1,0:T(8,128)(2,1)S(1)}, bf16[1,128,768]{2,1,0:T(8,128)(2,1)}, u32[]{:S(2)}) copy-start(bf16[1,128,768]{2,1,0:T(8,128)(2,1)} %param.9) | copy-start | bytes 589828
  44.3 26.3 %copy-start.6 = (f32[256]{0:T(256)S(1)}, f32[256]{0:T(256)}, u32[]{:S(2)}) copy-start(f32[256]{0:T(256)} %gain_ref.6) | copy-start | bytes 3076
  44.3 26.3 %copy-start.7 = (f32[256]{0:T(256)S(1)}, f32[256]{0:T(256)}, u32[]{:S(2)}) copy-start(f32[256]{0:T(256)} %bias_ref.3) | copy-start | bytes 3076
  81.1 17.0 %copy-start.2 = (bf16[1,128,768]{2,1,0:T(8,128)(2,1)S(1)}, bf16[1,128,768]{2,1,0:T(8,128)(2,1)}, u32[]{:S(2)}) copy-start(bf16[1,128,768]{2,1,0:T(8,128)(2,1)} %param.8) | copy-start | bytes 589828
  96.1 4.2 %collective-permute-start = (bf16[776,512]{1,0:T(8,128)(2,1)S(1)}, bf16[776,512]{1,0:T(8,128)(2,1)S(1)}, u32[]{:S(2)}, u32[]{:S(2)}) collective-permute-start(bf16[776,512]{1,0:T(8,128)(2,1)S(1)} %get-tuple-element.44), channel_id=1, source_target_pairs={{0,8},{8,0},{1,9},{9,1},{2,10},{10,2},{3,11},{11,3},{4,12},{12,4},... | collective-permute-start | bytes 2383880 | tf_op jit(solution)/shard_map/ppermute | solution.py:415
